TPU v7x, 256 devices: a whole 4x4x8 slice. The times are simulated.
256 devices in a mesh: series: 8 (over x, y_lo), tm: 32 (over z, y_hi, core).
Axes of the slice: x: 4, y: 4 (y_hi: 2, y_lo: 2; y = y_hi * 2 + y_lo), z: 8, core: 2. Of those that a mesh axis runs over, the one named last changes fastest.
Arguments:
- observed: bfloat16 [10240, 24576], P('series', 'tm'), may hold values from -6 to 6
- mask: int32 [10240, 24576], P('series', 'tm'), may hold values 0 or 1
- series_factors: float32 [10240, 256], P('series'), may hold values from -6 to 6
- time_factors: float32 [256, 24576], P(None, 'tm'), may hold values from -0.375 to 0.375
- ar_weights: float32 [3, 256], replicated, may hold values from -0.7 to 0.7
Outputs:
- series_out: float32 [10240, 256], P('series')
- time_out: float32 [256, 24576], P(None, 'tm')
- imputed: bfloat16 [10240, 24576], P('series', 'tm')
Inputs may be any that keep to these rules, and one draw needn't show every extreme that they name: mask holds only 0 and 1.
All inputs are finite; a program needn't handle non-finite values. No bound on the sum of `mask` on one device may be relied on, other than what follows from the above.
Results may differ from a plain program's by a relative error of at most 0.0089.
Values sent between devices are 32-bit elements; how exact they have to be, the bound alone decides.
No kernel may reach another device: no remote copies, remote signals or barrier semaphores. Data moves between devices by JAX's collectives and lax.ppermute only.
A program may use at most 128 MiB of HBM per device.

v0:
```python
import jax
import jax.numpy as jnp
from jax import lax
from jax.sharding import Mesh
from jax.sharding import PartitionSpec as P

ITERS = 2
TM = ("tm_0", "tm_1", "tm_2")


lag_hours = (1, 24, 168)


def padded_to(lines, length):
    spare = -lines.shape[0] % length
    if not spare:
        return lines
    return jnp.concatenate([lines, jnp.zeros((spare, *lines.shape[1:]), lines.dtype)])


def from_everyone(array, axis):
    length = lax.axis_size(axis)
    return lax.all_to_all(
        jnp.broadcast_to(array[None], (length, *array.shape)), axis, 0, 0, tiled=True
    )


def laid_out(parts, dim):
    parts = jnp.moveaxis(parts, 0, dim)
    shape = parts.shape
    return parts.reshape(*shape[:dim], shape[dim] * shape[dim + 1], *shape[dim + 2 :])


def gather_axes(array, axes, dim):
    far, near = axes
    leading = from_everyone(array, far)
    parts = jnp.swapaxes(from_everyone(leading, near), 0, 1)
    return laid_out(parts.reshape(-1, *array.shape), dim)


def in_blocks(array, dim, length):
    before, after = (array.shape[:dim], array.shape[dim + 1 :])
    return jnp.moveaxis(array.reshape(*before, length, -1, *after), dim, 0)


def summed_on_arrival(array, axis, dim):
    parts = in_blocks(array, dim, lax.axis_size(axis))
    arrived = lax.all_to_all(parts, axis, split_axis=0, concat_axis=0, tiled=True)
    return arrived.sum(axis=0)


def sum_in_two_steps(array, axes, dim):
    far, near = axes
    parts = in_blocks(array, dim, lax.axis_size(far))
    nearer = summed_on_arrival(parts, near, dim + 1)
    arrived = lax.all_to_all(nearer, far, split_axis=0, concat_axis=0, tiled=True)
    return arrived.sum(axis=0)


def total_of(array, axes):
    lines = array.reshape(-1, array.shape[-1])
    padded = padded_to(lines, lax.axis_size(axes[0]) * lax.axis_size(axes[1]))
    whole = gather_axes(sum_in_two_steps(padded, axes, 0), axes, 0)
    return lax.slice_in_dim(whole, 0, len(lines)).reshape(array.shape)


def over_copies(array, axis):
    return from_everyone(array, axis).sum(axis=0)


def passed_along(array, axis, by):
    length = lax.axis_size(axis)
    pairs = [(i, i + by) for i in range(length) if 0 <= i + by < length]
    return lax.ppermute(array, axis, pairs)


def combine_lags(extended, weights, offset, width):
    total = None
    for lag_index, lag_size in enumerate(lag_hours):
        begin = offset + lag_size
        piece = weights[lag_index][:, None] * extended[:, begin : begin + width]
        total = piece if total is None else total + piece
    return total


def local(observed, mask, series_factors, time_factors, ar_weights):
    row_count, hour_count = observed.shape
    factor_rank = time_factors.shape[0]
    hours_all = hour_count * lax.axis_size(TM)
    sensors_all = row_count * lax.axis_size("series")
    step_f = factor_rank / hours_all
    step_x = 1.0 / sensors_all
    ridge_f = 0.1 * hours_all / factor_rank
    ridge_x = 0.1 * sensors_all
    lam_ar = sensors_all / 8.0
    first_hour = lax.axis_index(TM) * hour_count
    series_now = series_factors
    time_now = time_factors
    for sweep in range(ITERS):
        series_low = series_now.astype(jnp.bfloat16)
        time_low = time_now.astype(jnp.bfloat16)
        product = jnp.dot(series_low, time_low, preferred_element_type=jnp.float32)
        misfit = jnp.where(
            mask != 0, product - observed.astype(jnp.float32), jnp.zeros_like(product)
        ).astype(jnp.bfloat16)
        grad_series = total_of(
            lax.dot_general(
                misfit, time_low, (((1,), (1,)), ((), ())), preferred_element_type=jnp.float32
            ),
            (("tm_0", "tm_1"), "tm_2"),
        )
        series_next = series_now - step_f * (grad_series + ridge_f * series_now)
        grad_data = over_copies(
            lax.dot_general(
                series_low, misfit, (((0,), (0,)), ((), ())), preferred_element_type=jnp.float32
            ),
            "series",
        )
        left_edge = passed_along(time_now[:, hour_count - 168 :], TM, 1)
        extended = jnp.concatenate([left_edge, time_now], axis=1)
        lag_resid = time_now
        for lag_index, lag_size in enumerate(lag_hours):
            lag_resid = (
                lag_resid
                - ar_weights[lag_index][:, None]
                * extended[:, 168 - lag_size : 168 - lag_size + hour_count]
            )
        in_range = first_hour + jnp.arange(hour_count) >= 168
        lag_resid = jnp.where(in_range[None, :], lag_resid, jnp.zeros_like(lag_resid))
        right_edge = passed_along(lag_resid[:, :168], TM, -1)
        resid_wide = jnp.concatenate([lag_resid, right_edge], axis=1)
        backward = combine_lags(resid_wide, ar_weights, 0, hour_count)
        time_next = time_now - step_x * (
            grad_data + ridge_x * time_now + lam_ar * (lag_resid - backward)
        )
        series_now, time_now = (series_next, time_next)
    imputed = jnp.dot(
        series_now.astype(jnp.bfloat16),
        time_now.astype(jnp.bfloat16),
        preferred_element_type=jnp.float32,
    ).astype(jnp.bfloat16)
    return (series_now, time_now, imputed)


def solution(mesh):
    split = Mesh(
        mesh.devices.reshape(mesh.shape["series"], 8, 2, 2), ("series", "tm_0", "tm_1", "tm_2")
    )
    in_specs = (P("series", TM), P("series", TM), P("series", None), P(None, TM), P())
    out_specs = (P("series", None), P(None, TM), P("series", TM))
    return jax.shard_map(local, mesh=split, in_specs=in_specs, out_specs=out_specs, check_vma=False)
```

profile of v0, /device:TPU:1, one launch (start us, length us, event | category | flops | bytes accessed | tf_op | source)
XLA Modules:
  0.0 361.4 jit_solution(2277439647055620440)
XLA Ops:
  0.7 2.8 broadcast_compare_fusion
  6.3 8.5 %all_to_all.50 = f32[2,16,40,256]{3,2,1,0:T(8,128)} all-to-all(f32[2,16,40,256]{3,2,1,0:T(8,128)S(1)} %bitcast.39), channel_id=1, replica_groups=mesh['series'=8,'tm_0'=8,'tm_1'=2,'tm_2'=2] {'tm_2'}, dimensions={0} | all-to-all | bytes 2621440 | tf_op jit(solution)/shard_map/all_to_all | solution.py:48
  16.3 30.2 %all_to_all.51 = f32[16,40,256]{2,1,0:T(8,128)S(1)} all-to-all(f32[16,40,256]{2,1,0:T(8,128)S(1)} %reduce_sum.54), channel_id=1, replica_groups=mesh['series'=8,'tm_0'=8,'tm_1'=2,'tm_2'=2] {'tm_0','tm_1'}, dimensions={0} | all-to-all | bytes 1310720 | tf_op jit(solution)/shard_map/all_to_all | solution.py:56
  47.5 3.6 all-to-all-start.2
  51.1 3.1 convolution_bitcast_fusion
  55.6 14.1 %all-to-all-done.2 = f32[16,40,256]{2,1,0:T(8,128)S(1)} async-done(((f32[16,40,256]{2,1,0:T(8,128)}), f32[16,40,256]{2,1,0:T(8,128)S(1)}, u32[]{:S(2)}, u32[]{:S(2)}) %all-to-all-start.2) | async-done | bytes 655392 | tf_op jit(solution)/shard_map/all_to_all | solution.py:23
  69.8 9.4 %all_to_all.52 = f32[2,16,40,256]{3,2,1,0:T(8,128)} all-to-all(f32[2,16,40,256]{3,2,1,0:T(8,128)S(1)} %broadcast_in_dim.24), channel_id=1, replica_groups=mesh['series'=8,'tm_0'=8,'tm_1'=2,'tm_2'=2] {'tm_2'}, dimensions={0} | all-to-all | bytes 2621440 | tf_op jit(solution)/shard_map/all_to_all | solution.py:23
  79.2 3.2 broadcast_in_dim.25
  82.4 4.9 %all-to-all-start.4 = ((f32[8,256,768]{2,1,0:T(8,128)}), f32[8,256,768]{2,1,0:T(8,128)}, u32[]{:S(2)}, u32[]{:S(2)}) async-start(f32[8,256,768]{2,1,0:T(8,128)} %broadcast_in_dim.25), calls=%async_computation.4 | async-start | bytes 12582912 | tf_op jit(solution)/shard_map/all_to_all | solution.py:23
  87.4 2.8 collective-permute-start
  90.2 70.5 %collective-permute-done = f32[256,168]{1,0:T(8,128)S(1)} collective-permute-done((f32[256,168]{1,0:T(8,128)S(1)}, f32[256,168]{1,0:T(8,128)S(1)}, u32[]{:S(2)}, u32[]{:S(2)}) %collective-permute-start) | collective-permute-done | bytes 172064 | tf_op jit(solution)/shard_map/ppermute | solution.py:74
  166.3 11.2 %all-to-all-done.4 = f32[8,256,768]{2,1,0:T(8,128)} async-done(((f32[8,256,768]{2,1,0:T(8,128)}), f32[8,256,768]{2,1,0:T(8,128)}, u32[]{:S(2)}, u32[]{:S(2)}) %all-to-all-start.4) | async-done | bytes 6291488 | tf_op jit(solution)/shard_map/all_to_all | solution.py:23
  177.4 4.1 %reduce_sum.56 = f32[256,768]{1,0:T(8,128)} reduce(f32[8,256,768]{2,1,0:T(8,128)} %all-to-all-done.4, f32[]{:T(128)} %constant.15.clone.1), dimensions={0}, to_apply=%region_2.3 | reduce | flops 1376256 | bytes 7077892 | tf_op jit(solution)/shard_map/reduce_sum | solution.py:68
  185.7 6.5 %all_to_all.53 = f32[2,16,40,256]{3,2,1,0:T(8,128)} all-to-all(f32[2,16,40,256]{3,2,1,0:T(8,128)S(1)} %bitcast.40), channel_id=1, replica_groups=mesh['series'=8,'tm_0'=8,'tm_1'=2,'tm_2'=2] {'tm_2'}, dimensions={0} | all-to-all | bytes 2621440 | tf_op jit(solution)/shard_map/all_to_all | solution.py:48
  194.5 25.8 %all_to_all.54 = f32[16,40,256]{2,1,0:T(8,128)} all-to-all(f32[16,40,256]{2,1,0:T(8,128)} %reduce_sum.57), channel_id=1, replica_groups=mesh['series'=8,'tm_0'=8,'tm_1'=2,'tm_2'=2] {'tm_0','tm_1'}, dimensions={0} | all-to-all | bytes 1310720 | tf_op jit(solution)/shard_map/all_to_all | solution.py:56
  222.3 4.3 %all-to-all-start.7 = ((f32[16,40,256]{2,1,0:T(8,128)}), f32[16,40,256]{2,1,0:T(8,128)}, u32[]{:S(2)}, u32[]{:S(2)}) async-start(f32[16,40,256]{2,1,0:T(8,128)} %broadcast_in_dim.27), calls=%async_computation.7 | async-start | bytes 1310720 | tf_op jit(solution)/shard_map/all_to_all | solution.py:23
  228.2 17.9 %all-to-all-done.7 = f32[16,40,256]{2,1,0:T(8,128)} async-done(((f32[16,40,256]{2,1,0:T(8,128)}), f32[16,40,256]{2,1,0:T(8,128)}, u32[]{:S(2)}, u32[]{:S(2)}) %all-to-all-start.7) | async-done | bytes 655392 | tf_op jit(solution)/shard_map/all_to_all | solution.py:23
  247.3 7.8 %all_to_all.55 = f32[2,16,40,256]{3,2,1,0:T(8,128)S(1)} all-to-all(f32[2,16,40,256]{3,2,1,0:T(8,128)S(1)} %broadcast_in_dim.28), channel_id=1, replica_groups=mesh['series'=8,'tm_0'=8,'tm_1'=2,'tm_2'=2] {'tm_2'}, dimensions={0} | all-to-all | bytes 2621440 | tf_op jit(solution)/shard_map/all_to_all | solution.py:23
  255.1 3.2 broadcast_in_dim.29
  258.3 4.8 %all-to-all-start.9 = ((f32[8,256,768]{2,1,0:T(8,128)}), f32[8,256,768]{2,1,0:T(8,128)}, u32[]{:S(2)}, u32[]{:S(2)}) async-start(f32[8,256,768]{2,1,0:T(8,128)} %broadcast_in_dim.29), calls=%async_computation.9 | async-start | bytes 12582912 | tf_op jit(solution)/shard_map/all_to_all | solution.py:23
  263.2 2.6 collective-permute-start.2
  265.8 70.7 %collective-permute-done.2 = f32[256,168]{1,0:T(8,128)S(1)} collective-permute-done((f32[256,168]{1,0:T(8,128)S(1)}, f32[256,168]{1,0:T(8,128)S(1)}, u32[]{:S(2)}, u32[]{:S(2)}) %collective-permute-start.2) | collective-permute-done | bytes 172064 | tf_op jit(solution)/shard_map/ppermute | solution.py:74
  340.0 13.2 %all-to-all-done.9 = f32[8,256,768]{2,1,0:T(8,128)} async-done(((f32[8,256,768]{2,1,0:T(8,128)}), f32[8,256,768]{2,1,0:T(8,128)}, u32[]{:S(2)}, u32[]{:S(2)}) %all-to-all-start.9) | async-done | bytes 6291488 | tf_op jit(solution)/shard_map/all_to_all | solution.py:23
  353.3 4.1 %reduce_sum.59 = f32[256,768]{1,0:T(8,128)} reduce(f32[8,256,768]{2,1,0:T(8,128)} %all-to-all-done.9, f32[]{:T(128)} %constant.15.clone.1), dimensions={0}, to_apply=%region_5.6 | reduce | flops 1376256 | bytes 7077892 | tf_op jit(solution)/shard_map/reduce_sum | solution.py:68
  (67 shorter events, 31.1 us)
Async XLA Ops:
  0.6 2.8 copy-start
  0.6 2.8 copy-start.3
  0.7 3.4 copy-start.7
  4.0 1.0 copy-start.5
  5.0 1.3 copy-start.9
  47.5 22.2 %all-to-all-start.2 = ((f32[16,40,256]{2,1,0:T(8,128)}), f32[16,40,256]{2,1,0:T(8,128)S(1)}, u32[]{:S(2)}, u32[]{:S(2)}) async-start(f32[16,40,256]{2,1,0:T(8,128)} %broadcast_in_dim.23), calls=%async_computation.2 | async-start | bytes 1310720 | tf_op jit(solution)/shard_map/all_to_all | solution.py:23
  82.4 7.8 %copy-start.15 = (f32[3,256]{1,0:T(4,128)S(1)}, f32[3,256]{1,0:T(4,128)}, u32[]{:S(2)}) copy-start(f32[3,256]{1,0:T(4,128)} %param.9) | copy-start | bytes 9220
  82.4 95.1 %all-to-all-start.4 = ((f32[8,256,768]{2,1,0:T(8,128)}), f32[8,256,768]{2,1,0:T(8,128)}, u32[]{:S(2)}, u32[]{:S(2)}) async-start(f32[8,256,768]{2,1,0:T(8,128)} %broadcast_in_dim.25), calls=%async_computation.4 | async-start | bytes 12582912 | tf_op jit(solution)/shard_map/all_to_all | solution.py:23
  87.4 73.3 %collective-permute-start = (f32[256,168]{1,0:T(8,128)S(1)}, f32[256,168]{1,0:T(8,128)S(1)}, u32[]{:S(2)}, u32[]{:S(2)}) collective-permute-start(f32[256,168]{1,0:T(8,128)S(1)} %slice.67), channel_id=1, source_target_pairs={{0,1},{1,2},{2,3},{3,4},{4,5},{5,6},{6,7},{7,8},{8,9},{9,10},{10,1... | collective-permute-start | bytes 516104 | tf_op jit(solution)/shard_map/ppermute | solution.py:74
  161.6 3.4 copy-start.11
  161.6 20.0 %collective-permute-start.1 = (f32[256,168]{1,0:T(8,128)S(1)}, f32[256,168]{1,0:T(8,128)}, u32[]{:S(2)}, u32[]{:S(2)}) collective-permute-start(f32[256,168]{1,0:T(8,128)S(1)} %slice.89), channel_id=1, source_target_pairs={{1,0},{2,1},{3,2},{4,3},{5,4},{6,5},{7,6},{8,7},{9,8},{10,9},{11,1... | collective-permute-start | bytes 516104 | tf_op jit(solution)/shard_map/ppermute | solution.py:74
  165.0 1.1 copy-start.1
  166.3 15.3 %copy-start.12 = (f32[256,768]{1,0:T(8,128)S(1)}, f32[256,768]{1,0:T(8,128)}, u32[]{:S(2)}) copy-start(f32[256,768]{1,0:T(8,128)} %copy-done.11) | copy-start | bytes 2359300
  181.6 2.4 copy-start.6
  181.6 2.4 copy-start.8
  222.3 23.8 %all-to-all-start.7 = ((f32[16,40,256]{2,1,0:T(8,128)}), f32[16,40,256]{2,1,0:T(8,128)}, u32[]{:S(2)}, u32[]{:S(2)}) async-start(f32[16,40,256]{2,1,0:T(8,128)} %broadcast_in_dim.27), calls=%async_computation.7 | async-start | bytes 1310720 | tf_op jit(solution)/shard_map/all_to_all | solution.py:23
  247.3 7.8 %copy-start.13 = (f32[256,768]{1,0:T(8,128)S(1)}, f32[256,768]{1,0:T(8,128)}, u32[]{:S(2)}) copy-start(f32[256,768]{1,0:T(8,128)} %fusion.62) | copy-start | bytes 2359300
  258.3 94.9 %all-to-all-start.9 = ((f32[8,256,768]{2,1,0:T(8,128)}), f32[8,256,768]{2,1,0:T(8,128)}, u32[]{:S(2)}, u32[]{:S(2)}) async-start(f32[8,256,768]{2,1,0:T(8,128)} %broadcast_in_dim.29), calls=%async_computation.9 | async-start | bytes 12582912 | tf_op jit(solution)/shard_map/all_to_all | solution.py:23
  263.2 73.3 %collective-permute-start.2 = (f32[256,168]{1,0:T(8,128)S(1)}, f32[256,168]{1,0:T(8,128)S(1)}, u32[]{:S(2)}, u32[]{:S(2)}) collective-permute-start(f32[256,168]{1,0:T(8,128)S(1)} %slice.94), channel_id=1, source_target_pairs={{0,1},{1,2},{2,3},{3,4},{4,5},{5,6},{6,7},{7,8},{8,9},{9,10},{10,1... | collective-permute-start | bytes 516104 | tf_op jit(solution)/shard_map/ppermute | solution.py:74
  337.4 2.2 copy-start.2
  337.4 2.2 copy-start.4
  337.4 20.0 %collective-permute-start.3 = (f32[256,168]{1,0:T(8,128)S(1)}, f32[256,168]{1,0:T(8,128)S(1)}, u32[]{:S(2)}, u32[]{:S(2)}) collective-permute-start(f32[256,168]{1,0:T(8,128)S(1)} %slice.99), channel_id=1, source_target_pairs={{1,0},{2,1},{3,2},{4,3},{5,4},{6,5},{7,6},{8,7},{9,8},{10,9},{11,1... | collective-permute-start | bytes 516104 | tf_op jit(solution)/shard_map/ppermute | solution.py:74
  340.0 19.4 %copy-start.10 = (f32[1280,256]{1,0:T(8,128)}, f32[1280,256]{1,0:T(8,128)S(1)}, u32[]{:S(2)}) copy-start(f32[1280,256]{1,0:T(8,128)S(1)} %fusion.5) | copy-start | bytes 3932164
  359.4 2.0 copy-start.14
where the time goes:
time: 363 us; the launch traced here: 361 us
  waiting for transfers between devices  198 us (55%)
  blocking collectives  88.2 us (24%)
  starting transfers between devices  26.8 us (7%)
  other arithmetic  22.7 us (6%)
  local copies, waits for them, and re-layouts  15.2 us (4%)
  matrix products  9.88 us (3%)
    ppermute x4, waiting for transfers between devices, passed_along(): return lax.ppermute(array, axis, pairs)  141 us
    all_to_all x4, waiting for transfers between devices, from_everyone(): lax.all_to_all(jnp.broadcast_to(array[None], (length, *array.shape)), axi...  56.4 us
    all_to_all x2, blocking collectives, sum_in_two_steps(): lax.all_to_all(nearer, far, split_axis=0, concat_axis=0, tiled=True)  56.1 us
    all_to_all x4, starting transfers between devices, from_everyone(): lax.all_to_all(jnp.broadcast_to(array[None], (length, *array.shape)), axi...  17.5 us
    all_to_all x2, blocking collectives, from_everyone(): lax.all_to_all(jnp.broadcast_to(array[None], (length, *array.shape)), axi...  17.2 us
    all_to_all x2, blocking collectives, summed_on_arrival(): lax.all_to_all(parts, axis, split_axis=0, concat_axis=0, tiled=True)  14.9 us
    broadcast_in_dim x6, local copies, waits for them, and re-layouts, from_everyone(): jnp.broadcast_to(array[None], (length, *array.shape))  9.4 us
    ppermute x4, starting transfers between devices, passed_along(): return lax.ppermute(array, axis, pairs)  9.32 us
  transfers between devices with their start and end apart: 8, of which 6 were waited for; matrix products, arithmetic and copies ran while one was open for 5% of the time, Pallas kernels for 0%

commit v1 on v0

v1 whole, which is shorter than its diff:
```python
import jax
import jax.numpy as jnp
from jax import lax
from jax.sharding import Mesh
from jax.sharding import PartitionSpec as P

ITERS = 2
LAGS = (1, 24, 168)
EDGE = 168
SERIES = ("x", "y_lo")
FAR = ("z", "y_hi")
CORE = "core"
TM = (*FAR, CORE)
SWAP = ((0, 1), (1, 0))


def scattered_sum(array, axis):
    parts = array.reshape(lax.axis_size(axis), -1, array.shape[-1])
    return lax.all_to_all(parts, axis, 0, 0, tiled=True).sum(axis=0)


def gathered(array, axis):
    parts = jnp.broadcast_to(array[None], (lax.axis_size(axis), *array.shape))
    parts = lax.all_to_all(parts, axis, 0, 0, tiled=True)
    return parts.reshape(-1, array.shape[-1])


def passed_along(array, axis, by):
    length = lax.axis_size(axis)
    pairs = [(i, i + by) for i in range(length) if 0 <= i + by < length]
    return lax.ppermute(array, axis, pairs)


def lag_terms(now, weights, first, last):
    hours = now.shape[1]
    before = passed_along(now[:, hours - EDGE :], TM, 1)
    after = passed_along(now[:, :EDGE], TM, -1)
    wide = jnp.concatenate([before, now, after], axis=1)
    length = hours + EDGE
    resid = wide[:, EDGE:]
    for lag, weight in zip(LAGS, weights):
        resid = resid - weight[:, None] * wide[:, EDGE - lag : EDGE - lag + length]
    column = jnp.arange(length)
    inside = (~first | (column >= EDGE)) & (~last | (column < hours))
    resid = jnp.where(inside[None, :], resid, 0.0)
    back = None
    for lag, weight in zip(LAGS, weights):
        term = weight[:, None] * resid[:, lag : lag + hours]
        back = term if back is None else back + term
    return resid[:, :hours] - back


def local(observed, mask, series_factors, time_factors, ar_weights):
    rows, hours = observed.shape
    rank = time_factors.shape[0]
    hours_all = hours * lax.axis_size(TM)
    rows_all = rows * lax.axis_size(SERIES)
    step_f = rank / hours_all
    step_x = 1.0 / rows_all
    ridge_f = 0.1 * hours_all / rank
    ridge_x = 0.1 * rows_all
    lam = rows_all / 8.0

    half = rows // 2
    core = lax.axis_index(CORE)
    band = rank // lax.axis_size(SERIES)
    own_band = lax.axis_index(SERIES) * band
    place = lax.axis_index(TM)
    first, last = place == 0, place == lax.axis_size(TM) - 1

    keep = mask != 0
    wanted = observed.astype(jnp.float32)
    x_part = lax.dynamic_slice_in_dim(time_factors, own_band, band, 0)
    w_part = lax.dynamic_slice_in_dim(ar_weights, own_band, band, 1)
    f_full, x_full = series_factors, time_factors
    for _ in range(ITERS):
        f_low = f_full.astype(jnp.bfloat16)
        x_low = x_full.astype(jnp.bfloat16)
        product = jnp.dot(f_low, x_low, preferred_element_type=jnp.float32)
        misfit = jnp.where(keep, product - wanted, 0.0).astype(jnp.bfloat16)
        grad_f = lax.dot_general(
            misfit, x_low, (((1,), (1,)), ((), ())), preferred_element_type=jnp.float32
        )
        grad_x = lax.dot_general(
            f_low, misfit, (((0,), (0,)), ((), ())), preferred_element_type=jnp.float32
        )
        lag = lag_terms(x_part, w_part, first, last)
        theirs = lax.dynamic_slice_in_dim(grad_f, (1 - core) * half, half, 0)
        mine = lax.dynamic_slice_in_dim(grad_f, core * half, half, 0)
        mine = mine + lax.ppermute(theirs, CORE, SWAP)
        f_sum = scattered_sum(mine, FAR)
        x_sum = scattered_sum(grad_x, SERIES)
        x_push = x_sum + lam * lag
        x_part = x_part - step_x * (x_push + ridge_x * x_part)
        x_full = x_full - step_x * (gathered(x_push, SERIES) + ridge_x * x_full)
        mine = gathered(f_sum, FAR)
        theirs = lax.ppermute(mine, CORE, SWAP)
        f_sum = jnp.concatenate(
            [jnp.where(core == 0, mine, theirs), jnp.where(core == 0, theirs, mine)], axis=0
        )
        f_full = f_full - step_f * (f_sum + ridge_f * f_full)
    imputed = jnp.dot(
        f_full.astype(jnp.bfloat16), x_full.astype(jnp.bfloat16), preferred_element_type=jnp.float32
    ).astype(jnp.bfloat16)
    return f_full, x_full, imputed


def solution(mesh):
    far = mesh.shape["tm"] // 4
    near = mesh.shape["series"] // 2
    split = Mesh(
        mesh.devices.reshape(near, 2, far, 2, 2), (*SERIES, *TM)
    )
    in_specs = (P(SERIES, TM), P(SERIES, TM), P(SERIES, None), P(None, TM), P())
    out_specs = (P(SERIES, None), P(None, TM), P(SERIES, TM))
    return jax.shard_map(local, mesh=split, in_specs=in_specs, out_specs=out_specs, check_vma=False)
```

time: 363 us -> 209 us (0.58)
  the two profiles are of different devices: /device:TPU:1 before, /device:TPU:8 now
where the time goes in v1:
time: 209 us; the launch traced here: 208 us
  waiting for transfers between devices  104 us (50%)
  starting transfers between devices  59 us (28%)
  other arithmetic  20.3 us (10%)
  matrix products  13.1 us (6%)
  local copies, waits for them, and re-layouts  10.7 us (5%)
    all_to_all x4, waiting for transfers between devices, scattered_sum(): return lax.all_to_all(parts, axis, 0, 0, tiled=True).sum(axis=0)  57.3 us
    all_to_all x4, waiting for transfers between devices, gathered(): parts = lax.all_to_all(parts, axis, 0, 0, tiled=True)  40.9 us
    all_to_all x4, starting transfers between devices, scattered_sum(): return lax.all_to_all(parts, axis, 0, 0, tiled=True).sum(axis=0)  29.8 us
    all_to_all x4, starting transfers between devices, gathered(): parts = lax.all_to_all(parts, axis, 0, 0, tiled=True)  19.9 us
    ppermute x4, starting transfers between devices, passed_along(): return lax.ppermute(array, axis, pairs)  9.23 us
    dot_general x2, matrix products, local(): lax.dot_general(f_low, misfit, (((0,), (0,)), ((), ())), preferred_elemen...  4.57 us
    broadcast_in_dim x4, local copies, waits for them, and re-layouts, gathered(): parts = jnp.broadcast_to(array[None], (lax.axis_size(axis), *array.shape))  4.54 us
    ppermute x2, waiting for transfers between devices, local(): mine = mine + lax.ppermute(theirs, CORE, SWAP)  4.52 us
  transfers between devices with their start and end apart: 16, of which 11 were waited for; matrix products, arithmetic and copies ran while one was open for 9% of the time, Pallas kernels for 0%

profile of v1, /device:TPU:8, one launch (start us, length us, event | category | flops | bytes accessed | tf_op | source)
XLA Modules:
  0.0 207.6 jit_solution(3547173000361259632)
XLA Ops:
  0.7 3.7 %broadcast_compare_fusion = pred[1280,768]{1,0:T(32,128)(4,1)} fusion(s32[1280,768]{1,0:T(8,128)} %param.6), kind=kLoop, calls=%fused_computation.7 | loop fusion | flops 983040 | bytes 4915200 | tf_op jit(solution)/shard_map/ne | solution.py:71
  4.3 3.0 %fusion.2 = bf16[1280,768]{1,0:T(8,128)(2,1)S(1)} fusion(pred[1280,768]{1,0:T(32,128)(4,1)} %broadcast_compare_fusion, bf16[1280,768]{1,0:T(8,128)(2,1)} %param.5, f32[1280,256]{1,0:T(8,128)S(1)} %copy-done.1, f32[256,768]{1,0:T(8,128)} %param.8), kind=kOutput, calls=%fused_computation.5 | convolution fusion | flops 507772928 | bytes 7012352 | tf_op jit(solution)/shard_map/dot_general | solution.py:79
  11.2 2.4 %collective-permute-done = f32[640,256]{1,0:T(8,128)} collective-permute-done((f32[640,256]{1,0:T(8,128)}, f32[640,256]{1,0:T(8,128)}, u32[]{:S(2)}, u32[]{:S(2)}) %collective-permute-start) | collective-permute-done | bytes 655392 | tf_op jit(solution)/shard_map/ppermute | solution.py:90
  13.6 2.2 %dynamic-slice_add_fusion.1 = f32[640,256]{1,0:T(8,128)} fusion(f32[640,256]{1,0:T(8,128)} %collective-permute-done, f32[1280,256]{1,0:T(8,128)} %fusion.21, s32[]{:T(128)S(6)} %select_n.48), kind=kLoop, calls=%fused_computation.22 | loop fusion | flops 163840 | bytes 1966084 | tf_op jit(solution)/shard_map/add | solution.py:90
  15.8 10.3 %all-to-all-start = ((f32[16,40,256]{2,1,0:T(8,128)}), f32[16,40,256]{2,1,0:T(8,128)}, u32[]{:S(2)}, u32[]{:S(2)}) async-start(f32[16,40,256]{2,1,0:T(8,128)} %bitcast.43), calls=%async_computation | async-start | bytes 1310720 | tf_op jit(solution)/shard_map/all_to_all | solution.py:19
  27.8 20.6 %all-to-all-done = f32[16,40,256]{2,1,0:T(8,128)} async-done(((f32[16,40,256]{2,1,0:T(8,128)}), f32[16,40,256]{2,1,0:T(8,128)}, u32[]{:S(2)}, u32[]{:S(2)}) %all-to-all-start) | async-done | bytes 655392 | tf_op jit(solution)/shard_map/all_to_all | solution.py:19
  48.4 5.7 %all-to-all-start.2 = ((f32[8,32,768]{2,1,0:T(8,128)}), f32[8,32,768]{2,1,0:T(8,128)S(1)}, u32[]{:S(2)}, u32[]{:S(2)}) async-start(f32[8,32,768]{2,1,0:T(8,128)} %bitcast.40), calls=%async_computation.2 | async-start | bytes 1572864 | tf_op jit(solution)/shard_map/all_to_all | solution.py:19
  55.3 8.5 %all-to-all-done.2 = f32[8,32,768]{2,1,0:T(8,128)S(1)} async-done(((f32[8,32,768]{2,1,0:T(8,128)}), f32[8,32,768]{2,1,0:T(8,128)S(1)}, u32[]{:S(2)}, u32[]{:S(2)}) %all-to-all-start.2) | async-done | bytes 786464 | tf_op jit(solution)/shard_map/all_to_all | solution.py:19
  64.7 4.9 %all-to-all-start.1 = ((f32[16,40,256]{2,1,0:T(8,128)}), f32[16,40,256]{2,1,0:T(8,128)S(1)}, u32[]{:S(2)}, u32[]{:S(2)}) async-start(f32[16,40,256]{2,1,0:T(8,128)} %broadcast_in_dim.48), calls=%async_computation.1 | async-start | bytes 1310720 | tf_op jit(solution)/shard_map/all_to_all | solution.py:24
  71.7 3.6 %collective-permute-start.3 = (f32[32,168]{1,0:T(8,128)}, f32[32,168]{1,0:T(8,128)}, u32[]{:S(2)}, u32[]{:S(2)}) collective-permute-start(f32[32,168]{1,0:T(8,128)} %get-tuple-element.10), channel_id=1, source_target_pairs={{0,1},{1,2},{2,3},{3,4},{4,5},{5,6},{6,7},{7,8},{8,9},{9,10},{10,1... | collective-permute-start | bytes 64520 | tf_op jit(solution)/shard_map/ppermute | solution.py:31
  82.9 7.8 %all-to-all-done.1 = f32[16,40,256]{2,1,0:T(8,128)S(1)} async-done(((f32[16,40,256]{2,1,0:T(8,128)}), f32[16,40,256]{2,1,0:T(8,128)S(1)}, u32[]{:S(2)}, u32[]{:S(2)}) %all-to-all-start.1) | async-done | bytes 655392 | tf_op jit(solution)/shard_map/all_to_all | solution.py:24
  91.6 5.4 %all-to-all-start.3 = ((f32[8,32,768]{2,1,0:T(8,128)}), f32[8,32,768]{2,1,0:T(8,128)S(1)}, u32[]{:S(2)}, u32[]{:S(2)}) async-start(f32[8,32,768]{2,1,0:T(8,128)} %broadcast_in_dim.51), calls=%async_computation.3 | async-start | bytes 1572864 | tf_op jit(solution)/shard_map/all_to_all | solution.py:24
  97.0 8.9 %all-to-all-done.3 = f32[8,32,768]{2,1,0:T(8,128)S(1)} async-done(((f32[8,32,768]{2,1,0:T(8,128)}), f32[8,32,768]{2,1,0:T(8,128)S(1)}, u32[]{:S(2)}, u32[]{:S(2)}) %all-to-all-start.3) | async-done | bytes 786464 | tf_op jit(solution)/shard_map/all_to_all | solution.py:24
  110.1 2.1 %collective-permute-done.4 = f32[640,256]{1,0:T(8,128)S(1)} collective-permute-done((f32[640,256]{1,0:T(8,128)S(1)}, f32[640,256]{1,0:T(8,128)S(1)}, u32[]{:S(2)}, u32[]{:S(2)}) %collective-permute-start.4) | collective-permute-done | bytes 655392 | tf_op jit(solution)/shard_map/ppermute | solution.py:90
  113.1 8.9 %all-to-all-start.4 = ((f32[16,40,256]{2,1,0:T(8,128)}), f32[16,40,256]{2,1,0:T(8,128)}, u32[]{:S(2)}, u32[]{:S(2)}) async-start(f32[16,40,256]{2,1,0:T(8,128)} %bitcast.42), calls=%async_computation.4 | async-start | bytes 1310720 | tf_op jit(solution)/shard_map/all_to_all | solution.py:19
  122.0 3.0 %fusion.14 = f32[256,768]{1,0:T(8,128)} fusion(bf16[1280,768]{1,0:T(8,128)(2,1)S(1)} %fusion.3, f32[1280,256]{1,0:T(8,128)S(1)} %copy-done.1, f32[640,256]{1,0:T(8,128)} %copy-done.7, f32[640,256]{1,0:T(8,128)} %copy-done.5), kind=kOutput, calls=%fused_computation.24 | convolution fusion | flops 505282560 | bytes 5373952 | tf_op jit(solution)/shard_map/dot_general | solution.py:84
  125.0 19.4 %all-to-all-done.4 = f32[16,40,256]{2,1,0:T(8,128)} async-done(((f32[16,40,256]{2,1,0:T(8,128)}), f32[16,40,256]{2,1,0:T(8,128)}, u32[]{:S(2)}, u32[]{:S(2)}) %all-to-all-start.4) | async-done | bytes 655392 | tf_op jit(solution)/shard_map/all_to_all | solution.py:19
  144.4 4.8 %all-to-all-start.6 = ((f32[8,32,768]{2,1,0:T(8,128)}), f32[8,32,768]{2,1,0:T(8,128)S(1)}, u32[]{:S(2)}, u32[]{:S(2)}) async-start(f32[8,32,768]{2,1,0:T(8,128)} %bitcast.41), calls=%async_computation.6 | async-start | bytes 1572864 | tf_op jit(solution)/shard_map/all_to_all | solution.py:19
  150.4 8.8 %all-to-all-done.6 = f32[8,32,768]{2,1,0:T(8,128)S(1)} async-done(((f32[8,32,768]{2,1,0:T(8,128)}), f32[8,32,768]{2,1,0:T(8,128)S(1)}, u32[]{:S(2)}, u32[]{:S(2)}) %all-to-all-start.6) | async-done | bytes 786464 | tf_op jit(solution)/shard_map/all_to_all | solution.py:19
  160.1 4.8 %all-to-all-start.5 = ((f32[16,40,256]{2,1,0:T(8,128)}), f32[16,40,256]{2,1,0:T(8,128)S(1)}, u32[]{:S(2)}, u32[]{:S(2)}) async-start(f32[16,40,256]{2,1,0:T(8,128)} %broadcast_in_dim.52), calls=%async_computation.5 | async-start | bytes 1310720 | tf_op jit(solution)/shard_map/all_to_all | solution.py:24
  166.2 3.0 %collective-permute-start.7 = (f32[32,168]{1,0:T(8,128)S(1)}, f32[32,168]{1,0:T(8,128)S(1)}, u32[]{:S(2)}, u32[]{:S(2)}) collective-permute-start(f32[32,168]{1,0:T(8,128)S(1)} %get-tuple-element.12), channel_id=1, source_target_pairs={{0,1},{1,2},{2,3},{3,4},{4,5},{5,6},{6,7},{7,8},{8,9},{9,10},{10,1... | collective-permute-start | bytes 64520 | tf_op jit(solution)/shard_map/ppermute | solution.py:31
  171.3 15.1 %all-to-all-done.5 = f32[16,40,256]{2,1,0:T(8,128)S(1)} async-done(((f32[16,40,256]{2,1,0:T(8,128)}), f32[16,40,256]{2,1,0:T(8,128)S(1)}, u32[]{:S(2)}, u32[]{:S(2)}) %all-to-all-start.5) | async-done | bytes 655392 | tf_op jit(solution)/shard_map/all_to_all | solution.py:24
  188.2 4.8 %all-to-all-start.7 = ((f32[8,32,768]{2,1,0:T(8,128)}), f32[8,32,768]{2,1,0:T(8,128)}, u32[]{:S(2)}, u32[]{:S(2)}) async-start(f32[8,32,768]{2,1,0:T(8,128)} %broadcast_in_dim.53), calls=%async_computation.7 | async-start | bytes 1572864 | tf_op jit(solution)/shard_map/all_to_all | solution.py:24
  193.0 9.1 %all-to-all-done.7 = f32[8,32,768]{2,1,0:T(8,128)} async-done(((f32[8,32,768]{2,1,0:T(8,128)}), f32[8,32,768]{2,1,0:T(8,128)}, u32[]{:S(2)}, u32[]{:S(2)}) %all-to-all-start.7) | async-done | bytes 786464 | tf_op jit(solution)/shard_map/all_to_all | solution.py:24
  (79 shorter events, 35.6 us)
Async XLA Ops:
  0.6 74.7 %copy-start = (f32[3,256]{1,0:T(4,128)S(1)}, f32[3,256]{1,0:T(4,128)}, u32[]{:S(2)}) copy-start(f32[3,256]{1,0:T(4,128)} %param.9) | copy-start | bytes 9220
  0.7 3.7 %copy-start.1 = (f32[1280,256]{1,0:T(8,128)S(1)}, f32[1280,256]{1,0:T(8,128)}, u32[]{:S(2)}) copy-start(f32[1280,256]{1,0:T(8,128)} %param.7) | copy-start | bytes 3932164
  4.3 3.1 %copy-start.2 = (f32[256,768]{1,0:T(8,128)S(1)}, f32[256,768]{1,0:T(8,128)}, u32[]{:S(2)}) copy-start(f32[256,768]{1,0:T(8,128)} %param.8) | copy-start | bytes 2359300
  11.2 2.4 %collective-permute-start = (f32[640,256]{1,0:T(8,128)}, f32[640,256]{1,0:T(8,128)}, u32[]{:S(2)}, u32[]{:S(2)}) collective-permute-start(f32[640,256]{1,0:T(8,128)} %constant_dynamic-slice_fusion.4), channel_id=1, source_target_pairs={{0,1},{1,0},{2,3},{3,2},{4,5},{5,4},{6,7},{7,6},{8,9},{9,8},{10,11... | collective-permute-start | bytes 1966088 | tf_op jit(solution)/shard_map/ppermute | solution.py:90
  15.8 32.6 %all-to-all-start = ((f32[16,40,256]{2,1,0:T(8,128)}), f32[16,40,256]{2,1,0:T(8,128)}, u32[]{:S(2)}, u32[]{:S(2)}) async-start(f32[16,40,256]{2,1,0:T(8,128)} %bitcast.43), calls=%async_computation | async-start | bytes 1310720 | tf_op jit(solution)/shard_map/all_to_all | solution.py:19
  48.4 15.5 %all-to-all-start.2 = ((f32[8,32,768]{2,1,0:T(8,128)}), f32[8,32,768]{2,1,0:T(8,128)S(1)}, u32[]{:S(2)}, u32[]{:S(2)}) async-start(f32[8,32,768]{2,1,0:T(8,128)} %bitcast.40), calls=%async_computation.2 | async-start | bytes 1572864 | tf_op jit(solution)/shard_map/all_to_all | solution.py:19
  54.1 15.6 %copy-start.3 = (f32[256,768]{1,0:T(8,128)S(1)}, f32[256,768]{1,0:T(8,128)}, u32[]{:S(2)}) copy-start(f32[256,768]{1,0:T(8,128)} %param.8) | copy-start | bytes 2359300
  64.7 26.0 %all-to-all-start.1 = ((f32[16,40,256]{2,1,0:T(8,128)}), f32[16,40,256]{2,1,0:T(8,128)S(1)}, u32[]{:S(2)}, u32[]{:S(2)}) async-start(f32[16,40,256]{2,1,0:T(8,128)} %broadcast_in_dim.48), calls=%async_computation.1 | async-start | bytes 1310720 | tf_op jit(solution)/shard_map/all_to_all | solution.py:24
  70.4 6.2 %collective-permute-start.2 = (f32[32,168]{1,0:T(8,128)}, f32[32,168]{1,0:T(8,128)}, u32[]{:S(2)}, u32[]{:S(2)}) collective-permute-start(f32[32,168]{1,0:T(8,128)} %get-tuple-element.9), channel_id=1, source_target_pairs={{1,0},{2,1},{3,2},{4,3},{5,4},{6,5},{7,6},{8,7},{9,8},{10,9},{11,1... | collective-permute-start | bytes 64520 | tf_op jit(solution)/shard_map/ppermute | solution.py:31
  71.7 4.9 %collective-permute-start.3 = (f32[32,168]{1,0:T(8,128)}, f32[32,168]{1,0:T(8,128)}, u32[]{:S(2)}, u32[]{:S(2)}) collective-permute-start(f32[32,168]{1,0:T(8,128)} %get-tuple-element.10), channel_id=1, source_target_pairs={{0,1},{1,2},{2,3},{3,4},{4,5},{5,6},{6,7},{7,8},{8,9},{9,10},{10,1... | collective-permute-start | bytes 64520 | tf_op jit(solution)/shard_map/ppermute | solution.py:31
  91.6 14.3 %all-to-all-start.3 = ((f32[8,32,768]{2,1,0:T(8,128)}), f32[8,32,768]{2,1,0:T(8,128)S(1)}, u32[]{:S(2)}, u32[]{:S(2)}) async-start(f32[8,32,768]{2,1,0:T(8,128)} %broadcast_in_dim.51), calls=%async_computation.3 | async-start | bytes 1572864 | tf_op jit(solution)/shard_map/all_to_all | solution.py:24
  97.0 9.1 %collective-permute-start.1 = (f32[640,256]{1,0:T(8,128)S(1)}, f32[640,256]{1,0:T(8,128)}, u32[]{:S(2)}, u32[]{:S(2)}) collective-permute-start(f32[640,256]{1,0:T(8,128)S(1)} %bitcast.44), channel_id=1, source_target_pairs={{0,1},{1,0},{2,3},{3,2},{4,5},{5,4},{6,7},{7,6},{8,9},{9,8},{10,11... | collective-permute-start | bytes 1966088 | tf_op jit(solution)/shard_map/ppermute | solution.py:97
  110.0 2.2 %collective-permute-start.4 = (f32[640,256]{1,0:T(8,128)S(1)}, f32[640,256]{1,0:T(8,128)S(1)}, u32[]{:S(2)}, u32[]{:S(2)}) collective-permute-start(f32[640,256]{1,0:T(8,128)S(1)} %constant_dynamic-slice_fusion.1), channel_id=1, source_target_pairs={{0,1},{1,0},{2,3},{3,2},{4,5},{5,4},{6,7},{7,6},{8,9},{9,8},{10,11... | collective-permute-start | bytes 1966088 | tf_op jit(solution)/shard_map/ppermute | solution.py:90
  113.1 31.3 %all-to-all-start.4 = ((f32[16,40,256]{2,1,0:T(8,128)}), f32[16,40,256]{2,1,0:T(8,128)}, u32[]{:S(2)}, u32[]{:S(2)}) async-start(f32[16,40,256]{2,1,0:T(8,128)} %bitcast.42), calls=%async_computation.4 | async-start | bytes 1310720 | tf_op jit(solution)/shard_map/all_to_all | solution.py:19
  144.4 14.8 %all-to-all-start.6 = ((f32[8,32,768]{2,1,0:T(8,128)}), f32[8,32,768]{2,1,0:T(8,128)S(1)}, u32[]{:S(2)}, u32[]{:S(2)}) async-start(f32[8,32,768]{2,1,0:T(8,128)} %bitcast.41), calls=%async_computation.6 | async-start | bytes 1572864 | tf_op jit(solution)/shard_map/all_to_all | solution.py:19
  149.2 15.6 %copy-start.15 = (f32[32,768]{1,0:T(8,128)S(1)}, f32[32,768]{1,0:T(8,128)}, u32[]{:S(2)}) copy-start(f32[32,768]{1,0:T(8,128)} %get-tuple-element.3) | copy-start | bytes 294916
  150.4 19.8 %copy-start.16 = (pred[936]{0:T(1024)(128)(4,1)S(1)}, pred[936]{0:T(1024)(128)(4,1)}, u32[]{:S(2)}) copy-start(pred[936]{0:T(1024)(128)(4,1)} %fusion.43) | copy-start | bytes 2812
  160.1 26.3 %all-to-all-start.5 = ((f32[16,40,256]{2,1,0:T(8,128)}), f32[16,40,256]{2,1,0:T(8,128)S(1)}, u32[]{:S(2)}, u32[]{:S(2)}) async-start(f32[16,40,256]{2,1,0:T(8,128)} %broadcast_in_dim.52), calls=%async_computation.5 | async-start | bytes 1310720 | tf_op jit(solution)/shard_map/all_to_all | solution.py:24
  164.9 4.3 %collective-permute-start.6 = (f32[32,168]{1,0:T(8,128)S(1)}, f32[32,168]{1,0:T(8,128)S(1)}, u32[]{:S(2)}, u32[]{:S(2)}) collective-permute-start(f32[32,168]{1,0:T(8,128)S(1)} %get-tuple-element.11), channel_id=1, source_target_pairs={{1,0},{2,1},{3,2},{4,3},{5,4},{6,5},{7,6},{8,7},{9,8},{10,9},{11,1... | collective-permute-start | bytes 64520 | tf_op jit(solution)/shard_map/ppermute | solution.py:31
  166.2 3.9 %collective-permute-start.7 = (f32[32,168]{1,0:T(8,128)S(1)}, f32[32,168]{1,0:T(8,128)S(1)}, u32[]{:S(2)}, u32[]{:S(2)}) collective-permute-start(f32[32,168]{1,0:T(8,128)S(1)} %get-tuple-element.12), channel_id=1, source_target_pairs={{0,1},{1,2},{2,3},{3,4},{4,5},{5,6},{6,7},{7,8},{8,9},{9,10},{10,1... | collective-permute-start | bytes 64520 | tf_op jit(solution)/shard_map/ppermute | solution.py:31
  171.3 30.9 %copy-start.4 = (f32[256,768]{1,0:T(8,128)S(1)}, f32[256,768]{1,0:T(8,128)}, u32[]{:S(2)}) copy-start(f32[256,768]{1,0:T(8,128)} %param.8) | copy-start | bytes 2359300
  171.3 30.9 %copy-start.12 = (f32[8,32,768]{2,1,0:T(8,128)S(1)}, f32[8,32,768]{2,1,0:T(8,128)}, u32[]{:S(2)}) copy-start(f32[8,32,768]{2,1,0:T(8,128)} %copy-done.11) | copy-start | bytes 2359300
  188.2 13.9 %all-to-all-start.7 = ((f32[8,32,768]{2,1,0:T(8,128)}), f32[8,32,768]{2,1,0:T(8,128)}, u32[]{:S(2)}, u32[]{:S(2)}) async-start(f32[8,32,768]{2,1,0:T(8,128)} %broadcast_in_dim.53), calls=%async_computation.7 | async-start | bytes 1572864 | tf_op jit(solution)/shard_map/all_to_all | solution.py:24
  193.0 10.5 %collective-permute-start.5 = (f32[640,256]{1,0:T(8,128)S(1)}, f32[640,256]{1,0:T(8,128)}, u32[]{:S(2)}, u32[]{:S(2)}) collective-permute-start(f32[640,256]{1,0:T(8,128)S(1)} %bitcast.45), channel_id=1, source_target_pairs={{0,1},{1,0},{2,3},{3,2},{4,5},{5,4},{6,7},{7,6},{8,9},{9,8},{10,11... | collective-permute-start | bytes 1966088 | tf_op jit(solution)/shard_map/ppermute | solution.py:97
  (9 other events, 16.5 us)

commit v2 on v1

v2 whole, which is shorter than its diff:
```python
import functools

import jax
import jax.numpy as jnp
from jax import lax
from jax.experimental import pallas as pl
from jax.experimental.pallas import tpu as pltpu
from jax.sharding import Mesh
from jax.sharding import PartitionSpec as P

ITERS = 2
LAGS = (1, 24, 168)
EDGE = 168
SERIES = ("x", "y_lo")
FAR = ("z", "y_hi")
CORE = "core"
TM = (*FAR, CORE)
SWAP = ((0, 1), (1, 0))
STEPS = 2
HIDDEN = 1e30
PARAMS = pltpu.CompilerParams(
    vmem_limit_bytes=20 * 2**20, dimension_semantics=("arbitrary",)
)
BF16, F32 = jnp.bfloat16, jnp.float32


def scattered_sum(array, axis):
    parts = array.reshape(lax.axis_size(axis), -1, array.shape[-1])
    return lax.all_to_all(parts, axis, 0, 0, tiled=True).sum(axis=0)


def gathered(array, axis):
    parts = jnp.broadcast_to(array[None], (lax.axis_size(axis), *array.shape))
    parts = lax.all_to_all(parts, axis, 0, 0, tiled=True)
    return parts.reshape(-1, array.shape[-1])


def traded(array, axis, bits):
    length = lax.axis_size(axis)
    return lax.ppermute(array, axis, [(i, i ^ bits) for i in range(length)])


def passed_along(array, axis, by):
    length = lax.axis_size(axis)
    pairs = [(i, i + by) for i in range(length) if 0 <= i + by < length]
    return lax.ppermute(array, axis, pairs)


def edges_of(now):
    return passed_along(now[:, -EDGE:], TM, 1), passed_along(now[:, :EDGE], TM, -1)


def lag_terms(now, edges, weights, first, last):
    before, after = edges
    hours = now.shape[1]
    wide = jnp.concatenate([before, now, after], axis=1)
    length = hours + EDGE
    resid = wide[:, EDGE:]
    for lag, weight in zip(LAGS, weights):
        resid = resid - weight[:, None] * wide[:, EDGE - lag : EDGE - lag + length]
    column = jnp.arange(length)
    inside = (~first | (column >= EDGE)) & (~last | (column < hours))
    resid = jnp.where(inside[None, :], resid, 0.0)
    back = None
    for lag, weight in zip(LAGS, weights):
        term = weight[:, None] * resid[:, lag : lag + hours]
        back = term if back is None else back + term
    return resid[:, :hours] - back


def natural(i, core):
    return ((i // STEPS + 1 + core) % 2) * STEPS + i % STEPS


def dot(a, b):
    return jnp.dot(a, b, preferred_element_type=F32)


def gradient(misfit, x_low, theirs_ref, mine_ref):
    grad = lax.dot_general(
        misfit, x_low, (((1,), (1,)), ((), ())), preferred_element_type=F32
    )

    @pl.when(pl.program_id(0) < STEPS)
    def _():
        theirs_ref[...] = grad

    @pl.when(pl.program_id(0) >= STEPS)
    def _():
        mine_ref[...] = grad


def first_pass(core_ref, x_ref, f_ref, seen_ref, mask_ref, theirs_ref, mine_ref, misfit_ref, f_low_ref, kept_ref, x_low_ref):
    @pl.when(pl.program_id(0) == 0)
    def _():
        x_low_ref[...] = x_ref[...].astype(BF16)

    x_low = x_low_ref[...]
    f_low = f_ref[...].astype(BF16)
    keep = mask_ref[...] != 0
    seen = seen_ref[...].astype(F32)
    misfit = jnp.where(keep, dot(f_low, x_low) - seen, 0.0).astype(BF16)
    kept_ref[...] = jnp.where(keep, seen, HIDDEN).astype(BF16)
    f_low_ref[...] = f_low
    misfit_ref[...] = misfit
    gradient(misfit, x_low, theirs_ref, mine_ref)


def assembled(along, pieces, *outs):
    for k, piece in enumerate(pieces):
        size = piece.shape[0]
        start = pl.multiple_of((along ^ k) * size, size)
        for out in outs:
            out[pl.ds(start, size), :] = piece[...].astype(out.dtype)


def later_pass(place_ref, *refs):
    *pieces, f_theirs_ref, f_mine_ref, kept_ref = refs[:-5]
    theirs_ref, mine_ref, misfit_ref, f_low_ref, x_low_ref = refs[-5:]

    @pl.when(pl.program_id(0) == 0)
    def _():
        assembled(place_ref[1], pieces, x_low_ref)

    x_low = x_low_ref[...]
    f_low = jnp.where(pl.program_id(0) < STEPS, f_theirs_ref[...], f_mine_ref[...]).astype(BF16)
    kept = kept_ref[...].astype(F32)
    misfit = jnp.where(kept < HIDDEN / 2, dot(f_low, x_low) - kept, 0.0).astype(BF16)
    f_low_ref[...] = f_low
    misfit_ref[...] = misfit
    gradient(misfit, x_low, theirs_ref, mine_ref)


def last_pass(place_ref, *refs):
    *pieces, f_theirs_ref, f_mine_ref = refs[:-4]
    f_ref, x_ref, imputed_ref, x_low_ref = refs[-4:]

    @pl.when(pl.program_id(0) == 0)
    def _():
        assembled(place_ref[1], pieces, x_low_ref, x_ref)

    f_now = jnp.where(pl.program_id(0) < STEPS, f_theirs_ref[...], f_mine_ref[...])
    f_ref[...] = f_now
    imputed_ref[...] = dot(f_now.astype(BF16), x_low_ref[...]).astype(BF16)


def row_pass(kernel, place, ins, outs, rank, hours, name):
    def spec(kind, shape):
        maps = {
            "whole": lambda i, p: (0, 0),
            "natural": lambda i, p: (natural(i, p[0]), 0),
            "step": lambda i, p: (i, 0),
            "theirs": lambda i, p: (jnp.minimum(i, STEPS - 1), 0),
            "mine": lambda i, p: (jnp.maximum(i - STEPS, 0), 0),
        }
        tiles = {"whole": 1, "theirs": STEPS, "mine": STEPS}.get(kind, 2 * STEPS)
        return pl.BlockSpec((shape[0] // tiles, shape[1]), maps[kind])

    rows = max(s.shape[0] for _, s in outs)
    moved = sum(a.size * a.dtype.itemsize for _, a in [*ins, *outs])
    return pl.pallas_call(
        kernel,
        out_shape=[s for _, s in outs],
        grid_spec=pltpu.PrefetchScalarGridSpec(
            num_scalar_prefetch=1,
            grid=(2 * STEPS,),
            in_specs=[spec(k, a.shape) for k, a in ins],
            out_specs=[spec(k, s.shape) for k, s in outs],
            scratch_shapes=[pltpu.VMEM((rank, hours), BF16)],
        ),
        compiler_params=PARAMS,
        cost_estimate=pl.CostEstimate(
            flops=4 * rows * rank * hours, bytes_accessed=moved, transcendentals=0
        ),
        name=name,
    )(place, *[a for _, a in ins])


def local(observed, mask, series_factors, time_factors, ar_weights):
    rows, hours = observed.shape
    rank = time_factors.shape[0]
    hours_all = hours * lax.axis_size(TM)
    rows_all = rows * lax.axis_size(SERIES)
    step_f = rank / hours_all
    step_x = 1.0 / rows_all
    ridge_f = 0.1 * hours_all / rank
    ridge_x = 0.1 * rows_all
    lam = rows_all / 8.0

    half = rows // 2
    core = lax.axis_index(CORE)
    line = half // lax.axis_size(FAR)
    own_row = core * half + lax.axis_index(FAR) * line
    peers = lax.axis_size("x")
    band = rank // peers
    along = lax.axis_index("x")
    position = lax.axis_index(TM)
    first, last = position == 0, position == lax.axis_size(TM) - 1
    place = jnp.stack([core, along])

    def shape(n, m, dtype=F32):
        return jax.ShapeDtypeStruct((n, m), dtype)

    grads = [
        ("theirs", shape(half, rank)),
        ("mine", shape(half, rank)),
        ("step", shape(rows, hours, BF16)),
        ("step", shape(rows, rank, BF16)),
    ]
    f_part = lax.dynamic_slice_in_dim(series_factors, own_row, line, 0)
    x_part = lax.dynamic_slice_in_dim(time_factors, along * band, band, 0)
    w_part = lax.dynamic_slice_in_dim(ar_weights, along * band, band, 1)
    for sweep in range(ITERS):
        if sweep == 0:
            theirs, mine, misfit, f_low, kept = row_pass(
                first_pass,
                place,
                [("whole", time_factors), ("natural", series_factors), ("natural", observed), ("natural", mask)],
                [*grads, ("step", shape(rows, hours, BF16))],
                rank,
                hours,
                "first_pass",
            )
        else:
            theirs, mine, misfit, f_low = row_pass(
                later_pass,
                place,
                [*[("whole", p) for p in pieces], ("theirs", f_theirs), ("mine", f_mine), ("step", kept)],
                grads,
                rank,
                hours,
                "later_pass",
            )
        mine = mine + lax.ppermute(theirs, CORE, SWAP)
        grad_x = lax.dot_general(
            f_low, misfit, (((0,), (0,)), ((), ())), preferred_element_type=F32
        )
        mine, grad_x, x_part = lax.optimization_barrier((mine, grad_x, x_part))
        if sweep == 0:
            edges = edges_of(x_part)
        f_sum = scattered_sum(mine, FAR)
        x_sum = lax.dynamic_slice_in_dim(grad_x, along * band, band, 0)
        for k in range(1, peers):
            part = lax.dynamic_slice_in_dim(grad_x, (along ^ k) * band, band, 0)
            x_sum = x_sum + traded(part, "x", k)
        x_sum = x_sum + lax.ppermute(x_sum, "y_lo", SWAP)
        lag = lag_terms(x_part, edges, w_part, first, last)
        f_part = f_part - step_f * (f_sum + ridge_f * f_part)
        x_part = x_part - step_x * (x_sum + ridge_x * x_part + lam * lag)
        f_part, x_part = lax.optimization_barrier((f_part, x_part))
        f_mine = gathered(f_part, FAR)
        pieces = [x_part] + [traded(x_part, "x", k) for k in range(1, peers)]
        if sweep + 1 < ITERS:
            edges = edges_of(x_part)
            f_mine, pieces, edges = lax.optimization_barrier((f_mine, pieces, edges))
        else:
            f_mine, pieces = lax.optimization_barrier((f_mine, pieces))
        f_theirs = lax.ppermute(f_mine, CORE, SWAP)
    return row_pass(
        last_pass,
        place,
        [*[("whole", p) for p in pieces], ("theirs", f_theirs), ("mine", f_mine)],
        [("natural", shape(rows, rank)), ("whole", shape(rank, hours)), ("natural", shape(rows, hours, BF16))],
        rank,
        hours,
        "last_pass",
    )


def solution(mesh):
    far = mesh.shape["tm"] // 4
    near = mesh.shape["series"] // 2
    split = Mesh(mesh.devices.reshape(near, 2, far, 2, 2), (*SERIES, *TM))
    in_specs = (P(SERIES, TM), P(SERIES, TM), P(SERIES, None), P(None, TM), P())
    out_specs = (P(SERIES, None), P(None, TM), P(SERIES, TM))
    return jax.shard_map(local, mesh=split, in_specs=in_specs, out_specs=out_specs, check_vma=False)
```

time: 209 us -> 159 us (0.76)
  the two profiles are of different devices: /device:TPU:8 before, /device:TPU:1 now
where the time goes in v2:
time: 159 us; the launch traced here: 158 us
  starting transfers between devices  74.3 us (47%)
  waiting for transfers between devices  48.1 us (30%)
  local copies, waits for them, and re-layouts  14 us (9%)
  Pallas kernels  10.1 us (6%)
  other arithmetic  6.29 us (4%)
  matrix products  3.84 us (2%)
    ppermute x4, starting transfers between devices, passed_along(): return lax.ppermute(array, axis, pairs)  17.7 us
    all_to_all x2, starting transfers between devices, gathered(): parts = lax.all_to_all(parts, axis, 0, 0, tiled=True)  16.5 us
    ppermute x12, waiting for transfers between devices, traded(): return lax.ppermute(array, axis, [(i, i ^ bits) for i in range(length)])  16.3 us
    ppermute x12, starting transfers between devices, traded(): return lax.ppermute(array, axis, [(i, i ^ bits) for i in range(length)])  14.8 us
    ppermute x2, waiting for transfers between devices, local(): x_sum = x_sum + lax.ppermute(x_sum, 'y_lo', SWAP)  12.9 us
    all_to_all x2, starting transfers between devices, scattered_sum(): return lax.all_to_all(parts, axis, 0, 0, tiled=True).sum(axis=0)  12.8 us
    pallas_call x3, Pallas kernels, row_pass(): pl.pallas_call(kernel, out_shape=[s for _, s in outs], grid_spec=pltpu.Pr...  10.1 us
    all_to_all x2, waiting for transfers between devices, gathered(): parts = lax.all_to_all(parts, axis, 0, 0, tiled=True)  8.55 us
  transfers between devices with their start and end apart: 26, of which 15 were waited for; matrix products, arithmetic and copies ran while one was open for 7% of the time, Pallas kernels for 0%

profile of v2, /device:TPU:1, one launch (start us, length us, event | category | flops | bytes accessed | tf_op | source)
XLA Modules:
  0.0 157.6 jit_solution(17825658721674867568)
XLA Ops:
  6.8 3.9 %first_pass.1 = (f32[640,256]{1,0:T(8,128)}, f32[640,256]{1,0:T(8,128)S(1)}, bf16[1280,768]{1,0:T(8,128)(2,1)S(1)}, bf16[1280,256]{1,0:T(8,128)(2,1)S(1)}, bf16[1280,768]{1,0:T(8,128)(2,1)S(1)}) custom-call(s32[2]{0:T(128)S(1)} %pad_add_fusion.core_ref.place_ref, f32[256,768]{1,0:T(8,128)S(1)} %copy-done.5, f32[1280,256]{1,0:T(8,128)S(1)} %copy-done.4, ...), custom_call_target="tpu_custom_call" | custom-call | flops 1006632960 | bytes 13893632 | tf_op jit(solution)/shard_map/first_pass/pallas_call | solution.py:161
  12.0 3.2 %collective-permute-start = (f32[640,256]{1,0:T(8,128)}, f32[640,256]{1,0:T(8,128)}, u32[]{:S(2)}, u32[]{:S(2)}) collective-permute-start(f32[640,256]{1,0:T(8,128)} %get-tuple-element.35), channel_id=1, source_target_pairs={{0,1},{1,0},{2,3},{3,2},{4,5},{5,4},{6,7},{7,6},{8,9},{9,8},{10,11... | collective-permute-start | bytes 1966088 | tf_op jit(solution)/shard_map/ppermute | solution.py:234
  16.9 3.1 %fusion.27 = f32[256,768]{1,0:T(8,128)} fusion(bf16[1280,256]{1,0:T(8,128)(2,1)S(1)} %get-tuple-element.36, bf16[1280,768]{1,0:T(8,128)(2,1)} %copy-done.2), kind=kOutput, calls=%fused_computation.57 | convolution fusion | flops 503316480 | bytes 3407872 | tf_op jit(solution)/shard_map/dot_general | solution.py:235
  22.1 9.2 %all-to-all-start = ((f32[16,40,256]{2,1,0:T(8,128)}), f32[16,40,256]{2,1,0:T(8,128)S(1)}, u32[]{:S(2)}, u32[]{:S(2)}) async-start(f32[16,40,256]{2,1,0:T(8,128)} %bitcast.2), calls=%async_computation | async-start | bytes 1310720 | tf_op jit(solution)/shard_map/all_to_all | solution.py:29
  37.1 2.7 %collective-permute-start.5 = (f32[64,168]{1,0:T(8,128)S(1)}, f32[64,168]{1,0:T(8,128)S(1)}, u32[]{:S(2)}, u32[]{:S(2)}) collective-permute-start(f32[64,168]{1,0:T(8,128)S(1)} %get-tuple-element.73), channel_id=1, source_target_pairs={{1,0},{2,1},{3,2},{4,3},{5,4},{6,5},{7,6},{8,7},{9,8},{10,9},{11,1... | collective-permute-start | bytes 129032 | tf_op jit(solution)/shard_map/ppermute | solution.py:46
  39.8 5.0 %collective-permute-start.6 = (f32[64,168]{1,0:T(8,128)S(1)}, f32[64,168]{1,0:T(8,128)S(1)}, u32[]{:S(2)}, u32[]{:S(2)}) collective-permute-start(f32[64,168]{1,0:T(8,128)S(1)} %get-tuple-element.74), channel_id=1, source_target_pairs={{0,1},{1,2},{2,3},{3,4},{4,5},{5,6},{6,7},{7,8},{8,9},{9,10},{10,1... | collective-permute-start | bytes 129032 | tf_op jit(solution)/shard_map/ppermute | solution.py:46
  48.7 5.1 %collective-permute-done.4 = f32[64,768]{1,0:T(8,128)S(1)} collective-permute-done((f32[64,768]{1,0:T(8,128)S(1)}, f32[64,768]{1,0:T(8,128)S(1)}, u32[]{:S(2)}, u32[]{:S(2)}) %collective-permute-start.4) | collective-permute-done | bytes 196640 | tf_op jit(solution)/shard_map/ppermute | solution.py:246
  55.8 9.5 %all-to-all-start.1 = ((f32[16,40,256]{2,1,0:T(8,128)}), f32[16,40,256]{2,1,0:T(8,128)S(1)}, u32[]{:S(2)}, u32[]{:S(2)}) async-start(f32[16,40,256]{2,1,0:T(8,128)} %broadcast_in_dim.32), calls=%async_computation.1 | async-start | bytes 1310720 | tf_op jit(solution)/shard_map/all_to_all | solution.py:34
  65.3 2.6 %collective-permute-start.9 = (f32[64,768]{1,0:T(8,128)S(1)}, f32[64,768]{1,0:T(8,128)S(1)}, u32[]{:S(2)}, u32[]{:S(2)}) collective-permute-start(f32[64,768]{1,0:T(8,128)S(1)} %fusion.20.refs_0_), channel_id=1, source_target_pairs={{0,192},{64,128},{128,64},{192,0},{1,193},{65,129},{129,65},{193,1... | collective-permute-start | bytes 589832 | tf_op jit(solution)/shard_map/ppermute | solution.py:40
  68.7 5.1 %collective-permute-start.11 = (f32[64,168]{1,0:T(8,128)S(1)}, f32[64,168]{1,0:T(8,128)S(1)}, u32[]{:S(2)}, u32[]{:S(2)}) collective-permute-start(f32[64,168]{1,0:T(8,128)S(1)} %get-tuple-element.71), channel_id=1, source_target_pairs={{1,0},{2,1},{3,2},{4,3},{5,4},{6,5},{7,6},{8,7},{9,8},{10,9},{11,1... | collective-permute-start | bytes 129032 | tf_op jit(solution)/shard_map/ppermute | solution.py:46
  73.8 4.9 %collective-permute-start.10 = (f32[64,168]{1,0:T(8,128)S(1)}, f32[64,168]{1,0:T(8,128)S(1)}, u32[]{:S(2)}, u32[]{:S(2)}) collective-permute-start(f32[64,168]{1,0:T(8,128)S(1)} %get-tuple-element.72), channel_id=1, source_target_pairs={{0,1},{1,2},{2,3},{3,4},{4,5},{5,6},{6,7},{7,8},{8,9},{9,10},{10,1... | collective-permute-start | bytes 129032 | tf_op jit(solution)/shard_map/ppermute | solution.py:46
  79.5 3.3 %collective-permute-done.10 = f32[64,168]{1,0:T(8,128)S(1)} collective-permute-done((f32[64,168]{1,0:T(8,128)S(1)}, f32[64,168]{1,0:T(8,128)S(1)}, u32[]{:S(2)}, u32[]{:S(2)}) %collective-permute-start.10) | collective-permute-done | bytes 43040 | tf_op jit(solution)/shard_map/ppermute | solution.py:46
  83.9 5.2 %collective-permute-start.12 = (f32[640,256]{1,0:T(8,128)S(1)}, f32[640,256]{1,0:T(8,128)S(1)}, u32[]{:S(2)}, u32[]{:S(2)}) collective-permute-start(f32[640,256]{1,0:T(8,128)S(1)} %bitcast.16), channel_id=1, source_target_pairs={{0,1},{1,0},{2,3},{3,2},{4,5},{5,4},{6,7},{7,6},{8,9},{9,8},{10,11... | collective-permute-start | bytes 1966088 | tf_op jit(solution)/shard_map/ppermute | solution.py:258
  90.9 2.9 %later_pass.1 = (f32[640,256]{1,0:T(8,128)S(1)}, f32[640,256]{1,0:T(8,128)S(1)}, bf16[1280,768]{1,0:T(8,128)(2,1)S(1)}, bf16[1280,256]{1,0:T(8,128)(2,1)S(1)}) custom-call(s32[2]{0:T(128)S(1)} %pad_add_fusion.core_ref.place_ref, f32[64,768]{1,0:T(8,128)S(1)} %fusion.20.refs_0_, f32[64,768]{1,0:T(8,128)S(1)} %collective-permute-done.7.refs_1_, ...), custom_call_target="tpu_custom_call" | custom-call | flops 1006632960 | bytes 7995392 | tf_op jit(solution)/shard_map/later_pass/pallas_call | solution.py:161
  96.9 3.6 %all-to-all-start.2 = ((f32[16,40,256]{2,1,0:T(8,128)}), f32[16,40,256]{2,1,0:T(8,128)S(1)}, u32[]{:S(2)}, u32[]{:S(2)}) async-start(f32[16,40,256]{2,1,0:T(8,128)} %bitcast.7), calls=%async_computation.2 | async-start | bytes 1310720 | tf_op jit(solution)/shard_map/all_to_all | solution.py:29
  104.5 2.3 %collective-permute-done.14 = f32[64,768]{1,0:T(8,128)S(1)} collective-permute-done((f32[64,768]{1,0:T(8,128)S(1)}, f32[64,768]{1,0:T(8,128)S(1)}, u32[]{:S(2)}, u32[]{:S(2)}) %collective-permute-start.14) | collective-permute-done | bytes 196640 | tf_op jit(solution)/shard_map/ppermute | solution.py:40
  106.7 4.6 %collective-permute-done.16 = f32[64,768]{1,0:T(8,128)S(1)} collective-permute-done((f32[64,768]{1,0:T(8,128)S(1)}, f32[64,768]{1,0:T(8,128)S(1)}, u32[]{:S(2)}, u32[]{:S(2)}) %collective-permute-start.16) | collective-permute-done | bytes 196640 | tf_op jit(solution)/shard_map/ppermute | solution.py:40
  114.0 7.9 %collective-permute-done.17 = f32[64,768]{1,0:T(8,128)S(1)} collective-permute-done((f32[64,768]{1,0:T(8,128)S(1)}, f32[64,768]{1,0:T(8,128)S(1)}, u32[]{:S(2)}, u32[]{:S(2)}) %collective-permute-start.17) | collective-permute-done | bytes 196640 | tf_op jit(solution)/shard_map/ppermute | solution.py:246
  123.1 7.0 %all-to-all-start.3 = ((f32[16,40,256]{2,1,0:T(8,128)}), f32[16,40,256]{2,1,0:T(8,128)S(1)}, u32[]{:S(2)}, u32[]{:S(2)}) async-start(f32[16,40,256]{2,1,0:T(8,128)} %broadcast_in_dim.33), calls=%async_computation.3 | async-start | bytes 1310720 | tf_op jit(solution)/shard_map/all_to_all | solution.py:34
  130.2 3.2 %collective-permute-start.20 = (f32[64,768]{1,0:T(8,128)S(1)}, f32[64,768]{1,0:T(8,128)S(1)}, u32[]{:S(2)}, u32[]{:S(2)}) collective-permute-start(f32[64,768]{1,0:T(8,128)S(1)} %fusion.13.refs_0_), channel_id=1, source_target_pairs={{0,192},{64,128},{128,64},{192,0},{1,193},{65,129},{129,65},{193,1... | collective-permute-start | bytes 589832 | tf_op jit(solution)/shard_map/ppermute | solution.py:40
  134.2 7.4 %collective-permute-done.20.refs_3_ = f32[64,768]{1,0:T(8,128)S(1)} collective-permute-done((f32[64,768]{1,0:T(8,128)S(1)}, f32[64,768]{1,0:T(8,128)S(1)}, u32[]{:S(2)}, u32[]{:S(2)}) %collective-permute-start.20) | collective-permute-done | bytes 196640 | tf_op jit(solution)/shard_map/ppermute | solution.py:40
  141.7 8.1 %all-to-all-done.3 = f32[16,40,256]{2,1,0:T(8,128)S(1)} async-done(((f32[16,40,256]{2,1,0:T(8,128)}), f32[16,40,256]{2,1,0:T(8,128)S(1)}, u32[]{:S(2)}, u32[]{:S(2)}) %all-to-all-start.3) | async-done | bytes 655392 | tf_op jit(solution)/shard_map/all_to_all | solution.py:34
  149.8 2.7 %collective-permute-start.21 = (f32[640,256]{1,0:T(8,128)S(1)}, f32[640,256]{1,0:T(8,128)S(1)}, u32[]{:S(2)}, u32[]{:S(2)}) collective-permute-start(f32[640,256]{1,0:T(8,128)S(1)} %bitcast.18), channel_id=1, source_target_pairs={{0,1},{1,0},{2,3},{3,2},{4,5},{5,4},{6,7},{7,6},{8,9},{9,8},{10,11... | collective-permute-start | bytes 1966088 | tf_op jit(solution)/shard_map/ppermute | solution.py:258
  154.2 3.4 %last_pass.1 = (f32[1280,256]{1,0:T(8,128)}, f32[256,768]{1,0:T(8,128)}, bf16[1280,768]{1,0:T(8,128)(2,1)}) custom-call(s32[2]{0:T(128)S(1)} %pad_add_fusion.core_ref.place_ref, f32[64,768]{1,0:T(8,128)S(1)} %fusion.13.refs_0_, f32[64,768]{1,0:T(8,128)S(1)} %collective-permute-done.18.refs_1_, f32[64,768]{1,0:T(8,128)S(1)} %collective-permute-done.19.refs_2_, ...), custom_call_target="tpu_custom_call" | custom-call | flops 1006632960 | bytes 6160384 | tf_op jit(solution)/shard_map/last_pass/pallas_call | solution.py:161
  (76 shorter events, 41.0 us)
Async XLA Ops:
  12.0 8.1 %collective-permute-start = (f32[640,256]{1,0:T(8,128)}, f32[640,256]{1,0:T(8,128)}, u32[]{:S(2)}, u32[]{:S(2)}) collective-permute-start(f32[640,256]{1,0:T(8,128)} %get-tuple-element.35), channel_id=1, source_target_pairs={{0,1},{1,0},{2,3},{3,2},{4,5},{5,4},{6,7},{7,6},{8,9},{9,8},{10,11... | collective-permute-start | bytes 1966088 | tf_op jit(solution)/shard_map/ppermute | solution.py:234
  22.1 31.9 %all-to-all-start = ((f32[16,40,256]{2,1,0:T(8,128)}), f32[16,40,256]{2,1,0:T(8,128)S(1)}, u32[]{:S(2)}, u32[]{:S(2)}) async-start(f32[16,40,256]{2,1,0:T(8,128)} %bitcast.2), calls=%async_computation | async-start | bytes 1310720 | tf_op jit(solution)/shard_map/all_to_all | solution.py:29
  33.3 13.4 %collective-permute-start.1 = (f32[64,768]{1,0:T(8,128)}, f32[64,768]{1,0:T(8,128)S(1)}, u32[]{:S(2)}, u32[]{:S(2)}) collective-permute-start(f32[64,768]{1,0:T(8,128)} %get-tuple-element.68), channel_id=1, source_target_pairs={{0,64},{64,0},{128,192},{192,128},{1,65},{65,1},{129,193},{193,129... | collective-permute-start | bytes 589832 | tf_op jit(solution)/shard_map/ppermute | solution.py:40
  34.6 12.2 %collective-permute-start.3 = (f32[64,768]{1,0:T(8,128)}, f32[64,768]{1,0:T(8,128)}, u32[]{:S(2)}, u32[]{:S(2)}) collective-permute-start(f32[64,768]{1,0:T(8,128)} %get-tuple-element.69), channel_id=1, source_target_pairs={{0,192},{64,128},{128,64},{192,0},{1,193},{65,129},{129,65},{193,1... | collective-permute-start | bytes 589832 | tf_op jit(solution)/shard_map/ppermute | solution.py:40
  36.4 10.4 %collective-permute-start.2 = (f32[64,768]{1,0:T(8,128)}, f32[64,768]{1,0:T(8,128)}, u32[]{:S(2)}, u32[]{:S(2)}) collective-permute-start(f32[64,768]{1,0:T(8,128)} %get-tuple-element.70), channel_id=1, source_target_pairs={{0,128},{64,192},{128,0},{192,64},{1,129},{65,193},{129,1},{193,65... | collective-permute-start | bytes 589832 | tf_op jit(solution)/shard_map/ppermute | solution.py:40
  37.1 9.5 %collective-permute-start.5 = (f32[64,168]{1,0:T(8,128)S(1)}, f32[64,168]{1,0:T(8,128)S(1)}, u32[]{:S(2)}, u32[]{:S(2)}) collective-permute-start(f32[64,168]{1,0:T(8,128)S(1)} %get-tuple-element.73), channel_id=1, source_target_pairs={{1,0},{2,1},{3,2},{4,3},{5,4},{6,5},{7,6},{8,7},{9,8},{10,9},{11,1... | collective-permute-start | bytes 129032 | tf_op jit(solution)/shard_map/ppermute | solution.py:46
  39.8 6.7 %collective-permute-start.6 = (f32[64,168]{1,0:T(8,128)S(1)}, f32[64,168]{1,0:T(8,128)S(1)}, u32[]{:S(2)}, u32[]{:S(2)}) collective-permute-start(f32[64,168]{1,0:T(8,128)S(1)} %get-tuple-element.74), channel_id=1, source_target_pairs={{0,1},{1,2},{2,3},{3,4},{4,5},{5,6},{6,7},{7,8},{8,9},{9,10},{10,1... | collective-permute-start | bytes 129032 | tf_op jit(solution)/shard_map/ppermute | solution.py:46
  48.0 5.8 %collective-permute-start.4 = (f32[64,768]{1,0:T(8,128)S(1)}, f32[64,768]{1,0:T(8,128)S(1)}, u32[]{:S(2)}, u32[]{:S(2)}) collective-permute-start(f32[64,768]{1,0:T(8,128)S(1)} %add_add_fusion.1), channel_id=1, source_target_pairs={{0,32},{32,0},{1,33},{33,1},{2,34},{34,2},{3,35},{35,3},{4,36},{36... | collective-permute-start | bytes 589832 | tf_op jit(solution)/shard_map/ppermute | solution.py:246
  55.8 28.1 %all-to-all-start.1 = ((f32[16,40,256]{2,1,0:T(8,128)}), f32[16,40,256]{2,1,0:T(8,128)S(1)}, u32[]{:S(2)}, u32[]{:S(2)}) async-start(f32[16,40,256]{2,1,0:T(8,128)} %broadcast_in_dim.32), calls=%async_computation.1 | async-start | bytes 1310720 | tf_op jit(solution)/shard_map/all_to_all | solution.py:34
  65.3 17.5 %collective-permute-start.9 = (f32[64,768]{1,0:T(8,128)S(1)}, f32[64,768]{1,0:T(8,128)S(1)}, u32[]{:S(2)}, u32[]{:S(2)}) collective-permute-start(f32[64,768]{1,0:T(8,128)S(1)} %fusion.20.refs_0_), channel_id=1, source_target_pairs={{0,192},{64,128},{128,64},{192,0},{1,193},{65,129},{129,65},{193,1... | collective-permute-start | bytes 589832 | tf_op jit(solution)/shard_map/ppermute | solution.py:40
  67.9 14.9 %collective-permute-start.8 = (f32[64,768]{1,0:T(8,128)S(1)}, f32[64,768]{1,0:T(8,128)S(1)}, u32[]{:S(2)}, u32[]{:S(2)}) collective-permute-start(f32[64,768]{1,0:T(8,128)S(1)} %fusion.20.refs_0_), channel_id=1, source_target_pairs={{0,128},{64,192},{128,0},{192,64},{1,129},{65,193},{129,1},{193,65... | collective-permute-start | bytes 589832 | tf_op jit(solution)/shard_map/ppermute | solution.py:40
  68.4 15.1 %collective-permute-start.7 = (f32[64,768]{1,0:T(8,128)S(1)}, f32[64,768]{1,0:T(8,128)S(1)}, u32[]{:S(2)}, u32[]{:S(2)}) collective-permute-start(f32[64,768]{1,0:T(8,128)S(1)} %fusion.20.refs_0_), channel_id=1, source_target_pairs={{0,64},{64,0},{128,192},{192,128},{1,65},{65,1},{129,193},{193,129... | collective-permute-start | bytes 589832 | tf_op jit(solution)/shard_map/ppermute | solution.py:40
  68.7 10.8 %collective-permute-start.11 = (f32[64,168]{1,0:T(8,128)S(1)}, f32[64,168]{1,0:T(8,128)S(1)}, u32[]{:S(2)}, u32[]{:S(2)}) collective-permute-start(f32[64,168]{1,0:T(8,128)S(1)} %get-tuple-element.71), channel_id=1, source_target_pairs={{1,0},{2,1},{3,2},{4,3},{5,4},{6,5},{7,6},{8,7},{9,8},{10,9},{11,1... | collective-permute-start | bytes 129032 | tf_op jit(solution)/shard_map/ppermute | solution.py:46
  73.8 9.0 %collective-permute-start.10 = (f32[64,168]{1,0:T(8,128)S(1)}, f32[64,168]{1,0:T(8,128)S(1)}, u32[]{:S(2)}, u32[]{:S(2)}) collective-permute-start(f32[64,168]{1,0:T(8,128)S(1)} %get-tuple-element.72), channel_id=1, source_target_pairs={{0,1},{1,2},{2,3},{3,4},{4,5},{5,6},{6,7},{7,8},{8,9},{9,10},{10,1... | collective-permute-start | bytes 129032 | tf_op jit(solution)/shard_map/ppermute | solution.py:46
  83.9 7.0 %collective-permute-start.12 = (f32[640,256]{1,0:T(8,128)S(1)}, f32[640,256]{1,0:T(8,128)S(1)}, u32[]{:S(2)}, u32[]{:S(2)}) collective-permute-start(f32[640,256]{1,0:T(8,128)S(1)} %bitcast.16), channel_id=1, source_target_pairs={{0,1},{1,0},{2,3},{3,2},{4,5},{5,4},{6,7},{7,6},{8,9},{9,8},{10,11... | collective-permute-start | bytes 1966088 | tf_op jit(solution)/shard_map/ppermute | solution.py:258
  96.9 25.3 %all-to-all-start.2 = ((f32[16,40,256]{2,1,0:T(8,128)}), f32[16,40,256]{2,1,0:T(8,128)S(1)}, u32[]{:S(2)}, u32[]{:S(2)}) async-start(f32[16,40,256]{2,1,0:T(8,128)} %bitcast.7), calls=%async_computation.2 | async-start | bytes 1310720 | tf_op jit(solution)/shard_map/all_to_all | solution.py:29
  100.5 6.2 %collective-permute-start.14 = (f32[64,768]{1,0:T(8,128)S(1)}, f32[64,768]{1,0:T(8,128)S(1)}, u32[]{:S(2)}, u32[]{:S(2)}) collective-permute-start(f32[64,768]{1,0:T(8,128)S(1)} %get-tuple-element.65), channel_id=1, source_target_pairs={{0,64},{64,0},{128,192},{192,128},{1,65},{65,1},{129,193},{193,129... | collective-permute-start | bytes 589832 | tf_op jit(solution)/shard_map/ppermute | solution.py:40
  101.8 9.5 %collective-permute-start.16 = (f32[64,768]{1,0:T(8,128)S(1)}, f32[64,768]{1,0:T(8,128)S(1)}, u32[]{:S(2)}, u32[]{:S(2)}) collective-permute-start(f32[64,768]{1,0:T(8,128)S(1)} %get-tuple-element.66), channel_id=1, source_target_pairs={{0,192},{64,128},{128,64},{192,0},{1,193},{65,129},{129,65},{193,1... | collective-permute-start | bytes 589832 | tf_op jit(solution)/shard_map/ppermute | solution.py:40
  103.6 9.6 %collective-permute-start.15 = (f32[64,768]{1,0:T(8,128)S(1)}, f32[64,768]{1,0:T(8,128)S(1)}, u32[]{:S(2)}, u32[]{:S(2)}) collective-permute-start(f32[64,768]{1,0:T(8,128)S(1)} %get-tuple-element.67), channel_id=1, source_target_pairs={{0,128},{64,192},{128,0},{192,64},{1,129},{65,193},{129,1},{193,65... | collective-permute-start | bytes 589832 | tf_op jit(solution)/shard_map/ppermute | solution.py:40
  113.2 8.6 %collective-permute-start.17 = (f32[64,768]{1,0:T(8,128)S(1)}, f32[64,768]{1,0:T(8,128)S(1)}, u32[]{:S(2)}, u32[]{:S(2)}) collective-permute-start(f32[64,768]{1,0:T(8,128)S(1)} %add_add_fusion), channel_id=1, source_target_pairs={{0,32},{32,0},{1,33},{33,1},{2,34},{34,2},{3,35},{35,3},{4,36},{36... | collective-permute-start | bytes 589832 | tf_op jit(solution)/shard_map/ppermute | solution.py:246
  123.1 26.7 %all-to-all-start.3 = ((f32[16,40,256]{2,1,0:T(8,128)}), f32[16,40,256]{2,1,0:T(8,128)S(1)}, u32[]{:S(2)}, u32[]{:S(2)}) async-start(f32[16,40,256]{2,1,0:T(8,128)} %broadcast_in_dim.33), calls=%async_computation.3 | async-start | bytes 1310720 | tf_op jit(solution)/shard_map/all_to_all | solution.py:34
  130.2 11.4 %collective-permute-start.20 = (f32[64,768]{1,0:T(8,128)S(1)}, f32[64,768]{1,0:T(8,128)S(1)}, u32[]{:S(2)}, u32[]{:S(2)}) collective-permute-start(f32[64,768]{1,0:T(8,128)S(1)} %fusion.13.refs_0_), channel_id=1, source_target_pairs={{0,192},{64,128},{128,64},{192,0},{1,193},{65,129},{129,65},{193,1... | collective-permute-start | bytes 589832 | tf_op jit(solution)/shard_map/ppermute | solution.py:40
  133.3 8.2 %collective-permute-start.19 = (f32[64,768]{1,0:T(8,128)S(1)}, f32[64,768]{1,0:T(8,128)S(1)}, u32[]{:S(2)}, u32[]{:S(2)}) collective-permute-start(f32[64,768]{1,0:T(8,128)S(1)} %fusion.13.refs_0_), channel_id=1, source_target_pairs={{0,128},{64,192},{128,0},{192,64},{1,129},{65,193},{129,1},{193,65... | collective-permute-start | bytes 589832 | tf_op jit(solution)/shard_map/ppermute | solution.py:40
  134.2 7.5 %collective-permute-start.18 = (f32[64,768]{1,0:T(8,128)S(1)}, f32[64,768]{1,0:T(8,128)S(1)}, u32[]{:S(2)}, u32[]{:S(2)}) collective-permute-start(f32[64,768]{1,0:T(8,128)S(1)} %fusion.13.refs_0_), channel_id=1, source_target_pairs={{0,64},{64,0},{128,192},{192,128},{1,65},{65,1},{129,193},{193,129... | collective-permute-start | bytes 589832 | tf_op jit(solution)/shard_map/ppermute | solution.py:40
  (11 other events, 54.5 us)

commit v3 on v2

--- a/solution.py
+++ b/solution.py
@@ -18,9 +18,7 @@
 SWAP = ((0, 1), (1, 0))
 STEPS = 2
 HIDDEN = 1e30
-PARAMS = pltpu.CompilerParams(
-    vmem_limit_bytes=20 * 2**20, dimension_semantics=("arbitrary",)
-)
+MIB = 2**20
 BF16, F32 = jnp.bfloat16, jnp.float32
 
 
@@ -76,21 +74,42 @@
     return jnp.dot(a, b, preferred_element_type=F32)
 
 
-def gradient(misfit, x_low, theirs_ref, mine_ref):
-    grad = lax.dot_general(
+def gradients(misfit, f_low, x_low, along, theirs_ref, mine_ref, pieces, grad_x_ref):
+    i = pl.program_id(0)
+    grad_f = lax.dot_general(
         misfit, x_low, (((1,), (1,)), ((), ())), preferred_element_type=F32
     )
-
-    @pl.when(pl.program_id(0) < STEPS)
-    def _():
-        theirs_ref[...] = grad
-
-    @pl.when(pl.program_id(0) >= STEPS)
-    def _():
-        mine_ref[...] = grad
-
-
-def first_pass(core_ref, x_ref, f_ref, seen_ref, mask_ref, theirs_ref, mine_ref, misfit_ref, f_low_ref, kept_ref, x_low_ref):
+    grad_x = lax.dot_general(
+        f_low, misfit, (((0,), (0,)), ((), ())), preferred_element_type=F32
+    )
+
+    @pl.when(i < STEPS)
+    def _():
+        theirs_ref[...] = grad_f
+
+    @pl.when(i >= STEPS)
+    def _():
+        mine_ref[...] = grad_f
+
+    @pl.when(i == 0)
+    def _():
+        grad_x_ref[...] = grad_x
+
+    @pl.when(i > 0)
+    def _():
+        grad_x_ref[...] += grad_x
+
+    @pl.when(i == 2 * STEPS - 1)
+    def _():
+        for k, piece in enumerate(pieces):
+            size = piece.shape[0]
+            start = pl.multiple_of((along ^ k) * size, size)
+            piece[...] = grad_x_ref[pl.ds(start, size), :]
+
+
+def first_pass(place_ref, x_ref, f_ref, seen_ref, mask_ref, *refs):
+    theirs_ref, mine_ref, *pieces, kept_ref, x_low_ref, grad_x_ref = refs
+
     @pl.when(pl.program_id(0) == 0)
     def _():
         x_low_ref[...] = x_ref[...].astype(BF16)
@@ -101,9 +120,7 @@
     seen = seen_ref[...].astype(F32)
     misfit = jnp.where(keep, dot(f_low, x_low) - seen, 0.0).astype(BF16)
     kept_ref[...] = jnp.where(keep, seen, HIDDEN).astype(BF16)
-    f_low_ref[...] = f_low
-    misfit_ref[...] = misfit
-    gradient(misfit, x_low, theirs_ref, mine_ref)
+    gradients(misfit, f_low, x_low, place_ref[1], theirs_ref, mine_ref, pieces, grad_x_ref)
 
 
 def assembled(along, pieces, *outs):
@@ -115,20 +132,19 @@
 
 
 def later_pass(place_ref, *refs):
-    *pieces, f_theirs_ref, f_mine_ref, kept_ref = refs[:-5]
-    theirs_ref, mine_ref, misfit_ref, f_low_ref, x_low_ref = refs[-5:]
+    count = (len(refs) - 7) // 2
+    came, (f_theirs_ref, f_mine_ref, kept_ref) = refs[:count], refs[count : count + 3]
+    theirs_ref, mine_ref, *pieces, x_low_ref, grad_x_ref = refs[count + 3 :]
 
     @pl.when(pl.program_id(0) == 0)
     def _():
-        assembled(place_ref[1], pieces, x_low_ref)
+        assembled(place_ref[1], came, x_low_ref)
 
     x_low = x_low_ref[...]
     f_low = jnp.where(pl.program_id(0) < STEPS, f_theirs_ref[...], f_mine_ref[...]).astype(BF16)
     kept = kept_ref[...].astype(F32)
     misfit = jnp.where(kept < HIDDEN / 2, dot(f_low, x_low) - kept, 0.0).astype(BF16)
-    f_low_ref[...] = f_low
-    misfit_ref[...] = misfit
-    gradient(misfit, x_low, theirs_ref, mine_ref)
+    gradients(misfit, f_low, x_low, place_ref[1], theirs_ref, mine_ref, pieces, grad_x_ref)
 
 
 def last_pass(place_ref, *refs):
@@ -144,7 +160,7 @@
     imputed_ref[...] = dot(f_now.astype(BF16), x_low_ref[...]).astype(BF16)
 
 
-def row_pass(kernel, place, ins, outs, rank, hours, name):
+def row_pass(kernel, place, ins, outs, rank, hours, name, limit, scratch=()):
     def spec(kind, shape):
         maps = {
             "whole": lambda i, p: (0, 0),
@@ -166,9 +182,9 @@
             grid=(2 * STEPS,),
             in_specs=[spec(k, a.shape) for k, a in ins],
             out_specs=[spec(k, s.shape) for k, s in outs],
-            scratch_shapes=[pltpu.VMEM((rank, hours), BF16)],
+            scratch_shapes=[pltpu.VMEM((rank, hours), BF16), *scratch],
         ),
-        compiler_params=PARAMS,
+        compiler_params=pltpu.CompilerParams(vmem_limit_bytes=limit * MIB),
         cost_estimate=pl.CostEstimate(
             flops=4 * rows * rank * hours, bytes_accessed=moved, transcendentals=0
         ),
@@ -204,15 +220,15 @@
     grads = [
         ("theirs", shape(half, rank)),
         ("mine", shape(half, rank)),
-        ("step", shape(rows, hours, BF16)),
-        ("step", shape(rows, rank, BF16)),
+        *[("whole", shape(band, hours))] * peers,
     ]
+    total = [pltpu.VMEM((rank, hours), F32)]
     f_part = lax.dynamic_slice_in_dim(series_factors, own_row, line, 0)
     x_part = lax.dynamic_slice_in_dim(time_factors, along * band, band, 0)
     w_part = lax.dynamic_slice_in_dim(ar_weights, along * band, band, 1)
     for sweep in range(ITERS):
         if sweep == 0:
-            theirs, mine, misfit, f_low, kept = row_pass(
+            theirs, mine, *parts, kept = row_pass(
                 first_pass,
                 place,
                 [("whole", time_factors), ("natural", series_factors), ("natural", observed), ("natural", mask)],
@@ -220,9 +236,11 @@
                 rank,
                 hours,
                 "first_pass",
+                58,
+                total,
             )
         else:
-            theirs, mine, misfit, f_low = row_pass(
+            theirs, mine, *parts = row_pass(
                 later_pass,
                 place,
                 [*[("whole", p) for p in pieces], ("theirs", f_theirs), ("mine", f_mine), ("step", kept)],
@@ -230,19 +248,17 @@
                 rank,
                 hours,
                 "later_pass",
+                20,
+                total,
             )
         mine = mine + lax.ppermute(theirs, CORE, SWAP)
-        grad_x = lax.dot_general(
-            f_low, misfit, (((0,), (0,)), ((), ())), preferred_element_type=F32
-        )
-        mine, grad_x, x_part = lax.optimization_barrier((mine, grad_x, x_part))
+        mine, parts, x_part = lax.optimization_barrier((mine, parts, x_part))
         if sweep == 0:
             edges = edges_of(x_part)
         f_sum = scattered_sum(mine, FAR)
-        x_sum = lax.dynamic_slice_in_dim(grad_x, along * band, band, 0)
+        x_sum = parts[0]
         for k in range(1, peers):
-            part = lax.dynamic_slice_in_dim(grad_x, (along ^ k) * band, band, 0)
-            x_sum = x_sum + traded(part, "x", k)
+            x_sum = x_sum + traded(parts[k], "x", k)
         x_sum = x_sum + lax.ppermute(x_sum, "y_lo", SWAP)
         lag = lag_terms(x_part, edges, w_part, first, last)
         f_part = f_part - step_f * (f_sum + ridge_f * f_part)
@@ -264,6 +280,7 @@
         rank,
         hours,
         "last_pass",
+        20,
     )
 
 

time: 159 us -> 154 us (0.969)
  local copies, waits for them, and re-layouts: 14 us -> 3.93 us
  Pallas kernels: 10.1 us -> 15.4 us
  matrix products: 3.84 us -> 0 us
  starting transfers between devices: 74.3 us -> 76.8 us
  waiting for transfers between devices: 48.1 us -> 50.6 us
    unnamed x18 -> x28, local copies, waits for them, and re-layouts: 8.02 us -> 0.67 us
    pallas_call x3, Pallas kernels: 10.1 us -> 15.4 us  [row_pass(): pl.pallas_call(kernel, out_shape=[s for _, s in outs], grid_spec=pltpu.Pr...]
    dot_general x2 -> x0, matrix products: 3.84 us -> none  [local(): lax.dot_general(f_low, misfit, (((0,), (0,)), ((), ())), preferred_elemen...]
    ppermute x2, waiting for transfers between devices: 12.9 us -> 10.9 us  [local(): x_sum = x_sum + lax.ppermute(x_sum, 'y_lo', SWAP)]
    dynamic_slice x2 -> x0, local copies, waits for them, and re-layouts: 2 us -> none  [local(): part = lax.dynamic_slice_in_dim(grad_x, (along ^ k) * band, band, 0)]
    ppermute x2, waiting for transfers between devices: 1.02 us -> 2.64 us  [local(): mine = mine + lax.ppermute(theirs, CORE, SWAP)]
  transfers between devices with their start and end apart: 26 -> 26, of which waited for: 15 -> 17; matrix products, arithmetic and copies ran while one was open for 7% -> 2% of each run, Pallas kernels for 0% -> 0%
where the time goes in v3:
time: 154 us; the launch traced here: 153 us
  starting transfers between devices  76.8 us (50%)
  waiting for transfers between devices  50.6 us (33%)
  Pallas kernels  15.4 us (10%)
  other arithmetic  5.66 us (4%)
  local copies, waits for them, and re-layouts  3.93 us (3%)
    ppermute x4, starting transfers between devices, passed_along(): return lax.ppermute(array, axis, pairs)  18.2 us
    ppermute x12, waiting for transfers between devices, traded(): return lax.ppermute(array, axis, [(i, i ^ bits) for i in range(length)])  17.5 us
    all_to_all x2, starting transfers between devices, gathered(): parts = lax.all_to_all(parts, axis, 0, 0, tiled=True)  17.4 us
    pallas_call x3, Pallas kernels, row_pass(): pl.pallas_call(kernel, out_shape=[s for _, s in outs], grid_spec=pltpu.Pr...  15.4 us
    ppermute x12, starting transfers between devices, traded(): return lax.ppermute(array, axis, [(i, i ^ bits) for i in range(length)])  14.6 us
    all_to_all x2, starting transfers between devices, scattered_sum(): return lax.all_to_all(parts, axis, 0, 0, tiled=True).sum(axis=0)  12.9 us
    ppermute x2, waiting for transfers between devices, local(): x_sum = x_sum + lax.ppermute(x_sum, 'y_lo', SWAP)  10.9 us
    all_to_all x2, waiting for transfers between devices, gathered(): parts = lax.all_to_all(parts, axis, 0, 0, tiled=True)  9.49 us
  transfers between devices with their start and end apart: 26, of which 17 were waited for; matrix products, arithmetic and copies ran while one was open for 2% of the time, Pallas kernels for 0%

profile of v3, /device:TPU:1, one launch (start us, length us, event | category | flops | bytes accessed | tf_op | source)
XLA Modules:
  0.0 153.3 jit_solution(12434704654980375695)
XLA Ops:
  1.3 8.2 %first_pass.1 = (f32[640,256]{1,0:T(8,128)}, f32[640,256]{1,0:T(8,128)}, f32[64,768]{1,0:T(8,128)}, f32[64,768]{1,0:T(8,128)}, f32[64,768]{1,0:T(8,128)}, /*index=5*/f32[64,768]{1,0:T(8,128)}, bf16[1280,768]{1,0:T(8,128)(2,1)}) custom-call(s32[2]{0:T(128)} %pad_add_fusion.place_ref, f32[256,768]{1,0:T(8,128)} %x_ref.1, f32[1280,256]{1,0:T(8,128)} %f_ref.1, ...), custom_call_target="tpu_custom_call" | custom-call | flops 1006632960 | bytes 12058624 | tf_op jit(solution)/shard_map/first_pass/pallas_call | solution.py:177
  9.5 3.3 %collective-permute-start = (f32[640,256]{1,0:T(8,128)}, f32[640,256]{1,0:T(8,128)S(1)}, u32[]{:S(2)}, u32[]{:S(2)}) collective-permute-start(f32[640,256]{1,0:T(8,128)} %get-tuple-element.45), channel_id=1, source_target_pairs={{0,1},{1,0},{2,3},{3,2},{4,5},{5,4},{6,7},{7,6},{8,9},{9,8},{10,11... | collective-permute-start | bytes 1966088 | tf_op jit(solution)/shard_map/ppermute | solution.py:254
  16.8 9.2 %all-to-all-start = ((f32[16,40,256]{2,1,0:T(8,128)}), f32[16,40,256]{2,1,0:T(8,128)S(1)}, u32[]{:S(2)}, u32[]{:S(2)}) async-start(f32[16,40,256]{2,1,0:T(8,128)} %bitcast.2), calls=%async_computation | async-start | bytes 1310720 | tf_op jit(solution)/shard_map/all_to_all | solution.py:27
  27.3 2.5 %collective-permute-start.2 = (f32[64,768]{1,0:T(8,128)S(1)}, f32[64,768]{1,0:T(8,128)S(1)}, u32[]{:S(2)}, u32[]{:S(2)}) collective-permute-start(f32[64,768]{1,0:T(8,128)S(1)} %copy-done.12), channel_id=1, source_target_pairs={{0,128},{64,192},{128,0},{192,64},{1,129},{65,193},{129,1},{193,65... | collective-permute-start | bytes 589832 | tf_op jit(solution)/shard_map/ppermute | solution.py:38
  30.0 3.4 %collective-permute-start.5 = (f32[64,168]{1,0:T(8,128)S(1)}, f32[64,168]{1,0:T(8,128)S(1)}, u32[]{:S(2)}, u32[]{:S(2)}) collective-permute-start(f32[64,168]{1,0:T(8,128)S(1)} %get-tuple-element.87), channel_id=1, source_target_pairs={{1,0},{2,1},{3,2},{4,3},{5,4},{6,5},{7,6},{8,7},{9,8},{10,9},{11,1... | collective-permute-start | bytes 129032 | tf_op jit(solution)/shard_map/ppermute | solution.py:44
  33.4 5.0 %collective-permute-start.6 = (f32[64,168]{1,0:T(8,128)S(1)}, f32[64,168]{1,0:T(8,128)S(1)}, u32[]{:S(2)}, u32[]{:S(2)}) collective-permute-start(f32[64,168]{1,0:T(8,128)S(1)} %get-tuple-element.88), channel_id=1, source_target_pairs={{0,1},{1,2},{2,3},{3,4},{4,5},{5,6},{6,7},{7,8},{8,9},{9,10},{10,1... | collective-permute-start | bytes 129032 | tf_op jit(solution)/shard_map/ppermute | solution.py:44
  41.8 6.2 %collective-permute-done.4 = f32[64,768]{1,0:T(8,128)S(1)} collective-permute-done((f32[64,768]{1,0:T(8,128)S(1)}, f32[64,768]{1,0:T(8,128)S(1)}, u32[]{:S(2)}, u32[]{:S(2)}) %collective-permute-start.4) | collective-permute-done | bytes 196640 | tf_op jit(solution)/shard_map/ppermute | solution.py:262
  50.0 8.9 %all-to-all-start.1 = ((f32[16,40,256]{2,1,0:T(8,128)}), f32[16,40,256]{2,1,0:T(8,128)S(1)}, u32[]{:S(2)}, u32[]{:S(2)}) async-start(f32[16,40,256]{2,1,0:T(8,128)} %broadcast_in_dim.32), calls=%async_computation.1 | async-start | bytes 1310720 | tf_op jit(solution)/shard_map/all_to_all | solution.py:32
  59.0 2.6 %collective-permute-start.9 = (f32[64,768]{1,0:T(8,128)S(1)}, f32[64,768]{1,0:T(8,128)S(1)}, u32[]{:S(2)}, u32[]{:S(2)}) collective-permute-start(f32[64,768]{1,0:T(8,128)S(1)} %fusion.20.refs_0_), channel_id=1, source_target_pairs={{0,192},{64,128},{128,64},{192,0},{1,193},{65,129},{129,65},{193,1... | collective-permute-start | bytes 589832 | tf_op jit(solution)/shard_map/ppermute | solution.py:38
  62.4 4.9 %collective-permute-start.11 = (f32[64,168]{1,0:T(8,128)S(1)}, f32[64,168]{1,0:T(8,128)S(1)}, u32[]{:S(2)}, u32[]{:S(2)}) collective-permute-start(f32[64,168]{1,0:T(8,128)S(1)} %get-tuple-element.85), channel_id=1, source_target_pairs={{1,0},{2,1},{3,2},{4,3},{5,4},{6,5},{7,6},{8,7},{9,8},{10,9},{11,1... | collective-permute-start | bytes 129032 | tf_op jit(solution)/shard_map/ppermute | solution.py:44
  67.3 4.9 %collective-permute-start.10 = (f32[64,168]{1,0:T(8,128)S(1)}, f32[64,168]{1,0:T(8,128)S(1)}, u32[]{:S(2)}, u32[]{:S(2)}) collective-permute-start(f32[64,168]{1,0:T(8,128)S(1)} %get-tuple-element.86), channel_id=1, source_target_pairs={{0,1},{1,2},{2,3},{3,4},{4,5},{5,6},{6,7},{7,8},{8,9},{9,10},{10,1... | collective-permute-start | bytes 129032 | tf_op jit(solution)/shard_map/ppermute | solution.py:44
  73.1 3.4 %collective-permute-done.10 = f32[64,168]{1,0:T(8,128)S(1)} collective-permute-done((f32[64,168]{1,0:T(8,128)S(1)}, f32[64,168]{1,0:T(8,128)S(1)}, u32[]{:S(2)}, u32[]{:S(2)}) %collective-permute-start.10) | collective-permute-done | bytes 43040 | tf_op jit(solution)/shard_map/ppermute | solution.py:44
  77.6 5.2 %collective-permute-start.12 = (f32[640,256]{1,0:T(8,128)S(1)}, f32[640,256]{1,0:T(8,128)S(1)}, u32[]{:S(2)}, u32[]{:S(2)}) collective-permute-start(f32[640,256]{1,0:T(8,128)S(1)} %bitcast.12), channel_id=1, source_target_pairs={{0,1},{1,0},{2,3},{3,2},{4,5},{5,4},{6,7},{7,6},{8,9},{9,8},{10,11... | collective-permute-start | bytes 1966088 | tf_op jit(solution)/shard_map/ppermute | solution.py:274
  84.5 3.8 %later_pass.1 = (f32[640,256]{1,0:T(8,128)S(1)}, f32[640,256]{1,0:T(8,128)S(1)}, f32[64,768]{1,0:T(8,128)S(1)}, f32[64,768]{1,0:T(8,128)S(1)}, f32[64,768]{1,0:T(8,128)S(1)}, /*index=5*/f32[64,768]{1,0:T(8,128)S(1)}) custom-call(s32[2]{0:T(128)S(1)} %copy-done.4, f32[64,768]{1,0:T(8,128)S(1)} %fusion.20.refs_0_, ...), custom_call_target="tpu_custom_call" | custom-call | flops 503316480 | bytes 6160384 | tf_op jit(solution)/shard_map/later_pass/pallas_call | solution.py:177
  91.5 3.7 %all-to-all-start.2 = ((f32[16,40,256]{2,1,0:T(8,128)}), f32[16,40,256]{2,1,0:T(8,128)S(1)}, u32[]{:S(2)}, u32[]{:S(2)}) async-start(f32[16,40,256]{2,1,0:T(8,128)} %bitcast.7), calls=%async_computation.2 | async-start | bytes 1310720 | tf_op jit(solution)/shard_map/all_to_all | solution.py:27
  96.6 2.5 %collective-permute-start.15 = (f32[64,768]{1,0:T(8,128)}, f32[64,768]{1,0:T(8,128)S(1)}, u32[]{:S(2)}, u32[]{:S(2)}) collective-permute-start(f32[64,768]{1,0:T(8,128)} %copy-done.6), channel_id=1, source_target_pairs={{0,128},{64,192},{128,0},{192,64},{1,129},{65,193},{129,1},{193,65... | collective-permute-start | bytes 589832 | tf_op jit(solution)/shard_map/ppermute | solution.py:38
  101.7 6.5 %collective-permute-done.15 = f32[64,768]{1,0:T(8,128)S(1)} collective-permute-done((f32[64,768]{1,0:T(8,128)}, f32[64,768]{1,0:T(8,128)S(1)}, u32[]{:S(2)}, u32[]{:S(2)}) %collective-permute-start.15) | collective-permute-done | bytes 196640 | tf_op jit(solution)/shard_map/ppermute | solution.py:38
  108.2 2.3 %collective-permute-done.16 = f32[64,768]{1,0:T(8,128)S(1)} collective-permute-done((f32[64,768]{1,0:T(8,128)}, f32[64,768]{1,0:T(8,128)S(1)}, u32[]{:S(2)}, u32[]{:S(2)}) %collective-permute-start.16) | collective-permute-done | bytes 196640 | tf_op jit(solution)/shard_map/ppermute | solution.py:38
  111.5 4.7 %collective-permute-done.17 = f32[64,768]{1,0:T(8,128)S(1)} collective-permute-done((f32[64,768]{1,0:T(8,128)S(1)}, f32[64,768]{1,0:T(8,128)S(1)}, u32[]{:S(2)}, u32[]{:S(2)}) %collective-permute-start.17) | collective-permute-done | bytes 196640 | tf_op jit(solution)/shard_map/ppermute | solution.py:262
  117.4 8.4 %all-to-all-start.3 = ((f32[16,40,256]{2,1,0:T(8,128)}), f32[16,40,256]{2,1,0:T(8,128)S(1)}, u32[]{:S(2)}, u32[]{:S(2)}) async-start(f32[16,40,256]{2,1,0:T(8,128)} %broadcast_in_dim.33), calls=%async_computation.3 | async-start | bytes 1310720 | tf_op jit(solution)/shard_map/all_to_all | solution.py:32
  129.2 4.9 %collective-permute-done.20.refs_3_ = f32[64,768]{1,0:T(8,128)S(1)} collective-permute-done((f32[64,768]{1,0:T(8,128)S(1)}, f32[64,768]{1,0:T(8,128)S(1)}, u32[]{:S(2)}, u32[]{:S(2)}) %collective-permute-start.20) | collective-permute-done | bytes 196640 | tf_op jit(solution)/shard_map/ppermute | solution.py:38
  135.5 9.1 %all-to-all-done.3 = f32[16,40,256]{2,1,0:T(8,128)S(1)} async-done(((f32[16,40,256]{2,1,0:T(8,128)}), f32[16,40,256]{2,1,0:T(8,128)S(1)}, u32[]{:S(2)}, u32[]{:S(2)}) %all-to-all-start.3) | async-done | bytes 655392 | tf_op jit(solution)/shard_map/all_to_all | solution.py:32
  144.6 3.6 %collective-permute-start.21 = (f32[640,256]{1,0:T(8,128)S(1)}, f32[640,256]{1,0:T(8,128)S(1)}, u32[]{:S(2)}, u32[]{:S(2)}) collective-permute-start(f32[640,256]{1,0:T(8,128)S(1)} %bitcast.14), channel_id=1, source_target_pairs={{0,1},{1,0},{2,3},{3,2},{4,5},{5,4},{6,7},{7,6},{8,9},{9,8},{10,11... | collective-permute-start | bytes 1966088 | tf_op jit(solution)/shard_map/ppermute | solution.py:274
  149.9 3.4 %last_pass.1 = (f32[1280,256]{1,0:T(8,128)}, f32[256,768]{1,0:T(8,128)}, bf16[1280,768]{1,0:T(8,128)(2,1)}) custom-call(s32[2]{0:T(128)S(1)} %copy-done.4, f32[64,768]{1,0:T(8,128)S(1)} %fusion.13.refs_0_, f32[64,768]{1,0:T(8,128)S(1)} %collective-permute-done.18.refs_1_, f32[64,768]{1,0:T(8,128)S(1)} %collective-permute-done.19.refs_2_, ...), custom_call_target="tpu_custom_call" | custom-call | flops 1006632960 | bytes 6160384 | tf_op jit(solution)/shard_map/last_pass/pallas_call | solution.py:177
  (82 shorter events, 31.9 us)
Async XLA Ops:
  16.8 31.5 %all-to-all-start = ((f32[16,40,256]{2,1,0:T(8,128)}), f32[16,40,256]{2,1,0:T(8,128)S(1)}, u32[]{:S(2)}, u32[]{:S(2)}) async-start(f32[16,40,256]{2,1,0:T(8,128)} %bitcast.2), calls=%async_computation | async-start | bytes 1310720 | tf_op jit(solution)/shard_map/all_to_all | solution.py:27
  26.0 15.0 %collective-permute-start.1 = (f32[64,768]{1,0:T(8,128)S(1)}, f32[64,768]{1,0:T(8,128)S(1)}, u32[]{:S(2)}, u32[]{:S(2)}) collective-permute-start(f32[64,768]{1,0:T(8,128)S(1)} %copy-done.13), channel_id=1, source_target_pairs={{0,64},{64,0},{128,192},{192,128},{1,65},{65,1},{129,193},{193,129... | collective-permute-start | bytes 589832 | tf_op jit(solution)/shard_map/ppermute | solution.py:38
  27.3 13.7 %collective-permute-start.2 = (f32[64,768]{1,0:T(8,128)S(1)}, f32[64,768]{1,0:T(8,128)S(1)}, u32[]{:S(2)}, u32[]{:S(2)}) collective-permute-start(f32[64,768]{1,0:T(8,128)S(1)} %copy-done.12), channel_id=1, source_target_pairs={{0,128},{64,192},{128,0},{192,64},{1,129},{65,193},{129,1},{193,65... | collective-permute-start | bytes 589832 | tf_op jit(solution)/shard_map/ppermute | solution.py:38
  29.7 11.2 %collective-permute-start.3 = (f32[64,768]{1,0:T(8,128)S(1)}, f32[64,768]{1,0:T(8,128)S(1)}, u32[]{:S(2)}, u32[]{:S(2)}) collective-permute-start(f32[64,768]{1,0:T(8,128)S(1)} %copy-done.11), channel_id=1, source_target_pairs={{0,192},{64,128},{128,64},{192,0},{1,193},{65,129},{129,65},{193,1... | collective-permute-start | bytes 589832 | tf_op jit(solution)/shard_map/ppermute | solution.py:38
  30.0 9.1 %collective-permute-start.5 = (f32[64,168]{1,0:T(8,128)S(1)}, f32[64,168]{1,0:T(8,128)S(1)}, u32[]{:S(2)}, u32[]{:S(2)}) collective-permute-start(f32[64,168]{1,0:T(8,128)S(1)} %get-tuple-element.87), channel_id=1, source_target_pairs={{1,0},{2,1},{3,2},{4,3},{5,4},{6,5},{7,6},{8,7},{9,8},{10,9},{11,1... | collective-permute-start | bytes 129032 | tf_op jit(solution)/shard_map/ppermute | solution.py:44
  33.4 7.3 %collective-permute-start.6 = (f32[64,168]{1,0:T(8,128)S(1)}, f32[64,168]{1,0:T(8,128)S(1)}, u32[]{:S(2)}, u32[]{:S(2)}) collective-permute-start(f32[64,168]{1,0:T(8,128)S(1)} %get-tuple-element.88), channel_id=1, source_target_pairs={{0,1},{1,2},{2,3},{3,4},{4,5},{5,6},{6,7},{7,8},{8,9},{9,10},{10,1... | collective-permute-start | bytes 129032 | tf_op jit(solution)/shard_map/ppermute | solution.py:44
  41.0 7.0 %collective-permute-start.4 = (f32[64,768]{1,0:T(8,128)S(1)}, f32[64,768]{1,0:T(8,128)S(1)}, u32[]{:S(2)}, u32[]{:S(2)}) collective-permute-start(f32[64,768]{1,0:T(8,128)S(1)} %add_add_fusion.1), channel_id=1, source_target_pairs={{0,32},{32,0},{1,33},{33,1},{2,34},{34,2},{3,35},{35,3},{4,36},{36... | collective-permute-start | bytes 589832 | tf_op jit(solution)/shard_map/ppermute | solution.py:262
  50.0 27.5 %all-to-all-start.1 = ((f32[16,40,256]{2,1,0:T(8,128)}), f32[16,40,256]{2,1,0:T(8,128)S(1)}, u32[]{:S(2)}, u32[]{:S(2)}) async-start(f32[16,40,256]{2,1,0:T(8,128)} %broadcast_in_dim.32), calls=%async_computation.1 | async-start | bytes 1310720 | tf_op jit(solution)/shard_map/all_to_all | solution.py:32
  59.0 17.5 %collective-permute-start.9 = (f32[64,768]{1,0:T(8,128)S(1)}, f32[64,768]{1,0:T(8,128)S(1)}, u32[]{:S(2)}, u32[]{:S(2)}) collective-permute-start(f32[64,768]{1,0:T(8,128)S(1)} %fusion.20.refs_0_), channel_id=1, source_target_pairs={{0,192},{64,128},{128,64},{192,0},{1,193},{65,129},{129,65},{193,1... | collective-permute-start | bytes 589832 | tf_op jit(solution)/shard_map/ppermute | solution.py:38
  61.5 15.0 %collective-permute-start.8 = (f32[64,768]{1,0:T(8,128)S(1)}, f32[64,768]{1,0:T(8,128)S(1)}, u32[]{:S(2)}, u32[]{:S(2)}) collective-permute-start(f32[64,768]{1,0:T(8,128)S(1)} %fusion.20.refs_0_), channel_id=1, source_target_pairs={{0,128},{64,192},{128,0},{192,64},{1,129},{65,193},{129,1},{193,65... | collective-permute-start | bytes 589832 | tf_op jit(solution)/shard_map/ppermute | solution.py:38
  62.1 15.1 %collective-permute-start.7 = (f32[64,768]{1,0:T(8,128)S(1)}, f32[64,768]{1,0:T(8,128)S(1)}, u32[]{:S(2)}, u32[]{:S(2)}) collective-permute-start(f32[64,768]{1,0:T(8,128)S(1)} %fusion.20.refs_0_), channel_id=1, source_target_pairs={{0,64},{64,0},{128,192},{192,128},{1,65},{65,1},{129,193},{193,129... | collective-permute-start | bytes 589832 | tf_op jit(solution)/shard_map/ppermute | solution.py:38
  62.4 10.7 %collective-permute-start.11 = (f32[64,168]{1,0:T(8,128)S(1)}, f32[64,168]{1,0:T(8,128)S(1)}, u32[]{:S(2)}, u32[]{:S(2)}) collective-permute-start(f32[64,168]{1,0:T(8,128)S(1)} %get-tuple-element.85), channel_id=1, source_target_pairs={{1,0},{2,1},{3,2},{4,3},{5,4},{6,5},{7,6},{8,7},{9,8},{10,9},{11,1... | collective-permute-start | bytes 129032 | tf_op jit(solution)/shard_map/ppermute | solution.py:44
  67.3 9.2 %collective-permute-start.10 = (f32[64,168]{1,0:T(8,128)S(1)}, f32[64,168]{1,0:T(8,128)S(1)}, u32[]{:S(2)}, u32[]{:S(2)}) collective-permute-start(f32[64,168]{1,0:T(8,128)S(1)} %get-tuple-element.86), channel_id=1, source_target_pairs={{0,1},{1,2},{2,3},{3,4},{4,5},{5,6},{6,7},{7,8},{8,9},{9,10},{10,1... | collective-permute-start | bytes 129032 | tf_op jit(solution)/shard_map/ppermute | solution.py:44
  77.6 7.0 %collective-permute-start.12 = (f32[640,256]{1,0:T(8,128)S(1)}, f32[640,256]{1,0:T(8,128)S(1)}, u32[]{:S(2)}, u32[]{:S(2)}) collective-permute-start(f32[640,256]{1,0:T(8,128)S(1)} %bitcast.12), channel_id=1, source_target_pairs={{0,1},{1,0},{2,3},{3,2},{4,5},{5,4},{6,7},{7,6},{8,9},{9,8},{10,11... | collective-permute-start | bytes 1966088 | tf_op jit(solution)/shard_map/ppermute | solution.py:274
  91.5 24.9 %all-to-all-start.2 = ((f32[16,40,256]{2,1,0:T(8,128)}), f32[16,40,256]{2,1,0:T(8,128)S(1)}, u32[]{:S(2)}, u32[]{:S(2)}) async-start(f32[16,40,256]{2,1,0:T(8,128)} %bitcast.7), calls=%async_computation.2 | async-start | bytes 1310720 | tf_op jit(solution)/shard_map/all_to_all | solution.py:27
  95.3 6.4 %collective-permute-start.14 = (f32[64,768]{1,0:T(8,128)}, f32[64,768]{1,0:T(8,128)S(1)}, u32[]{:S(2)}, u32[]{:S(2)}) collective-permute-start(f32[64,768]{1,0:T(8,128)} %copy-done.7), channel_id=1, source_target_pairs={{0,64},{64,0},{128,192},{192,128},{1,65},{65,1},{129,193},{193,129... | collective-permute-start | bytes 589832 | tf_op jit(solution)/shard_map/ppermute | solution.py:38
  96.6 11.6 %collective-permute-start.15 = (f32[64,768]{1,0:T(8,128)}, f32[64,768]{1,0:T(8,128)S(1)}, u32[]{:S(2)}, u32[]{:S(2)}) collective-permute-start(f32[64,768]{1,0:T(8,128)} %copy-done.6), channel_id=1, source_target_pairs={{0,128},{64,192},{128,0},{192,64},{1,129},{65,193},{129,1},{193,65... | collective-permute-start | bytes 589832 | tf_op jit(solution)/shard_map/ppermute | solution.py:38
  99.1 11.4 %collective-permute-start.16 = (f32[64,768]{1,0:T(8,128)}, f32[64,768]{1,0:T(8,128)S(1)}, u32[]{:S(2)}, u32[]{:S(2)}) collective-permute-start(f32[64,768]{1,0:T(8,128)} %copy-done.5), channel_id=1, source_target_pairs={{0,192},{64,128},{128,64},{192,0},{1,193},{65,129},{129,65},{193,1... | collective-permute-start | bytes 589832 | tf_op jit(solution)/shard_map/ppermute | solution.py:38
  110.5 5.7 %collective-permute-start.17 = (f32[64,768]{1,0:T(8,128)S(1)}, f32[64,768]{1,0:T(8,128)S(1)}, u32[]{:S(2)}, u32[]{:S(2)}) collective-permute-start(f32[64,768]{1,0:T(8,128)S(1)} %add_add_fusion), channel_id=1, source_target_pairs={{0,32},{32,0},{1,33},{33,1},{2,34},{34,2},{3,35},{35,3},{4,36},{36... | collective-permute-start | bytes 589832 | tf_op jit(solution)/shard_map/ppermute | solution.py:262
  117.4 27.2 %all-to-all-start.3 = ((f32[16,40,256]{2,1,0:T(8,128)}), f32[16,40,256]{2,1,0:T(8,128)S(1)}, u32[]{:S(2)}, u32[]{:S(2)}) async-start(f32[16,40,256]{2,1,0:T(8,128)} %broadcast_in_dim.33), calls=%async_computation.3 | async-start | bytes 1310720 | tf_op jit(solution)/shard_map/all_to_all | solution.py:32
  125.8 8.2 %collective-permute-start.20 = (f32[64,768]{1,0:T(8,128)S(1)}, f32[64,768]{1,0:T(8,128)S(1)}, u32[]{:S(2)}, u32[]{:S(2)}) collective-permute-start(f32[64,768]{1,0:T(8,128)S(1)} %fusion.13.refs_0_), channel_id=1, source_target_pairs={{0,192},{64,128},{128,64},{192,0},{1,193},{65,129},{129,65},{193,1... | collective-permute-start | bytes 589832 | tf_op jit(solution)/shard_map/ppermute | solution.py:38
  127.6 6.5 %collective-permute-start.19 = (f32[64,768]{1,0:T(8,128)S(1)}, f32[64,768]{1,0:T(8,128)S(1)}, u32[]{:S(2)}, u32[]{:S(2)}) collective-permute-start(f32[64,768]{1,0:T(8,128)S(1)} %fusion.13.refs_0_), channel_id=1, source_target_pairs={{0,128},{64,192},{128,0},{192,64},{1,129},{65,193},{129,1},{193,65... | collective-permute-start | bytes 589832 | tf_op jit(solution)/shard_map/ppermute | solution.py:38
  128.6 7.0 %collective-permute-start.18 = (f32[64,768]{1,0:T(8,128)S(1)}, f32[64,768]{1,0:T(8,128)S(1)}, u32[]{:S(2)}, u32[]{:S(2)}) collective-permute-start(f32[64,768]{1,0:T(8,128)S(1)} %fusion.13.refs_0_), channel_id=1, source_target_pairs={{0,64},{64,0},{128,192},{192,128},{1,65},{65,1},{129,193},{193,129... | collective-permute-start | bytes 589832 | tf_op jit(solution)/shard_map/ppermute | solution.py:38
  144.6 5.3 %collective-permute-start.21 = (f32[640,256]{1,0:T(8,128)S(1)}, f32[640,256]{1,0:T(8,128)S(1)}, u32[]{:S(2)}, u32[]{:S(2)}) collective-permute-start(f32[640,256]{1,0:T(8,128)S(1)} %bitcast.14), channel_id=1, source_target_pairs={{0,1},{1,0},{2,3},{3,2},{4,5},{5,4},{6,7},{7,6},{8,9},{9,8},{10,11... | collective-permute-start | bytes 1966088 | tf_op jit(solution)/shard_map/ppermute | solution.py:274
  (16 other events, 228.9 us)

commit v4 on v3

v4 whole, which is shorter than its diff:
```python
import functools

import jax
import jax.numpy as jnp
from jax import lax
from jax.experimental import pallas as pl
from jax.experimental.pallas import tpu as pltpu
from jax.sharding import Mesh
from jax.sharding import PartitionSpec as P

ITERS = 2
LAGS = (1, 24, 168)
EDGE = 168
SERIES = ("x", "y_lo")
FAR = ("z", "y_hi")
CORE = "core"
TM = (*FAR, CORE)
SWAP = ((0, 1), (1, 0))
STEPS = 2
HIDDEN = 1e30
BF16, F32 = jnp.bfloat16, jnp.float32


def scattered_sum(array, axis):
    parts = array.reshape(lax.axis_size(axis), -1, array.shape[-1])
    return lax.all_to_all(parts, axis, 0, 0, tiled=True).sum(axis=0)


def gathered(array, axis):
    parts = jnp.broadcast_to(array[None], (lax.axis_size(axis), *array.shape))
    parts = lax.all_to_all(parts, axis, 0, 0, tiled=True)
    return parts.reshape(-1, array.shape[-1])


def traded(array, axis, bits):
    length = lax.axis_size(axis)
    return lax.ppermute(array, axis, [(i, i ^ bits) for i in range(length)])


def passed_along(array, axis, by):
    length = lax.axis_size(axis)
    pairs = [(i, i + by) for i in range(length) if 0 <= i + by < length]
    return lax.ppermute(array, axis, pairs)


def edges_of(now):
    return passed_along(now[:, -EDGE:], TM, 1), passed_along(now[:, :EDGE], TM, -1)


def lag_terms(now, edges, weights, first, last):
    before, after = edges
    hours = now.shape[1]
    wide = jnp.concatenate([before, now, after], axis=1)
    length = hours + EDGE
    resid = wide[:, EDGE:]
    for lag, weight in zip(LAGS, weights):
        resid = resid - weight[:, None] * wide[:, EDGE - lag : EDGE - lag + length]
    column = jnp.arange(length)
    inside = (~first | (column >= EDGE)) & (~last | (column < hours))
    resid = jnp.where(inside[None, :], resid, 0.0)
    back = None
    for lag, weight in zip(LAGS, weights):
        term = weight[:, None] * resid[:, lag : lag + hours]
        back = term if back is None else back + term
    return resid[:, :hours] - back


def dot(a, b):
    return jnp.dot(a, b, preferred_element_type=F32)


def by_hours(misfit, x_low):
    return lax.dot_general(misfit, x_low, (((1,), (1,)), ((), ())), preferred_element_type=F32)


def by_rows(f_low, misfit):
    return lax.dot_general(f_low, misfit, (((0,), (0,)), ((), ())), preferred_element_type=F32)


def add_up(total_ref, term, start_ref=None):
    @pl.when(pl.program_id(0) == 0)
    def _():
        total_ref[...] = term if start_ref is None else start_ref[...] + term

    @pl.when(pl.program_id(0) > 0)
    def _():
        total_ref[...] += term


def share_out(along, total_ref, pieces):
    @pl.when(pl.program_id(0) == STEPS - 1)
    def _():
        for k, piece in enumerate(pieces):
            size = piece.shape[0]
            start = pl.multiple_of((along ^ k) * size, size)
            piece[...] = total_ref[pl.ds(start, size), :]


def assembled(along, pieces, *outs):
    @pl.when(pl.program_id(0) == 0)
    def _():
        for k, piece in enumerate(pieces):
            size = piece.shape[0]
            start = pl.multiple_of((along ^ k) * size, size)
            for out in outs:
                out[pl.ds(start, size), :] = piece[...].astype(out.dtype)


def first_half(x_ref, f_ref, seen_ref, mask_ref, grad_ref, kept_ref, x_low_ref):
    @pl.when(pl.program_id(0) == 0)
    def _():
        x_low_ref[...] = x_ref[...].astype(BF16)

    x_low = x_low_ref[...]
    f_low = f_ref[...].astype(BF16)
    keep = mask_ref[...] != 0
    seen = seen_ref[...].astype(F32)
    misfit = jnp.where(keep, dot(f_low, x_low) - seen, 0.0).astype(BF16)
    kept_ref[...] = jnp.where(keep, seen, HIDDEN).astype(BF16)
    grad_ref[...] = by_hours(misfit, x_low)
    return by_rows(f_low, misfit)


def first_theirs(_, x_ref, f_ref, seen_ref, mask_ref, grad_ref, kept_ref, total_ref, x_low_ref):
    add_up(total_ref, first_half(x_ref, f_ref, seen_ref, mask_ref, grad_ref, kept_ref, x_low_ref))


def first_mine(place_ref, x_ref, f_ref, seen_ref, mask_ref, start_ref, grad_ref, kept_ref, *refs):
    *pieces, x_low_ref, total_ref = refs
    term = first_half(x_ref, f_ref, seen_ref, mask_ref, grad_ref, kept_ref, x_low_ref)
    add_up(total_ref, term, start_ref)
    share_out(place_ref[1], total_ref, pieces)


def misfit_of(f_low, x_low, kept_ref):
    kept = kept_ref[...].astype(F32)
    return jnp.where(kept < HIDDEN / 2, dot(f_low, x_low) - kept, 0.0).astype(BF16)


def later_mine(place_ref, *refs):
    *came, f_ref, kept_ref, grad_ref, total_ref, x_low_ref = refs
    assembled(place_ref[1], came, x_low_ref)
    x_low = x_low_ref[...]
    f_low = f_ref[...].astype(BF16)
    misfit = misfit_of(f_low, x_low, kept_ref)
    grad_ref[...] = by_hours(misfit, x_low)
    add_up(total_ref, by_rows(f_low, misfit))


def later_theirs(_, x_low_ref, f_ref, kept_ref, grad_ref, misfit_ref):
    x_low = x_low_ref[...]
    misfit = misfit_of(f_ref[...].astype(BF16), x_low, kept_ref)
    misfit_ref[...] = misfit
    grad_ref[...] = by_hours(misfit, x_low)


def later_rows(place_ref, f_ref, misfit_ref, start_ref, *refs):
    *pieces, total_ref = refs
    add_up(total_ref, by_rows(f_ref[...].astype(BF16), misfit_ref[...]), start_ref)
    share_out(place_ref[1], total_ref, pieces)


def last_mine(place_ref, *refs):
    *came, f_ref, f_out_ref, imputed_ref, x_out_ref, x_low_ref = refs
    assembled(place_ref[1], came, x_out_ref, x_low_ref)
    f_out_ref[...] = f_ref[...]
    imputed_ref[...] = dot(f_ref[...].astype(BF16), x_low_ref[...]).astype(BF16)


def last_theirs(_, x_low_ref, f_ref, f_held_ref, imputed_held_ref, f_out_ref, imputed_ref):
    f_out_ref[...] = f_ref[...]
    imputed_ref[...] = dot(f_ref[...].astype(BF16), x_low_ref[...]).astype(BF16)


def half_pass(kernel, place, ins, outs, limit, matmuls, scratch=(), aliases=()):
    maps = {
        "whole": lambda i, p: (0, 0),
        "half": lambda i, p: (i, 0),
        "mine": lambda i, p: (p[0] * STEPS + i, 0),
        "theirs": lambda i, p: ((1 - p[0]) * STEPS + i, 0),
    }
    tiles = {"whole": 1, "half": STEPS, "mine": 2 * STEPS, "theirs": 2 * STEPS}

    def spec(kind, shape):
        if kind == "held":
            return pl.BlockSpec(memory_space=pl.ANY)
        return pl.BlockSpec((shape[0] // tiles[kind], shape[1]), maps[kind])

    moved = sum(
        a.size * a.dtype.itemsize // (2 if k in ("mine", "theirs") else 1)
        for k, a in [*ins, *outs]
        if k != "held"
    )
    work = max(a.size for _, a in [*ins, *outs]) * 256 // 2
    return pl.pallas_call(
        kernel,
        out_shape=[s for _, s in outs],
        grid_spec=pltpu.PrefetchScalarGridSpec(
            num_scalar_prefetch=1,
            grid=(STEPS,),
            in_specs=[spec(k, a.shape) for k, a in ins],
            out_specs=[spec(k, s.shape) for k, s in outs],
            scratch_shapes=list(scratch),
        ),
        compiler_params=pltpu.CompilerParams(vmem_limit_bytes=limit * 2**20),
        cost_estimate=pl.CostEstimate(
            flops=2 * matmuls * work, bytes_accessed=moved, transcendentals=0
        ),
        input_output_aliases=dict(aliases),
        name=kernel.__name__,
    )(place, *[a for _, a in ins])


def local(observed, mask, series_factors, time_factors, ar_weights):
    rows, hours = observed.shape
    rank = time_factors.shape[0]
    hours_all = hours * lax.axis_size(TM)
    rows_all = rows * lax.axis_size(SERIES)
    step_f = rank / hours_all
    step_x = 1.0 / rows_all
    ridge_f = 0.1 * hours_all / rank
    ridge_x = 0.1 * rows_all
    lam = rows_all / 8.0

    half = rows // 2
    core = lax.axis_index(CORE)
    line = half // lax.axis_size(FAR)
    own_row = core * half + lax.axis_index(FAR) * line
    peers = lax.axis_size("x")
    band = rank // peers
    along = lax.axis_index("x")
    position = lax.axis_index(TM)
    first, last = position == 0, position == lax.axis_size(TM) - 1
    place = jnp.stack([core, along])

    def shape(n, m, dtype=F32):
        return jax.ShapeDtypeStruct((n, m), dtype)

    grad = ("half", shape(half, rank))
    flags = ("half", shape(half, hours, BF16))
    total = ("whole", shape(rank, hours))
    low = ("whole", shape(rank, hours, BF16))
    shares = [("whole", shape(band, hours))] * peers
    total_scratch = pltpu.VMEM((rank, hours), F32)
    low_scratch = pltpu.VMEM((rank, hours), BF16)
    f_part = lax.dynamic_slice_in_dim(series_factors, own_row, line, 0)
    x_part = lax.dynamic_slice_in_dim(time_factors, along * band, band, 0)
    w_part = lax.dynamic_slice_in_dim(ar_weights, along * band, band, 1)
    for sweep in range(ITERS):
        if sweep == 0:
            theirs, kept_theirs, start = half_pass(
                first_theirs,
                place,
                [("whole", time_factors), ("theirs", series_factors), ("theirs", observed), ("theirs", mask)],
                [grad, flags, total],
                58,
                3,
                [low_scratch],
            )
            came = lax.ppermute(theirs, CORE, SWAP)
            mine, kept_mine, *parts = half_pass(
                first_mine,
                place,
                [("whole", time_factors), ("mine", series_factors), ("mine", observed), ("mine", mask), ("whole", start)],
                [grad, flags, *shares],
                58,
                3,
                [low_scratch, total_scratch],
            )
        else:
            mine, start, x_low = half_pass(
                later_mine,
                place,
                [*[("whole", p) for p in pieces], ("half", f_mine), ("half", kept_mine)],
                [grad, total, low],
                16,
                3,
            )
            theirs, misfit = half_pass(
                later_theirs,
                place,
                [("whole", x_low), ("half", f_theirs), ("half", kept_theirs)],
                [grad, flags],
                16,
                2,
            )
            came = lax.ppermute(theirs, CORE, SWAP)
            parts = half_pass(
                later_rows,
                place,
                [("half", f_theirs), ("half", misfit), ("whole", start)],
                shares,
                16,
                1,
                [total_scratch],
            )
        mine = mine + came
        mine, parts, x_part = lax.optimization_barrier((mine, parts, x_part))
        if sweep == 0:
            edges = edges_of(x_part)
        f_sum = scattered_sum(mine, FAR)
        x_sum = parts[0]
        for k in range(1, peers):
            x_sum = x_sum + traded(parts[k], "x", k)
        x_sum = x_sum + lax.ppermute(x_sum, "y_lo", SWAP)
        lag = lag_terms(x_part, edges, w_part, first, last)
        f_part = f_part - step_f * (f_sum + ridge_f * f_part)
        x_part = x_part - step_x * (x_sum + ridge_x * x_part + lam * lag)
        f_part, x_part = lax.optimization_barrier((f_part, x_part))
        f_mine = gathered(f_part, FAR)
        pieces = [x_part] + [traded(x_part, "x", k) for k in range(1, peers)]
        if sweep + 1 < ITERS:
            edges = edges_of(x_part)
            f_mine, pieces, edges = lax.optimization_barrier((f_mine, pieces, edges))
        else:
            f_mine, pieces = lax.optimization_barrier((f_mine, pieces))
        f_theirs = lax.ppermute(f_mine, CORE, SWAP)
    f_out, imputed, x_out, x_low = half_pass(
        last_mine,
        place,
        [*[("whole", p) for p in pieces], ("half", f_mine)],
        [("mine", shape(rows, rank)), ("mine", shape(rows, hours, BF16)), total, low],
        16,
        1,
    )
    f_out, imputed = half_pass(
        last_theirs,
        place,
        [("whole", x_low), ("half", f_theirs), ("held", f_out), ("held", imputed)],
        [("theirs", shape(rows, rank)), ("theirs", shape(rows, hours, BF16))],
        16,
        1,
        aliases={3: 0, 4: 1},
    )
    return f_out, x_out, imputed


def solution(mesh):
    far = mesh.shape["tm"] // 4
    near = mesh.shape["series"] // 2
    split = Mesh(mesh.devices.reshape(near, 2, far, 2, 2), (*SERIES, *TM))
    in_specs = (P(SERIES, TM), P(SERIES, TM), P(SERIES, None), P(None, TM), P())
    out_specs = (P(SERIES, None), P(None, TM), P(SERIES, TM))
    return jax.shard_map(local, mesh=split, in_specs=in_specs, out_specs=out_specs, check_vma=False)
```

time: 154 us -> 153 us (level)
  waiting for transfers between devices: 50.6 us -> 45.3 us
  Pallas kernels: 15.4 us -> 20.5 us
    pallas_call x3 -> x7, Pallas kernels: 15.4 us -> 20.5 us  [half_pass(): pl.pallas_call(kernel, out_shape=[s for _, s in outs], grid_spec=pltpu.Pr...]
    ppermute x2, waiting for transfers between devices: 3.45 us -> 0.01 us  [local(): f_theirs = lax.ppermute(f_mine, CORE, SWAP)]
    ppermute x2, waiting for transfers between devices: 2.64 us -> 0.46 us  [local(): came = lax.ppermute(theirs, CORE, SWAP)]
  transfers between devices with their start and end apart: 26 -> 26, of which waited for: 17 -> 15; matrix products, arithmetic and copies ran while one was open for 2% -> 2% of each run, Pallas kernels for 0% -> 8%
where the time goes in v4:
time: 153 us; the launch traced here: 152 us
  starting transfers between devices  75.5 us (49%)
  waiting for transfers between devices  45.3 us (30%)
  Pallas kernels  20.5 us (13%)
  other arithmetic  5.59 us (4%)
  local copies, waits for them, and re-layouts  4.08 us (3%)
    pallas_call x7, Pallas kernels, half_pass(): pl.pallas_call(kernel, out_shape=[s for _, s in outs], grid_spec=pltpu.Pr...  20.5 us
    ppermute x12, waiting for transfers between devices, traded(): return lax.ppermute(array, axis, [(i, i ^ bits) for i in range(length)])  18.3 us
    ppermute x4, starting transfers between devices, passed_along(): return lax.ppermute(array, axis, pairs)  17.9 us
    all_to_all x2, starting transfers between devices, gathered(): parts = lax.all_to_all(parts, axis, 0, 0, tiled=True)  16.6 us
    ppermute x12, starting transfers between devices, traded(): return lax.ppermute(array, axis, [(i, i ^ bits) for i in range(length)])  14.9 us
    all_to_all x2, starting transfers between devices, scattered_sum(): return lax.all_to_all(parts, axis, 0, 0, tiled=True).sum(axis=0)  12.8 us
    ppermute x2, waiting for transfers between devices, local(): x_sum = x_sum + lax.ppermute(x_sum, 'y_lo', SWAP)  11.6 us
    ppermute x2, starting transfers between devices, local(): f_theirs = lax.ppermute(f_mine, CORE, SWAP)  8.81 us
  transfers between devices with their start and end apart: 26, of which 15 were waited for; matrix products, arithmetic and copies ran while one was open for 2% of the time, Pallas kernels for 8%

profile of v4, /device:TPU:1, one launch (start us, length us, event | category | flops | bytes accessed | tf_op | source)
XLA Modules:
  0.0 152.0 jit_solution(14419834493784348978)
XLA Ops:
  1.2 5.3 %first_theirs.1 = (f32[640,256]{1,0:T(8,128)}, bf16[640,768]{1,0:T(8,128)(2,1)}, f32[256,768]{1,0:T(8,128)}) custom-call(s32[2]{0:T(128)} %pad_add_fusion._.place_ref, f32[256,768]{1,0:T(8,128)} %x_ref.3, f32[1280,256]{1,0:T(8,128)} %f_ref.3, bf16[1280,768]{1,0:T(8,128)(2,1)} %seen_ref.3, s32[1280,768]{1,0:T(8,128)} %mask_ref.3), custom_call_target="tpu_custom_call" | custom-call | flops 754974720 | bytes 6815744 | tf_op jit(solution)/shard_map/first_theirs/pallas_call | solution.py:195
  6.5 3.3 %collective-permute-start = (f32[640,256]{1,0:T(8,128)}, f32[640,256]{1,0:T(8,128)S(1)}, u32[]{:S(2)}, u32[]{:S(2)}) collective-permute-start(f32[640,256]{1,0:T(8,128)} %get-tuple-element.57), channel_id=1, source_target_pairs={{0,1},{1,0},{2,3},{3,2},{4,5},{5,4},{6,7},{7,6},{8,9},{9,8},{10,11... | collective-permute-start | bytes 1966088 | tf_op jit(solution)/shard_map/ppermute | solution.py:260
  9.8 5.6 %first_mine.1 = (f32[640,256]{1,0:T(8,128)}, bf16[640,768]{1,0:T(8,128)(2,1)}, f32[64,768]{1,0:T(8,128)}, f32[64,768]{1,0:T(8,128)}, f32[64,768]{1,0:T(8,128)}, /*index=5*/f32[64,768]{1,0:T(8,128)}) custom-call(s32[2]{0:T(128)} %pad_add_fusion._.place_ref, f32[256,768]{1,0:T(8,128)} %x_ref.3, f32[1280,256]{1,0:T(8,128)} %f_ref.3, ...), custom_call_target="tpu_custom_call" | custom-call | flops 754974720 | bytes 7602176 | tf_op jit(solution)/shard_map/first_mine/pallas_call | solution.py:195
  18.7 9.2 %all-to-all-start = ((f32[16,40,256]{2,1,0:T(8,128)}), f32[16,40,256]{2,1,0:T(8,128)S(1)}, u32[]{:S(2)}, u32[]{:S(2)}) async-start(f32[16,40,256]{2,1,0:T(8,128)} %bitcast.2), calls=%async_computation | async-start | bytes 1310720 | tf_op jit(solution)/shard_map/all_to_all | solution.py:26
  29.2 2.5 %collective-permute-start.2 = (f32[64,768]{1,0:T(8,128)S(1)}, f32[64,768]{1,0:T(8,128)S(1)}, u32[]{:S(2)}, u32[]{:S(2)}) collective-permute-start(f32[64,768]{1,0:T(8,128)S(1)} %copy-done.8), channel_id=1, source_target_pairs={{0,128},{64,192},{128,0},{192,64},{1,129},{65,193},{129,1},{193,65... | collective-permute-start | bytes 589832 | tf_op jit(solution)/shard_map/ppermute | solution.py:37
  31.9 3.1 %collective-permute-start.5 = (f32[64,168]{1,0:T(8,128)S(1)}, f32[64,168]{1,0:T(8,128)S(1)}, u32[]{:S(2)}, u32[]{:S(2)}) collective-permute-start(f32[64,168]{1,0:T(8,128)S(1)} %get-tuple-element.109), channel_id=1, source_target_pairs={{1,0},{2,1},{3,2},{4,3},{5,4},{6,5},{7,6},{8,7},{9,8},{10,9},{11,1... | collective-permute-start | bytes 129032 | tf_op jit(solution)/shard_map/ppermute | solution.py:43
  35.0 5.0 %collective-permute-start.6 = (f32[64,168]{1,0:T(8,128)S(1)}, f32[64,168]{1,0:T(8,128)S(1)}, u32[]{:S(2)}, u32[]{:S(2)}) collective-permute-start(f32[64,168]{1,0:T(8,128)S(1)} %get-tuple-element.110), channel_id=1, source_target_pairs={{0,1},{1,2},{2,3},{3,4},{4,5},{5,6},{6,7},{7,8},{8,9},{9,10},{10,1... | collective-permute-start | bytes 129032 | tf_op jit(solution)/shard_map/ppermute | solution.py:43
  43.7 6.2 %collective-permute-done.4 = f32[64,768]{1,0:T(8,128)S(1)} collective-permute-done((f32[64,768]{1,0:T(8,128)S(1)}, f32[64,768]{1,0:T(8,128)S(1)}, u32[]{:S(2)}, u32[]{:S(2)}) %collective-permute-start.4) | collective-permute-done | bytes 196640 | tf_op jit(solution)/shard_map/ppermute | solution.py:305
  52.0 8.9 %all-to-all-start.1 = ((f32[16,40,256]{2,1,0:T(8,128)}), f32[16,40,256]{2,1,0:T(8,128)S(1)}, u32[]{:S(2)}, u32[]{:S(2)}) async-start(f32[16,40,256]{2,1,0:T(8,128)} %broadcast_in_dim.32), calls=%async_computation.1 | async-start | bytes 1310720 | tf_op jit(solution)/shard_map/all_to_all | solution.py:31
  60.9 2.6 %collective-permute-start.9 = (f32[64,768]{1,0:T(8,128)S(1)}, f32[64,768]{1,0:T(8,128)S(1)}, u32[]{:S(2)}, u32[]{:S(2)}) collective-permute-start(f32[64,768]{1,0:T(8,128)S(1)} %fusion.20.refs_0_), channel_id=1, source_target_pairs={{0,192},{64,128},{128,64},{192,0},{1,193},{65,129},{129,65},{193,1... | collective-permute-start | bytes 589832 | tf_op jit(solution)/shard_map/ppermute | solution.py:37
  64.3 5.0 %collective-permute-start.11 = (f32[64,168]{1,0:T(8,128)S(1)}, f32[64,168]{1,0:T(8,128)S(1)}, u32[]{:S(2)}, u32[]{:S(2)}) collective-permute-start(f32[64,168]{1,0:T(8,128)S(1)} %get-tuple-element.107), channel_id=1, source_target_pairs={{1,0},{2,1},{3,2},{4,3},{5,4},{6,5},{7,6},{8,7},{9,8},{10,9},{11,1... | collective-permute-start | bytes 129032 | tf_op jit(solution)/shard_map/ppermute | solution.py:43
  69.4 4.9 %collective-permute-start.10 = (f32[64,168]{1,0:T(8,128)S(1)}, f32[64,168]{1,0:T(8,128)S(1)}, u32[]{:S(2)}, u32[]{:S(2)}) collective-permute-start(f32[64,168]{1,0:T(8,128)S(1)} %get-tuple-element.108), channel_id=1, source_target_pairs={{0,1},{1,2},{2,3},{3,4},{4,5},{5,6},{6,7},{7,8},{8,9},{9,10},{10,1... | collective-permute-start | bytes 129032 | tf_op jit(solution)/shard_map/ppermute | solution.py:43
  75.1 3.3 %collective-permute-done.10 = f32[64,168]{1,0:T(8,128)S(1)} collective-permute-done((f32[64,168]{1,0:T(8,128)S(1)}, f32[64,168]{1,0:T(8,128)S(1)}, u32[]{:S(2)}, u32[]{:S(2)}) %collective-permute-start.10) | collective-permute-done | bytes 43040 | tf_op jit(solution)/shard_map/ppermute | solution.py:43
  79.5 5.2 %collective-permute-start.12 = (f32[640,256]{1,0:T(8,128)S(1)}, f32[640,256]{1,0:T(8,128)S(1)}, u32[]{:S(2)}, u32[]{:S(2)}) collective-permute-start(f32[640,256]{1,0:T(8,128)S(1)} %bitcast.14), channel_id=1, source_target_pairs={{0,1},{1,0},{2,3},{3,2},{4,5},{5,4},{6,7},{7,6},{8,9},{9,8},{10,11... | collective-permute-start | bytes 1966088 | tf_op jit(solution)/shard_map/ppermute | solution.py:317
  91.6 3.6 %all-to-all-start.2 = ((f32[16,40,256]{2,1,0:T(8,128)}), f32[16,40,256]{2,1,0:T(8,128)S(1)}, u32[]{:S(2)}, u32[]{:S(2)}) async-start(f32[16,40,256]{2,1,0:T(8,128)} %bitcast.7), calls=%async_computation.2 | async-start | bytes 1310720 | tf_op jit(solution)/shard_map/all_to_all | solution.py:26
  96.5 2.5 %collective-permute-start.15 = (f32[64,768]{1,0:T(8,128)S(1)}, f32[64,768]{1,0:T(8,128)S(1)}, u32[]{:S(2)}, u32[]{:S(2)}) collective-permute-start(f32[64,768]{1,0:T(8,128)S(1)} %get-tuple-element.90), channel_id=1, source_target_pairs={{0,128},{64,192},{128,0},{192,64},{1,129},{65,193},{129,1},{193,65... | collective-permute-start | bytes 589832 | tf_op jit(solution)/shard_map/ppermute | solution.py:37
  101.6 6.4 %collective-permute-done.15 = f32[64,768]{1,0:T(8,128)S(1)} collective-permute-done((f32[64,768]{1,0:T(8,128)S(1)}, f32[64,768]{1,0:T(8,128)S(1)}, u32[]{:S(2)}, u32[]{:S(2)}) %collective-permute-start.15) | collective-permute-done | bytes 196640 | tf_op jit(solution)/shard_map/ppermute | solution.py:37
  111.0 5.4 %collective-permute-done.17 = f32[64,768]{1,0:T(8,128)S(1)} collective-permute-done((f32[64,768]{1,0:T(8,128)S(1)}, f32[64,768]{1,0:T(8,128)S(1)}, u32[]{:S(2)}, u32[]{:S(2)}) %collective-permute-start.17) | collective-permute-done | bytes 196640 | tf_op jit(solution)/shard_map/ppermute | solution.py:305
  117.6 7.7 %all-to-all-start.3 = ((f32[16,40,256]{2,1,0:T(8,128)}), f32[16,40,256]{2,1,0:T(8,128)S(1)}, u32[]{:S(2)}, u32[]{:S(2)}) async-start(f32[16,40,256]{2,1,0:T(8,128)} %broadcast_in_dim.33), calls=%async_computation.3 | async-start | bytes 1310720 | tf_op jit(solution)/shard_map/all_to_all | solution.py:31
  125.3 2.4 %collective-permute-start.20 = (f32[64,768]{1,0:T(8,128)S(1)}, f32[64,768]{1,0:T(8,128)S(1)}, u32[]{:S(2)}, u32[]{:S(2)}) collective-permute-start(f32[64,768]{1,0:T(8,128)S(1)} %fusion.13.refs_0_), channel_id=1, source_target_pairs={{0,192},{64,128},{128,64},{192,0},{1,193},{65,129},{129,65},{193,1... | collective-permute-start | bytes 589832 | tf_op jit(solution)/shard_map/ppermute | solution.py:37
  129.0 6.7 %collective-permute-done.20.refs_3_ = f32[64,768]{1,0:T(8,128)S(1)} collective-permute-done((f32[64,768]{1,0:T(8,128)S(1)}, f32[64,768]{1,0:T(8,128)S(1)}, u32[]{:S(2)}, u32[]{:S(2)}) %collective-permute-start.20) | collective-permute-done | bytes 196640 | tf_op jit(solution)/shard_map/ppermute | solution.py:37
  136.3 7.8 %all-to-all-done.3 = f32[16,40,256]{2,1,0:T(8,128)S(1)} async-done(((f32[16,40,256]{2,1,0:T(8,128)}), f32[16,40,256]{2,1,0:T(8,128)S(1)}, u32[]{:S(2)}, u32[]{:S(2)}) %all-to-all-start.3) | async-done | bytes 655392 | tf_op jit(solution)/shard_map/all_to_all | solution.py:31
  144.1 3.6 %collective-permute-start.21 = (f32[640,256]{1,0:T(8,128)S(1)}, f32[640,256]{1,0:T(8,128)S(1)}, u32[]{:S(2)}, u32[]{:S(2)}) collective-permute-start(f32[640,256]{1,0:T(8,128)S(1)} %bitcast.12), channel_id=1, source_target_pairs={{0,1},{1,0},{2,3},{3,2},{4,5},{5,4},{6,7},{7,6},{8,9},{9,8},{10,11... | collective-permute-start | bytes 1966088 | tf_op jit(solution)/shard_map/ppermute | solution.py:317
  147.6 2.3 %last_mine.1 = (f32[1280,256]{1,0:T(8,128)}, bf16[1280,768]{1,0:T(8,128)(2,1)}, f32[256,768]{1,0:T(8,128)}, bf16[256,768]{1,0:T(8,128)(2,1)S(1)}) custom-call(s32[2]{0:T(128)S(1)} %copy-done.3, f32[64,768]{1,0:T(8,128)S(1)} %fusion.13.refs_0_, f32[64,768]{1,0:T(8,128)S(1)} %collective-permute-done.18.refs_1_, f32[64,768]{1,0:T(8,128)S(1)} %collective-permute-done.19.refs_2_, ...), custom_call_target="tpu_custom_call" | custom-call | flops 251658240 | bytes 4259840 | tf_op jit(solution)/shard_map/last_mine/pallas_call | solution.py:195
  (78 shorter events, 32.5 us)
Async XLA Ops:
  6.5 10.1 %collective-permute-start = (f32[640,256]{1,0:T(8,128)}, f32[640,256]{1,0:T(8,128)S(1)}, u32[]{:S(2)}, u32[]{:S(2)}) collective-permute-start(f32[640,256]{1,0:T(8,128)} %get-tuple-element.57), channel_id=1, source_target_pairs={{0,1},{1,0},{2,3},{3,2},{4,5},{5,4},{6,7},{7,6},{8,9},{9,8},{10,11... | collective-permute-start | bytes 1966088 | tf_op jit(solution)/shard_map/ppermute | solution.py:260
  18.7 31.6 %all-to-all-start = ((f32[16,40,256]{2,1,0:T(8,128)}), f32[16,40,256]{2,1,0:T(8,128)S(1)}, u32[]{:S(2)}, u32[]{:S(2)}) async-start(f32[16,40,256]{2,1,0:T(8,128)} %bitcast.2), calls=%async_computation | async-start | bytes 1310720 | tf_op jit(solution)/shard_map/all_to_all | solution.py:26
  27.9 14.8 %collective-permute-start.1 = (f32[64,768]{1,0:T(8,128)S(1)}, f32[64,768]{1,0:T(8,128)S(1)}, u32[]{:S(2)}, u32[]{:S(2)}) collective-permute-start(f32[64,768]{1,0:T(8,128)S(1)} %copy-done.9), channel_id=1, source_target_pairs={{0,64},{64,0},{128,192},{192,128},{1,65},{65,1},{129,193},{193,129... | collective-permute-start | bytes 589832 | tf_op jit(solution)/shard_map/ppermute | solution.py:37
  29.2 13.5 %collective-permute-start.2 = (f32[64,768]{1,0:T(8,128)S(1)}, f32[64,768]{1,0:T(8,128)S(1)}, u32[]{:S(2)}, u32[]{:S(2)}) collective-permute-start(f32[64,768]{1,0:T(8,128)S(1)} %copy-done.8), channel_id=1, source_target_pairs={{0,128},{64,192},{128,0},{192,64},{1,129},{65,193},{129,1},{193,65... | collective-permute-start | bytes 589832 | tf_op jit(solution)/shard_map/ppermute | solution.py:37
  31.6 11.2 %collective-permute-start.3 = (f32[64,768]{1,0:T(8,128)S(1)}, f32[64,768]{1,0:T(8,128)S(1)}, u32[]{:S(2)}, u32[]{:S(2)}) collective-permute-start(f32[64,768]{1,0:T(8,128)S(1)} %copy-done.7), channel_id=1, source_target_pairs={{0,192},{64,128},{128,64},{192,0},{1,193},{65,129},{129,65},{193,1... | collective-permute-start | bytes 589832 | tf_op jit(solution)/shard_map/ppermute | solution.py:37
  31.9 8.6 %collective-permute-start.5 = (f32[64,168]{1,0:T(8,128)S(1)}, f32[64,168]{1,0:T(8,128)S(1)}, u32[]{:S(2)}, u32[]{:S(2)}) collective-permute-start(f32[64,168]{1,0:T(8,128)S(1)} %get-tuple-element.109), channel_id=1, source_target_pairs={{1,0},{2,1},{3,2},{4,3},{5,4},{6,5},{7,6},{8,7},{9,8},{10,9},{11,1... | collective-permute-start | bytes 129032 | tf_op jit(solution)/shard_map/ppermute | solution.py:43
  35.0 7.5 %collective-permute-start.6 = (f32[64,168]{1,0:T(8,128)S(1)}, f32[64,168]{1,0:T(8,128)S(1)}, u32[]{:S(2)}, u32[]{:S(2)}) collective-permute-start(f32[64,168]{1,0:T(8,128)S(1)} %get-tuple-element.110), channel_id=1, source_target_pairs={{0,1},{1,2},{2,3},{3,4},{4,5},{5,6},{6,7},{7,8},{8,9},{9,10},{10,1... | collective-permute-start | bytes 129032 | tf_op jit(solution)/shard_map/ppermute | solution.py:43
  42.9 7.0 %collective-permute-start.4 = (f32[64,768]{1,0:T(8,128)S(1)}, f32[64,768]{1,0:T(8,128)S(1)}, u32[]{:S(2)}, u32[]{:S(2)}) collective-permute-start(f32[64,768]{1,0:T(8,128)S(1)} %add_add_fusion.1), channel_id=1, source_target_pairs={{0,32},{32,0},{1,33},{33,1},{2,34},{34,2},{3,35},{35,3},{4,36},{36... | collective-permute-start | bytes 589832 | tf_op jit(solution)/shard_map/ppermute | solution.py:305
  52.0 27.5 %all-to-all-start.1 = ((f32[16,40,256]{2,1,0:T(8,128)}), f32[16,40,256]{2,1,0:T(8,128)S(1)}, u32[]{:S(2)}, u32[]{:S(2)}) async-start(f32[16,40,256]{2,1,0:T(8,128)} %broadcast_in_dim.32), calls=%async_computation.1 | async-start | bytes 1310720 | tf_op jit(solution)/shard_map/all_to_all | solution.py:31
  60.9 17.5 %collective-permute-start.9 = (f32[64,768]{1,0:T(8,128)S(1)}, f32[64,768]{1,0:T(8,128)S(1)}, u32[]{:S(2)}, u32[]{:S(2)}) collective-permute-start(f32[64,768]{1,0:T(8,128)S(1)} %fusion.20.refs_0_), channel_id=1, source_target_pairs={{0,192},{64,128},{128,64},{192,0},{1,193},{65,129},{129,65},{193,1... | collective-permute-start | bytes 589832 | tf_op jit(solution)/shard_map/ppermute | solution.py:37
  63.5 15.0 %collective-permute-start.8 = (f32[64,768]{1,0:T(8,128)S(1)}, f32[64,768]{1,0:T(8,128)S(1)}, u32[]{:S(2)}, u32[]{:S(2)}) collective-permute-start(f32[64,768]{1,0:T(8,128)S(1)} %fusion.20.refs_0_), channel_id=1, source_target_pairs={{0,128},{64,192},{128,0},{192,64},{1,129},{65,193},{129,1},{193,65... | collective-permute-start | bytes 589832 | tf_op jit(solution)/shard_map/ppermute | solution.py:37
  64.0 15.1 %collective-permute-start.7 = (f32[64,768]{1,0:T(8,128)S(1)}, f32[64,768]{1,0:T(8,128)S(1)}, u32[]{:S(2)}, u32[]{:S(2)}) collective-permute-start(f32[64,768]{1,0:T(8,128)S(1)} %fusion.20.refs_0_), channel_id=1, source_target_pairs={{0,64},{64,0},{128,192},{192,128},{1,65},{65,1},{129,193},{193,129... | collective-permute-start | bytes 589832 | tf_op jit(solution)/shard_map/ppermute | solution.py:37
  64.3 10.8 %collective-permute-start.11 = (f32[64,168]{1,0:T(8,128)S(1)}, f32[64,168]{1,0:T(8,128)S(1)}, u32[]{:S(2)}, u32[]{:S(2)}) collective-permute-start(f32[64,168]{1,0:T(8,128)S(1)} %get-tuple-element.107), channel_id=1, source_target_pairs={{1,0},{2,1},{3,2},{4,3},{5,4},{6,5},{7,6},{8,7},{9,8},{10,9},{11,1... | collective-permute-start | bytes 129032 | tf_op jit(solution)/shard_map/ppermute | solution.py:43
  69.4 9.0 %collective-permute-start.10 = (f32[64,168]{1,0:T(8,128)S(1)}, f32[64,168]{1,0:T(8,128)S(1)}, u32[]{:S(2)}, u32[]{:S(2)}) collective-permute-start(f32[64,168]{1,0:T(8,128)S(1)} %get-tuple-element.108), channel_id=1, source_target_pairs={{0,1},{1,2},{2,3},{3,4},{4,5},{5,6},{6,7},{7,8},{8,9},{9,10},{10,1... | collective-permute-start | bytes 129032 | tf_op jit(solution)/shard_map/ppermute | solution.py:43
  79.5 7.3 %collective-permute-start.12 = (f32[640,256]{1,0:T(8,128)S(1)}, f32[640,256]{1,0:T(8,128)S(1)}, u32[]{:S(2)}, u32[]{:S(2)}) collective-permute-start(f32[640,256]{1,0:T(8,128)S(1)} %bitcast.14), channel_id=1, source_target_pairs={{0,1},{1,0},{2,3},{3,2},{4,5},{5,4},{6,7},{7,6},{8,9},{9,8},{10,11... | collective-permute-start | bytes 1966088 | tf_op jit(solution)/shard_map/ppermute | solution.py:317
  91.6 25.0 %all-to-all-start.2 = ((f32[16,40,256]{2,1,0:T(8,128)}), f32[16,40,256]{2,1,0:T(8,128)S(1)}, u32[]{:S(2)}, u32[]{:S(2)}) async-start(f32[16,40,256]{2,1,0:T(8,128)} %bitcast.7), calls=%async_computation.2 | async-start | bytes 1310720 | tf_op jit(solution)/shard_map/all_to_all | solution.py:26
  95.2 6.4 %collective-permute-start.14 = (f32[64,768]{1,0:T(8,128)S(1)}, f32[64,768]{1,0:T(8,128)S(1)}, u32[]{:S(2)}, u32[]{:S(2)}) collective-permute-start(f32[64,768]{1,0:T(8,128)S(1)} %get-tuple-element.89), channel_id=1, source_target_pairs={{0,64},{64,0},{128,192},{192,128},{1,65},{65,1},{129,193},{193,129... | collective-permute-start | bytes 589832 | tf_op jit(solution)/shard_map/ppermute | solution.py:37
  96.5 11.6 %collective-permute-start.15 = (f32[64,768]{1,0:T(8,128)S(1)}, f32[64,768]{1,0:T(8,128)S(1)}, u32[]{:S(2)}, u32[]{:S(2)}) collective-permute-start(f32[64,768]{1,0:T(8,128)S(1)} %get-tuple-element.90), channel_id=1, source_target_pairs={{0,128},{64,192},{128,0},{192,64},{1,129},{65,193},{129,1},{193,65... | collective-permute-start | bytes 589832 | tf_op jit(solution)/shard_map/ppermute | solution.py:37
  98.9 11.2 %collective-permute-start.16 = (f32[64,768]{1,0:T(8,128)S(1)}, f32[64,768]{1,0:T(8,128)S(1)}, u32[]{:S(2)}, u32[]{:S(2)}) collective-permute-start(f32[64,768]{1,0:T(8,128)S(1)} %get-tuple-element.91), channel_id=1, source_target_pairs={{0,192},{64,128},{128,64},{192,0},{1,193},{65,129},{129,65},{193,1... | collective-permute-start | bytes 589832 | tf_op jit(solution)/shard_map/ppermute | solution.py:37
  110.2 6.1 %collective-permute-start.17 = (f32[64,768]{1,0:T(8,128)S(1)}, f32[64,768]{1,0:T(8,128)S(1)}, u32[]{:S(2)}, u32[]{:S(2)}) collective-permute-start(f32[64,768]{1,0:T(8,128)S(1)} %add_add_fusion), channel_id=1, source_target_pairs={{0,32},{32,0},{1,33},{33,1},{2,34},{34,2},{3,35},{35,3},{4,36},{36... | collective-permute-start | bytes 589832 | tf_op jit(solution)/shard_map/ppermute | solution.py:305
  117.6 26.5 %all-to-all-start.3 = ((f32[16,40,256]{2,1,0:T(8,128)}), f32[16,40,256]{2,1,0:T(8,128)S(1)}, u32[]{:S(2)}, u32[]{:S(2)}) async-start(f32[16,40,256]{2,1,0:T(8,128)} %broadcast_in_dim.33), calls=%async_computation.3 | async-start | bytes 1310720 | tf_op jit(solution)/shard_map/all_to_all | solution.py:31
  125.3 10.4 %collective-permute-start.20 = (f32[64,768]{1,0:T(8,128)S(1)}, f32[64,768]{1,0:T(8,128)S(1)}, u32[]{:S(2)}, u32[]{:S(2)}) collective-permute-start(f32[64,768]{1,0:T(8,128)S(1)} %fusion.13.refs_0_), channel_id=1, source_target_pairs={{0,192},{64,128},{128,64},{192,0},{1,193},{65,129},{129,65},{193,1... | collective-permute-start | bytes 589832 | tf_op jit(solution)/shard_map/ppermute | solution.py:37
  127.7 8.0 %collective-permute-start.19 = (f32[64,768]{1,0:T(8,128)S(1)}, f32[64,768]{1,0:T(8,128)S(1)}, u32[]{:S(2)}, u32[]{:S(2)}) collective-permute-start(f32[64,768]{1,0:T(8,128)S(1)} %fusion.13.refs_0_), channel_id=1, source_target_pairs={{0,128},{64,192},{128,0},{192,64},{1,129},{65,193},{129,1},{193,65... | collective-permute-start | bytes 589832 | tf_op jit(solution)/shard_map/ppermute | solution.py:37
  129.0 7.3 %collective-permute-start.18 = (f32[64,768]{1,0:T(8,128)S(1)}, f32[64,768]{1,0:T(8,128)S(1)}, u32[]{:S(2)}, u32[]{:S(2)}) collective-permute-start(f32[64,768]{1,0:T(8,128)S(1)} %fusion.13.refs_0_), channel_id=1, source_target_pairs={{0,64},{64,0},{128,192},{192,128},{1,65},{65,1},{129,193},{193,129... | collective-permute-start | bytes 589832 | tf_op jit(solution)/shard_map/ppermute | solution.py:37
  (12 other events, 218.1 us)

commit v5 on v4

--- a/solution.py
+++ b/solution.py
@@ -16,7 +16,7 @@
 CORE = "core"
 TM = (*FAR, CORE)
 SWAP = ((0, 1), (1, 0))
-STEPS = 2
+FIRST, LATER = 5, 2
 HIDDEN = 1e30
 BF16, F32 = jnp.bfloat16, jnp.float32
 
@@ -88,7 +88,7 @@
 
 
 def share_out(along, total_ref, pieces):
-    @pl.when(pl.program_id(0) == STEPS - 1)
+    @pl.when(pl.program_id(0) == pl.num_programs(0) - 1)
     def _():
         for k, piece in enumerate(pieces):
             size = piece.shape[0]
@@ -126,7 +126,13 @@
 
 
 def first_mine(place_ref, x_ref, f_ref, seen_ref, mask_ref, start_ref, grad_ref, kept_ref, *refs):
-    *pieces, x_low_ref, total_ref = refs
+    *pieces, x_part_ref, x_low_ref, total_ref = refs
+    size = x_part_ref.shape[0]
+
+    @pl.when(pl.program_id(0) == 0)
+    def _():
+        x_part_ref[...] = x_ref[pl.ds(pl.multiple_of(place_ref[1] * size, size), size), :]
+
     term = first_half(x_ref, f_ref, seen_ref, mask_ref, grad_ref, kept_ref, x_low_ref)
     add_up(total_ref, term, start_ref)
     share_out(place_ref[1], total_ref, pieces)
@@ -172,14 +178,14 @@
     imputed_ref[...] = dot(f_ref[...].astype(BF16), x_low_ref[...]).astype(BF16)
 
 
-def half_pass(kernel, place, ins, outs, limit, matmuls, scratch=(), aliases=()):
+def half_pass(kernel, place, ins, outs, steps, limit, matmuls, scratch=(), aliases=()):
     maps = {
         "whole": lambda i, p: (0, 0),
         "half": lambda i, p: (i, 0),
-        "mine": lambda i, p: (p[0] * STEPS + i, 0),
-        "theirs": lambda i, p: ((1 - p[0]) * STEPS + i, 0),
+        "mine": lambda i, p: (p[0] * steps + i, 0),
+        "theirs": lambda i, p: ((1 - p[0]) * steps + i, 0),
     }
-    tiles = {"whole": 1, "half": STEPS, "mine": 2 * STEPS, "theirs": 2 * STEPS}
+    tiles = {"whole": 1, "half": steps, "mine": 2 * steps, "theirs": 2 * steps}
 
     def spec(kind, shape):
         if kind == "held":
@@ -197,7 +203,7 @@
         out_shape=[s for _, s in outs],
         grid_spec=pltpu.PrefetchScalarGridSpec(
             num_scalar_prefetch=1,
-            grid=(STEPS,),
+            grid=(steps,),
             in_specs=[spec(k, a.shape) for k, a in ins],
             out_specs=[spec(k, s.shape) for k, s in outs],
             scratch_shapes=list(scratch),
@@ -244,7 +250,6 @@
     total_scratch = pltpu.VMEM((rank, hours), F32)
     low_scratch = pltpu.VMEM((rank, hours), BF16)
     f_part = lax.dynamic_slice_in_dim(series_factors, own_row, line, 0)
-    x_part = lax.dynamic_slice_in_dim(time_factors, along * band, band, 0)
     w_part = lax.dynamic_slice_in_dim(ar_weights, along * band, band, 1)
     for sweep in range(ITERS):
         if sweep == 0:
@@ -253,16 +258,18 @@
                 place,
                 [("whole", time_factors), ("theirs", series_factors), ("theirs", observed), ("theirs", mask)],
                 [grad, flags, total],
+                FIRST,
                 58,
                 3,
                 [low_scratch],
             )
             came = lax.ppermute(theirs, CORE, SWAP)
-            mine, kept_mine, *parts = half_pass(
+            mine, kept_mine, *parts, x_part = half_pass(
                 first_mine,
                 place,
                 [("whole", time_factors), ("mine", series_factors), ("mine", observed), ("mine", mask), ("whole", start)],
-                [grad, flags, *shares],
+                [grad, flags, *shares, shares[0]],
+                FIRST,
                 58,
                 3,
                 [low_scratch, total_scratch],
@@ -273,6 +280,7 @@
                 place,
                 [*[("whole", p) for p in pieces], ("half", f_mine), ("half", kept_mine)],
                 [grad, total, low],
+                LATER,
                 16,
                 3,
             )
@@ -281,6 +289,7 @@
                 place,
                 [("whole", x_low), ("half", f_theirs), ("half", kept_theirs)],
                 [grad, flags],
+                LATER,
                 16,
                 2,
             )
@@ -290,36 +299,33 @@
                 place,
                 [("half", f_theirs), ("half", misfit), ("whole", start)],
                 shares,
+                LATER,
                 16,
                 1,
                 [total_scratch],
             )
         mine = mine + came
         mine, parts, x_part = lax.optimization_barrier((mine, parts, x_part))
-        if sweep == 0:
-            edges = edges_of(x_part)
+        edges = edges_of(x_part)
         f_sum = scattered_sum(mine, FAR)
         x_sum = parts[0]
         for k in range(1, peers):
             x_sum = x_sum + traded(parts[k], "x", k)
+        lag = lag_terms(x_part, edges, w_part, first, last)
+        f_part, x_sum, lag = lax.optimization_barrier((f_part, x_sum, lag))
+        f_part = f_part - step_f * (f_sum + ridge_f * f_part)
         x_sum = x_sum + lax.ppermute(x_sum, "y_lo", SWAP)
-        lag = lag_terms(x_part, edges, w_part, first, last)
-        f_part = f_part - step_f * (f_sum + ridge_f * f_part)
         x_part = x_part - step_x * (x_sum + ridge_x * x_part + lam * lag)
-        f_part, x_part = lax.optimization_barrier((f_part, x_part))
         f_mine = gathered(f_part, FAR)
         pieces = [x_part] + [traded(x_part, "x", k) for k in range(1, peers)]
-        if sweep + 1 < ITERS:
-            edges = edges_of(x_part)
-            f_mine, pieces, edges = lax.optimization_barrier((f_mine, pieces, edges))
-        else:
-            f_mine, pieces = lax.optimization_barrier((f_mine, pieces))
+        f_mine, pieces = lax.optimization_barrier((f_mine, pieces))
         f_theirs = lax.ppermute(f_mine, CORE, SWAP)
     f_out, imputed, x_out, x_low = half_pass(
         last_mine,
         place,
         [*[("whole", p) for p in pieces], ("half", f_mine)],
         [("mine", shape(rows, rank)), ("mine", shape(rows, hours, BF16)), total, low],
+        LATER,
         16,
         1,
     )
@@ -328,6 +334,7 @@
         place,
         [("whole", x_low), ("half", f_theirs), ("held", f_out), ("held", imputed)],
         [("theirs", shape(rows, rank)), ("theirs", shape(rows, hours, BF16))],
+        LATER,
         16,
         1,
         aliases={3: 0, 4: 1},

time: 153 us -> 158 us (1.033)
  waiting for transfers between devices: 45.3 us -> 50.4 us
  Pallas kernels: 20.5 us -> 25 us
  starting transfers between devices: 75.5 us -> 72 us
    ppermute x12, waiting for transfers between devices: 18.3 us -> 32.7 us  [traded(): return lax.ppermute(array, axis, [(i, i ^ bits) for i in range(length)])]
    ppermute x4, waiting for transfers between devices: 6.68 us -> 0.01 us  [passed_along(): return lax.ppermute(array, axis, pairs)]
    pallas_call x7, Pallas kernels: 20.5 us -> 25 us  [half_pass(): pl.pallas_call(kernel, out_shape=[s for _, s in outs], grid_spec=pltpu.Pr...]
    all_to_all x2, waiting for transfers between devices: 8.23 us -> 4.62 us  [gathered(): parts = lax.all_to_all(parts, axis, 0, 0, tiled=True)]
    ppermute x4, starting transfers between devices: 17.9 us -> 14.4 us  [passed_along(): return lax.ppermute(array, axis, pairs)]
    all_to_all x2, starting transfers between devices: 12.8 us -> 15.7 us  [scattered_sum(): return lax.all_to_all(parts, axis, 0, 0, tiled=True).sum(axis=0)]
    ppermute x2, starting transfers between devices: 8.81 us -> 5.91 us  [local(): f_theirs = lax.ppermute(f_mine, CORE, SWAP)]
  transfers between devices with their start and end apart: 26 -> 26, of which waited for: 15 -> 15; matrix products, arithmetic and copies ran while one was open for 2% -> 2% of each run, Pallas kernels for 8% -> 9%
where the time goes in v5:
time: 158 us; the launch traced here: 157 us
  starting transfers between devices  72 us (46%)
  waiting for transfers between devices  50.4 us (32%)
  Pallas kernels  25 us (16%)
  other arithmetic  5.12 us (3%)
  local copies, waits for them, and re-layouts  3.17 us (2%)
    ppermute x12, waiting for transfers between devices, traded(): return lax.ppermute(array, axis, [(i, i ^ bits) for i in range(length)])  32.7 us
    pallas_call x7, Pallas kernels, half_pass(): pl.pallas_call(kernel, out_shape=[s for _, s in outs], grid_spec=pltpu.Pr...  25 us
    all_to_all x2, starting transfers between devices, gathered(): parts = lax.all_to_all(parts, axis, 0, 0, tiled=True)  17.3 us
    all_to_all x2, starting transfers between devices, scattered_sum(): return lax.all_to_all(parts, axis, 0, 0, tiled=True).sum(axis=0)  15.7 us
    ppermute x12, starting transfers between devices, traded(): return lax.ppermute(array, axis, [(i, i ^ bits) for i in range(length)])  14.6 us
    ppermute x4, starting transfers between devices, passed_along(): return lax.ppermute(array, axis, pairs)  14.4 us
    ppermute x2, waiting for transfers between devices, local(): x_sum = x_sum + lax.ppermute(x_sum, 'y_lo', SWAP)  12.4 us
    ppermute x2, starting transfers between devices, local(): f_theirs = lax.ppermute(f_mine, CORE, SWAP)  5.91 us
  transfers between devices with their start and end apart: 26, of which 15 were waited for; matrix products, arithmetic and copies ran while one was open for 2% of the time, Pallas kernels for 9%

profile of v5, /device:TPU:1, one launch (start us, length us, event | category | flops | bytes accessed | tf_op | source)
XLA Modules:
  0.0 156.6 jit_solution(14010253475231981331)
XLA Ops:
  1.3 7.5 %first_theirs.1 = (f32[640,256]{1,0:T(8,128)}, bf16[640,768]{1,0:T(8,128)(2,1)}, f32[256,768]{1,0:T(8,128)}) custom-call(s32[2]{0:T(128)} %pad_add_fusion._.place_ref, f32[256,768]{1,0:T(8,128)} %x_ref.3, f32[1280,256]{1,0:T(8,128)} %f_ref.3, bf16[1280,768]{1,0:T(8,128)(2,1)} %seen_ref.3, s32[1280,768]{1,0:T(8,128)} %mask_ref.3), custom_call_target="tpu_custom_call" | custom-call | flops 754974720 | bytes 6815744 | tf_op jit(solution)/shard_map/first_theirs/pallas_call | solution.py:201
  8.8 3.3 %collective-permute-start = (f32[640,256]{1,0:T(8,128)}, f32[640,256]{1,0:T(8,128)S(1)}, u32[]{:S(2)}, u32[]{:S(2)}) collective-permute-start(f32[640,256]{1,0:T(8,128)} %get-tuple-element.58), channel_id=1, source_target_pairs={{0,1},{1,0},{2,3},{3,2},{4,5},{5,4},{6,7},{7,6},{8,9},{9,8},{10,11... | collective-permute-start | bytes 1966088 | tf_op jit(solution)/shard_map/ppermute | solution.py:266
  12.1 7.9 %first_mine.1 = (f32[640,256]{1,0:T(8,128)}, bf16[640,768]{1,0:T(8,128)(2,1)}, f32[64,768]{1,0:T(8,128)}, f32[64,768]{1,0:T(8,128)}, f32[64,768]{1,0:T(8,128)}, /*index=5*/f32[64,768]{1,0:T(8,128)}, f32[64,768]{1,0:T(8,128)}) custom-call(s32[2]{0:T(128)} %pad_add_fusion._.place_ref, f32[256,768]{1,0:T(8,128)} %x_ref.3, f32[1280,256]{1,0:T(8,128)} %f_ref.3, ...), custom_call_target="tpu_custom_call" | custom-call | flops 754974720 | bytes 7798784 | tf_op jit(solution)/shard_map/first_mine/pallas_call | solution.py:201
  22.3 9.3 %all-to-all-start = ((f32[16,40,256]{2,1,0:T(8,128)}), f32[16,40,256]{2,1,0:T(8,128)S(1)}, u32[]{:S(2)}, u32[]{:S(2)}) async-start(f32[16,40,256]{2,1,0:T(8,128)} %bitcast.5), calls=%async_computation | async-start | bytes 1310720 | tf_op jit(solution)/shard_map/all_to_all | solution.py:26
  34.7 5.0 %collective-permute-start.5 = (f32[64,168]{1,0:T(8,128)S(1)}, f32[64,168]{1,0:T(8,128)S(1)}, u32[]{:S(2)}, u32[]{:S(2)}) collective-permute-start(f32[64,168]{1,0:T(8,128)S(1)} %get-tuple-element.112), channel_id=1, source_target_pairs={{0,1},{1,2},{2,3},{3,4},{4,5},{5,6},{6,7},{7,8},{8,9},{9,10},{10,1... | collective-permute-start | bytes 129032 | tf_op jit(solution)/shard_map/ppermute | solution.py:43
  41.0 2.5 %collective-permute-start.2 = (f32[64,768]{1,0:T(8,128)S(1)}, f32[64,768]{1,0:T(8,128)S(1)}, u32[]{:S(2)}, u32[]{:S(2)}) collective-permute-start(f32[64,768]{1,0:T(8,128)S(1)} %copy-done.7), channel_id=1, source_target_pairs={{0,128},{64,192},{128,0},{192,64},{1,129},{65,193},{129,1},{193,65... | collective-permute-start | bytes 589832 | tf_op jit(solution)/shard_map/ppermute | solution.py:37
  46.4 4.7 %collective-permute-done.2 = f32[64,768]{1,0:T(8,128)S(1)} collective-permute-done((f32[64,768]{1,0:T(8,128)S(1)}, f32[64,768]{1,0:T(8,128)S(1)}, u32[]{:S(2)}, u32[]{:S(2)}) %collective-permute-start.2) | collective-permute-done | bytes 196640 | tf_op jit(solution)/shard_map/ppermute | solution.py:37
  51.1 2.6 %collective-permute-done.3 = f32[64,768]{1,0:T(8,128)S(1)} collective-permute-done((f32[64,768]{1,0:T(8,128)S(1)}, f32[64,768]{1,0:T(8,128)S(1)}, u32[]{:S(2)}, u32[]{:S(2)}) %collective-permute-start.3) | collective-permute-done | bytes 196640 | tf_op jit(solution)/shard_map/ppermute | solution.py:37
  54.7 8.8 %all-to-all-start.1 = ((f32[16,40,256]{2,1,0:T(8,128)}), f32[16,40,256]{2,1,0:T(8,128)S(1)}, u32[]{:S(2)}, u32[]{:S(2)}) async-start(f32[16,40,256]{2,1,0:T(8,128)} %broadcast_in_dim.32), calls=%async_computation.1 | async-start | bytes 1310720 | tf_op jit(solution)/shard_map/all_to_all | solution.py:31
  64.0 6.1 %collective-permute-done.6 = f32[64,768]{1,0:T(8,128)S(1)} collective-permute-done((f32[64,768]{1,0:T(8,128)S(1)}, f32[64,768]{1,0:T(8,128)S(1)}, u32[]{:S(2)}, u32[]{:S(2)}) %collective-permute-start.6) | collective-permute-done | bytes 196640 | tf_op jit(solution)/shard_map/ppermute | solution.py:317
  73.5 8.2 %collective-permute-done.9.refs_3_ = f32[64,768]{1,0:T(8,128)S(1)} collective-permute-done((f32[64,768]{1,0:T(8,128)S(1)}, f32[64,768]{1,0:T(8,128)S(1)}, u32[]{:S(2)}, u32[]{:S(2)}) %collective-permute-start.9) | collective-permute-done | bytes 196640 | tf_op jit(solution)/shard_map/ppermute | solution.py:37
  83.5 3.0 %collective-permute-start.10 = (f32[640,256]{1,0:T(8,128)S(1)}, f32[640,256]{1,0:T(8,128)S(1)}, u32[]{:S(2)}, u32[]{:S(2)}) collective-permute-start(f32[640,256]{1,0:T(8,128)S(1)} %bitcast.14), channel_id=1, source_target_pairs={{0,1},{1,0},{2,3},{3,2},{4,5},{5,4},{6,7},{7,6},{8,9},{9,8},{10,11... | collective-permute-start | bytes 1966088 | tf_op jit(solution)/shard_map/ppermute | solution.py:322
  93.3 6.4 %all-to-all-start.2 = ((f32[16,40,256]{2,1,0:T(8,128)}), f32[16,40,256]{2,1,0:T(8,128)S(1)}, u32[]{:S(2)}, u32[]{:S(2)}) async-start(f32[16,40,256]{2,1,0:T(8,128)} %bitcast.7), calls=%async_computation.2 | async-start | bytes 1310720 | tf_op jit(solution)/shard_map/all_to_all | solution.py:26
  99.8 2.3 %collective-permute-start.15 = (f32[64,168]{1,0:T(8,128)S(1)}, f32[64,168]{1,0:T(8,128)S(1)}, u32[]{:S(2)}, u32[]{:S(2)}) collective-permute-start(f32[64,168]{1,0:T(8,128)S(1)} %get-tuple-element.109), channel_id=1, source_target_pairs={{1,0},{2,1},{3,2},{4,3},{5,4},{6,5},{7,6},{8,7},{9,8},{10,9},{11,1... | collective-permute-start | bytes 129032 | tf_op jit(solution)/shard_map/ppermute | solution.py:43
  102.1 5.0 %collective-permute-start.16 = (f32[64,168]{1,0:T(8,128)S(1)}, f32[64,168]{1,0:T(8,128)S(1)}, u32[]{:S(2)}, u32[]{:S(2)}) collective-permute-start(f32[64,168]{1,0:T(8,128)S(1)} %get-tuple-element.110), channel_id=1, source_target_pairs={{0,1},{1,2},{2,3},{3,4},{4,5},{5,6},{6,7},{7,8},{8,9},{9,10},{10,1... | collective-permute-start | bytes 129032 | tf_op jit(solution)/shard_map/ppermute | solution.py:43
  111.8 2.4 %collective-permute-done.12 = f32[64,768]{1,0:T(8,128)S(1)} collective-permute-done((f32[64,768]{1,0:T(8,128)S(1)}, f32[64,768]{1,0:T(8,128)S(1)}, u32[]{:S(2)}, u32[]{:S(2)}) %collective-permute-start.12) | collective-permute-done | bytes 196640 | tf_op jit(solution)/shard_map/ppermute | solution.py:37
  114.1 2.6 %collective-permute-done.13 = f32[64,768]{1,0:T(8,128)S(1)} collective-permute-done((f32[64,768]{1,0:T(8,128)S(1)}, f32[64,768]{1,0:T(8,128)S(1)}, u32[]{:S(2)}, u32[]{:S(2)}) %collective-permute-start.13) | collective-permute-done | bytes 196640 | tf_op jit(solution)/shard_map/ppermute | solution.py:37
  116.8 2.6 %collective-permute-done.14 = f32[64,768]{1,0:T(8,128)S(1)} collective-permute-done((f32[64,768]{1,0:T(8,128)S(1)}, f32[64,768]{1,0:T(8,128)S(1)}, u32[]{:S(2)}, u32[]{:S(2)}) %collective-permute-start.14) | collective-permute-done | bytes 196640 | tf_op jit(solution)/shard_map/ppermute | solution.py:37
  120.7 8.6 %all-to-all-start.3 = ((f32[16,40,256]{2,1,0:T(8,128)}), f32[16,40,256]{2,1,0:T(8,128)S(1)}, u32[]{:S(2)}, u32[]{:S(2)}) async-start(f32[16,40,256]{2,1,0:T(8,128)} %broadcast_in_dim.33), calls=%async_computation.3 | async-start | bytes 1310720 | tf_op jit(solution)/shard_map/all_to_all | solution.py:31
  129.4 6.3 %collective-permute-done.17 = f32[64,768]{1,0:T(8,128)S(1)} collective-permute-done((f32[64,768]{1,0:T(8,128)S(1)}, f32[64,768]{1,0:T(8,128)S(1)}, u32[]{:S(2)}, u32[]{:S(2)}) %collective-permute-start.17) | collective-permute-done | bytes 196640 | tf_op jit(solution)/shard_map/ppermute | solution.py:317
  139.0 5.8 %collective-permute-done.20.refs_3_ = f32[64,768]{1,0:T(8,128)S(1)} collective-permute-done((f32[64,768]{1,0:T(8,128)S(1)}, f32[64,768]{1,0:T(8,128)S(1)}, u32[]{:S(2)}, u32[]{:S(2)}) %collective-permute-start.20) | collective-permute-done | bytes 196640 | tf_op jit(solution)/shard_map/ppermute | solution.py:37
  146.6 2.7 %all-to-all-done.3 = f32[16,40,256]{2,1,0:T(8,128)S(1)} async-done(((f32[16,40,256]{2,1,0:T(8,128)}), f32[16,40,256]{2,1,0:T(8,128)S(1)}, u32[]{:S(2)}, u32[]{:S(2)}) %all-to-all-start.3) | async-done | bytes 655392 | tf_op jit(solution)/shard_map/all_to_all | solution.py:31
  149.3 3.0 %collective-permute-start.21 = (f32[640,256]{1,0:T(8,128)S(1)}, f32[640,256]{1,0:T(8,128)S(1)}, u32[]{:S(2)}, u32[]{:S(2)}) collective-permute-start(f32[640,256]{1,0:T(8,128)S(1)} %bitcast.12), channel_id=1, source_target_pairs={{0,1},{1,0},{2,3},{3,2},{4,5},{5,4},{6,7},{7,6},{8,9},{9,8},{10,11... | collective-permute-start | bytes 1966088 | tf_op jit(solution)/shard_map/ppermute | solution.py:322
  152.3 2.3 %last_mine.1 = (f32[1280,256]{1,0:T(8,128)}, bf16[1280,768]{1,0:T(8,128)(2,1)}, f32[256,768]{1,0:T(8,128)}, bf16[256,768]{1,0:T(8,128)(2,1)S(1)}) custom-call(s32[2]{0:T(128)S(1)} %copy-done.3, f32[64,768]{1,0:T(8,128)S(1)} %multiply_subtract_fusion.refs_0_, f32[64,768]{1,0:T(8,128)S(1)} %collective-permute-done.18.refs_1_, ...), custom_call_target="tpu_custom_call" | custom-call | flops 251658240 | bytes 4259840 | tf_op jit(solution)/shard_map/last_mine/pallas_call | solution.py:201
  (78 shorter events, 37.1 us)
Async XLA Ops:
  8.8 11.3 %collective-permute-start = (f32[640,256]{1,0:T(8,128)}, f32[640,256]{1,0:T(8,128)S(1)}, u32[]{:S(2)}, u32[]{:S(2)}) collective-permute-start(f32[640,256]{1,0:T(8,128)} %get-tuple-element.58), channel_id=1, source_target_pairs={{0,1},{1,0},{2,3},{3,2},{4,5},{5,4},{6,7},{7,6},{8,9},{9,8},{10,11... | collective-permute-start | bytes 1966088 | tf_op jit(solution)/shard_map/ppermute | solution.py:266
  22.3 31.5 %all-to-all-start = ((f32[16,40,256]{2,1,0:T(8,128)}), f32[16,40,256]{2,1,0:T(8,128)S(1)}, u32[]{:S(2)}, u32[]{:S(2)}) async-start(f32[16,40,256]{2,1,0:T(8,128)} %bitcast.5), calls=%async_computation | async-start | bytes 1310720 | tf_op jit(solution)/shard_map/all_to_all | solution.py:26
  32.5 11.2 %collective-permute-start.4 = (f32[64,168]{1,0:T(8,128)S(1)}, f32[64,168]{1,0:T(8,128)S(1)}, u32[]{:S(2)}, u32[]{:S(2)}) collective-permute-start(f32[64,168]{1,0:T(8,128)S(1)} %get-tuple-element.111), channel_id=1, source_target_pairs={{1,0},{2,1},{3,2},{4,3},{5,4},{6,5},{7,6},{8,7},{9,8},{10,9},{11,1... | collective-permute-start | bytes 129032 | tf_op jit(solution)/shard_map/ppermute | solution.py:43
  34.7 8.9 %collective-permute-start.5 = (f32[64,168]{1,0:T(8,128)S(1)}, f32[64,168]{1,0:T(8,128)S(1)}, u32[]{:S(2)}, u32[]{:S(2)}) collective-permute-start(f32[64,168]{1,0:T(8,128)S(1)} %get-tuple-element.112), channel_id=1, source_target_pairs={{0,1},{1,2},{2,3},{3,4},{4,5},{5,6},{6,7},{7,8},{8,9},{9,10},{10,1... | collective-permute-start | bytes 129032 | tf_op jit(solution)/shard_map/ppermute | solution.py:43
  39.7 6.7 %collective-permute-start.1 = (f32[64,768]{1,0:T(8,128)S(1)}, f32[64,768]{1,0:T(8,128)S(1)}, u32[]{:S(2)}, u32[]{:S(2)}) collective-permute-start(f32[64,768]{1,0:T(8,128)S(1)} %copy-done.8), channel_id=1, source_target_pairs={{0,64},{64,0},{128,192},{192,128},{1,65},{65,1},{129,193},{193,129... | collective-permute-start | bytes 589832 | tf_op jit(solution)/shard_map/ppermute | solution.py:37
  41.0 10.1 %collective-permute-start.2 = (f32[64,768]{1,0:T(8,128)S(1)}, f32[64,768]{1,0:T(8,128)S(1)}, u32[]{:S(2)}, u32[]{:S(2)}) collective-permute-start(f32[64,768]{1,0:T(8,128)S(1)} %copy-done.7), channel_id=1, source_target_pairs={{0,128},{64,192},{128,0},{192,64},{1,129},{65,193},{129,1},{193,65... | collective-permute-start | bytes 589832 | tf_op jit(solution)/shard_map/ppermute | solution.py:37
  43.5 10.3 %collective-permute-start.3 = (f32[64,768]{1,0:T(8,128)S(1)}, f32[64,768]{1,0:T(8,128)S(1)}, u32[]{:S(2)}, u32[]{:S(2)}) collective-permute-start(f32[64,768]{1,0:T(8,128)S(1)} %copy-done.6), channel_id=1, source_target_pairs={{0,192},{64,128},{128,64},{192,0},{1,193},{65,129},{129,65},{193,1... | collective-permute-start | bytes 589832 | tf_op jit(solution)/shard_map/ppermute | solution.py:37
  54.7 28.8 %all-to-all-start.1 = ((f32[16,40,256]{2,1,0:T(8,128)}), f32[16,40,256]{2,1,0:T(8,128)S(1)}, u32[]{:S(2)}, u32[]{:S(2)}) async-start(f32[16,40,256]{2,1,0:T(8,128)} %broadcast_in_dim.32), calls=%async_computation.1 | async-start | bytes 1310720 | tf_op jit(solution)/shard_map/all_to_all | solution.py:31
  63.5 6.6 %collective-permute-start.6 = (f32[64,768]{1,0:T(8,128)S(1)}, f32[64,768]{1,0:T(8,128)S(1)}, u32[]{:S(2)}, u32[]{:S(2)}) collective-permute-start(f32[64,768]{1,0:T(8,128)S(1)} %add_add_fusion.1), channel_id=1, source_target_pairs={{0,32},{32,0},{1,33},{33,1},{2,34},{34,2},{3,35},{35,3},{4,36},{36... | collective-permute-start | bytes 589832 | tf_op jit(solution)/shard_map/ppermute | solution.py:317
  70.2 11.5 %collective-permute-start.9 = (f32[64,768]{1,0:T(8,128)S(1)}, f32[64,768]{1,0:T(8,128)S(1)}, u32[]{:S(2)}, u32[]{:S(2)}) collective-permute-start(f32[64,768]{1,0:T(8,128)S(1)} %multiply_subtract_fusion.1.refs_0_), channel_id=1, source_target_pairs={{0,192},{64,128},{128,64},{192,0},{1,193},{65,129},{129,65},{193,1... | collective-permute-start | bytes 589832 | tf_op jit(solution)/shard_map/ppermute | solution.py:37
  70.7 10.9 %collective-permute-start.8 = (f32[64,768]{1,0:T(8,128)S(1)}, f32[64,768]{1,0:T(8,128)S(1)}, u32[]{:S(2)}, u32[]{:S(2)}) collective-permute-start(f32[64,768]{1,0:T(8,128)S(1)} %multiply_subtract_fusion.1.refs_0_), channel_id=1, source_target_pairs={{0,128},{64,192},{128,0},{192,64},{1,129},{65,193},{129,1},{193,65... | collective-permute-start | bytes 589832 | tf_op jit(solution)/shard_map/ppermute | solution.py:37
  71.6 10.1 %collective-permute-start.7 = (f32[64,768]{1,0:T(8,128)S(1)}, f32[64,768]{1,0:T(8,128)S(1)}, u32[]{:S(2)}, u32[]{:S(2)}) collective-permute-start(f32[64,768]{1,0:T(8,128)S(1)} %multiply_subtract_fusion.1.refs_0_), channel_id=1, source_target_pairs={{0,64},{64,0},{128,192},{192,128},{1,65},{65,1},{129,193},{193,129... | collective-permute-start | bytes 589832 | tf_op jit(solution)/shard_map/ppermute | solution.py:37
  93.3 26.4 %all-to-all-start.2 = ((f32[16,40,256]{2,1,0:T(8,128)}), f32[16,40,256]{2,1,0:T(8,128)S(1)}, u32[]{:S(2)}, u32[]{:S(2)}) async-start(f32[16,40,256]{2,1,0:T(8,128)} %bitcast.7), calls=%async_computation.2 | async-start | bytes 1310720 | tf_op jit(solution)/shard_map/all_to_all | solution.py:26
  99.8 11.3 %collective-permute-start.15 = (f32[64,168]{1,0:T(8,128)S(1)}, f32[64,168]{1,0:T(8,128)S(1)}, u32[]{:S(2)}, u32[]{:S(2)}) collective-permute-start(f32[64,168]{1,0:T(8,128)S(1)} %get-tuple-element.109), channel_id=1, source_target_pairs={{1,0},{2,1},{3,2},{4,3},{5,4},{6,5},{7,6},{8,7},{9,8},{10,9},{11,1... | collective-permute-start | bytes 129032 | tf_op jit(solution)/shard_map/ppermute | solution.py:43
  102.1 8.9 %collective-permute-start.16 = (f32[64,168]{1,0:T(8,128)S(1)}, f32[64,168]{1,0:T(8,128)S(1)}, u32[]{:S(2)}, u32[]{:S(2)}) collective-permute-start(f32[64,168]{1,0:T(8,128)S(1)} %get-tuple-element.110), channel_id=1, source_target_pairs={{0,1},{1,2},{2,3},{3,4},{4,5},{5,6},{6,7},{7,8},{8,9},{9,10},{10,1... | collective-permute-start | bytes 129032 | tf_op jit(solution)/shard_map/ppermute | solution.py:43
  107.1 7.0 %collective-permute-start.12 = (f32[64,768]{1,0:T(8,128)S(1)}, f32[64,768]{1,0:T(8,128)S(1)}, u32[]{:S(2)}, u32[]{:S(2)}) collective-permute-start(f32[64,768]{1,0:T(8,128)S(1)} %get-tuple-element.90), channel_id=1, source_target_pairs={{0,64},{64,0},{128,192},{192,128},{1,65},{65,1},{129,193},{193,129... | collective-permute-start | bytes 589832 | tf_op jit(solution)/shard_map/ppermute | solution.py:37
  107.2 9.6 %collective-permute-start.13 = (f32[64,768]{1,0:T(8,128)S(1)}, f32[64,768]{1,0:T(8,128)S(1)}, u32[]{:S(2)}, u32[]{:S(2)}) collective-permute-start(f32[64,768]{1,0:T(8,128)S(1)} %get-tuple-element.91), channel_id=1, source_target_pairs={{0,128},{64,192},{128,0},{192,64},{1,129},{65,193},{129,1},{193,65... | collective-permute-start | bytes 589832 | tf_op jit(solution)/shard_map/ppermute | solution.py:37
  109.1 10.2 %collective-permute-start.14 = (f32[64,768]{1,0:T(8,128)S(1)}, f32[64,768]{1,0:T(8,128)S(1)}, u32[]{:S(2)}, u32[]{:S(2)}) collective-permute-start(f32[64,768]{1,0:T(8,128)S(1)} %get-tuple-element.92), channel_id=1, source_target_pairs={{0,192},{64,128},{128,64},{192,0},{1,193},{65,129},{129,65},{193,1... | collective-permute-start | bytes 589832 | tf_op jit(solution)/shard_map/ppermute | solution.py:37
  120.7 28.6 %all-to-all-start.3 = ((f32[16,40,256]{2,1,0:T(8,128)}), f32[16,40,256]{2,1,0:T(8,128)S(1)}, u32[]{:S(2)}, u32[]{:S(2)}) async-start(f32[16,40,256]{2,1,0:T(8,128)} %broadcast_in_dim.33), calls=%async_computation.3 | async-start | bytes 1310720 | tf_op jit(solution)/shard_map/all_to_all | solution.py:31
  129.3 6.4 %collective-permute-start.17 = (f32[64,768]{1,0:T(8,128)S(1)}, f32[64,768]{1,0:T(8,128)S(1)}, u32[]{:S(2)}, u32[]{:S(2)}) collective-permute-start(f32[64,768]{1,0:T(8,128)S(1)} %add_add_fusion), channel_id=1, source_target_pairs={{0,32},{32,0},{1,33},{33,1},{2,34},{34,2},{3,35},{35,3},{4,36},{36... | collective-permute-start | bytes 589832 | tf_op jit(solution)/shard_map/ppermute | solution.py:317
  135.7 9.1 %collective-permute-start.20 = (f32[64,768]{1,0:T(8,128)S(1)}, f32[64,768]{1,0:T(8,128)S(1)}, u32[]{:S(2)}, u32[]{:S(2)}) collective-permute-start(f32[64,768]{1,0:T(8,128)S(1)} %multiply_subtract_fusion.refs_0_), channel_id=1, source_target_pairs={{0,192},{64,128},{128,64},{192,0},{1,193},{65,129},{129,65},{193,1... | collective-permute-start | bytes 589832 | tf_op jit(solution)/shard_map/ppermute | solution.py:37
  137.7 7.1 %collective-permute-start.19 = (f32[64,768]{1,0:T(8,128)S(1)}, f32[64,768]{1,0:T(8,128)S(1)}, u32[]{:S(2)}, u32[]{:S(2)}) collective-permute-start(f32[64,768]{1,0:T(8,128)S(1)} %multiply_subtract_fusion.refs_0_), channel_id=1, source_target_pairs={{0,128},{64,192},{128,0},{192,64},{1,129},{65,193},{129,1},{193,65... | collective-permute-start | bytes 589832 | tf_op jit(solution)/shard_map/ppermute | solution.py:37
  137.7 8.9 %collective-permute-start.18 = (f32[64,768]{1,0:T(8,128)S(1)}, f32[64,768]{1,0:T(8,128)S(1)}, u32[]{:S(2)}, u32[]{:S(2)}) collective-permute-start(f32[64,768]{1,0:T(8,128)S(1)} %multiply_subtract_fusion.refs_0_), channel_id=1, source_target_pairs={{0,64},{64,0},{128,192},{192,128},{1,65},{65,1},{129,193},{193,129... | collective-permute-start | bytes 589832 | tf_op jit(solution)/shard_map/ppermute | solution.py:37
  149.3 5.3 %collective-permute-start.21 = (f32[640,256]{1,0:T(8,128)S(1)}, f32[640,256]{1,0:T(8,128)S(1)}, u32[]{:S(2)}, u32[]{:S(2)}) collective-permute-start(f32[640,256]{1,0:T(8,128)S(1)} %bitcast.12), channel_id=1, source_target_pairs={{0,1},{1,0},{2,3},{3,2},{4,5},{5,4},{6,7},{7,6},{8,9},{9,8},{10,11... | collective-permute-start | bytes 1966088 | tf_op jit(solution)/shard_map/ppermute | solution.py:322
  (11 other events, 225.1 us)

commit v6 on v5

--- a/solution.py
+++ b/solution.py
@@ -16,7 +16,7 @@
 CORE = "core"
 TM = (*FAR, CORE)
 SWAP = ((0, 1), (1, 0))
-FIRST, LATER = 5, 2
+FIRST, LATER = 2, 2
 HIDDEN = 1e30
 BF16, F32 = jnp.bfloat16, jnp.float32
 
@@ -106,35 +106,35 @@
                 out[pl.ds(start, size), :] = piece[...].astype(out.dtype)
 
 
-def first_half(x_ref, f_ref, seen_ref, mask_ref, grad_ref, kept_ref, x_low_ref):
-    @pl.when(pl.program_id(0) == 0)
-    def _():
+def first_pass(place_ref, x_ref, f_ref, seen_ref, mask_ref, *refs):
+    halves, (*pieces, x_part_ref, x_low_ref, total_ref) = refs[:4], refs[4:]
+    i = pl.program_id(0)
+
+    @pl.when(i == 0)
+    def _():
+        size = x_part_ref.shape[0]
         x_low_ref[...] = x_ref[...].astype(BF16)
+        x_part_ref[...] = x_ref[pl.ds(pl.multiple_of(place_ref[1] * size, size), size), :]
 
     x_low = x_low_ref[...]
     f_low = f_ref[...].astype(BF16)
     keep = mask_ref[...] != 0
     seen = seen_ref[...].astype(F32)
     misfit = jnp.where(keep, dot(f_low, x_low) - seen, 0.0).astype(BF16)
-    kept_ref[...] = jnp.where(keep, seen, HIDDEN).astype(BF16)
-    grad_ref[...] = by_hours(misfit, x_low)
-    return by_rows(f_low, misfit)
-
-
-def first_theirs(_, x_ref, f_ref, seen_ref, mask_ref, grad_ref, kept_ref, total_ref, x_low_ref):
-    add_up(total_ref, first_half(x_ref, f_ref, seen_ref, mask_ref, grad_ref, kept_ref, x_low_ref))
-
-
-def first_mine(place_ref, x_ref, f_ref, seen_ref, mask_ref, start_ref, grad_ref, kept_ref, *refs):
-    *pieces, x_part_ref, x_low_ref, total_ref = refs
-    size = x_part_ref.shape[0]
-
-    @pl.when(pl.program_id(0) == 0)
-    def _():
-        x_part_ref[...] = x_ref[pl.ds(pl.multiple_of(place_ref[1] * size, size), size), :]
-
-    term = first_half(x_ref, f_ref, seen_ref, mask_ref, grad_ref, kept_ref, x_low_ref)
-    add_up(total_ref, term, start_ref)
+    kept = jnp.where(keep, seen, HIDDEN).astype(BF16)
+    grad = by_hours(misfit, x_low)
+
+    @pl.when(i < FIRST)
+    def _():
+        halves[0][...] = grad
+        halves[2][...] = kept
+
+    @pl.when(i >= FIRST)
+    def _():
+        halves[1][...] = grad
+        halves[3][...] = kept
+
+    add_up(total_ref, by_rows(f_low, misfit))
     share_out(place_ref[1], total_ref, pieces)
 
 
@@ -184,8 +184,12 @@
         "half": lambda i, p: (i, 0),
         "mine": lambda i, p: (p[0] * steps + i, 0),
         "theirs": lambda i, p: ((1 - p[0]) * steps + i, 0),
+        "both": lambda i, p: ((i // FIRST + 1 + p[0]) % 2 * FIRST + i % FIRST, 0),
+        "former": lambda i, p: (jnp.minimum(i, FIRST - 1), 0),
+        "latter": lambda i, p: (jnp.maximum(i - FIRST, 0), 0),
     }
     tiles = {"whole": 1, "half": steps, "mine": 2 * steps, "theirs": 2 * steps}
+    tiles.update(both=2 * FIRST, former=FIRST, latter=FIRST)
 
     def spec(kind, shape):
         if kind == "held":
@@ -253,27 +257,17 @@
     w_part = lax.dynamic_slice_in_dim(ar_weights, along * band, band, 1)
     for sweep in range(ITERS):
         if sweep == 0:
-            theirs, kept_theirs, start = half_pass(
-                first_theirs,
+            theirs, mine, kept_theirs, kept_mine, *parts, x_part = half_pass(
+                first_pass,
                 place,
-                [("whole", time_factors), ("theirs", series_factors), ("theirs", observed), ("theirs", mask)],
-                [grad, flags, total],
-                FIRST,
+                [("whole", time_factors), ("both", series_factors), ("both", observed), ("both", mask)],
+                [("former", grad[1]), ("latter", grad[1]), ("former", flags[1]), ("latter", flags[1]), *shares, shares[0]],
+                2 * FIRST,
                 58,
-                3,
-                [low_scratch],
+                6,
+                [low_scratch, total_scratch],
             )
             came = lax.ppermute(theirs, CORE, SWAP)
-            mine, kept_mine, *parts, x_part = half_pass(
-                first_mine,
-                place,
-                [("whole", time_factors), ("mine", series_factors), ("mine", observed), ("mine", mask), ("whole", start)],
-                [grad, flags, *shares, shares[0]],
-                FIRST,
-                58,
-                3,
-                [low_scratch, total_scratch],
-            )
         else:
             mine, start, x_low = half_pass(
                 later_mine,
@@ -306,11 +300,13 @@
             )
         mine = mine + came
         mine, parts, x_part = lax.optimization_barrier((mine, parts, x_part))
-        edges = edges_of(x_part)
         f_sum = scattered_sum(mine, FAR)
+        received = [traded(parts[k], "x", k) for k in range(1, peers)]
+        edge_x, received[0] = lax.optimization_barrier((x_part, received[0]))
+        edges = edges_of(edge_x)
         x_sum = parts[0]
-        for k in range(1, peers):
-            x_sum = x_sum + traded(parts[k], "x", k)
+        for part in received:
+            x_sum = x_sum + part
         lag = lag_terms(x_part, edges, w_part, first, last)
         f_part, x_sum, lag = lax.optimization_barrier((f_part, x_sum, lag))
         f_part = f_part - step_f * (f_sum + ridge_f * f_part)

time: 158 us -> 143 us (0.905)
  waiting for transfers between devices: 50.4 us -> 43.9 us
  Pallas kernels: 25 us -> 19.2 us
    ppermute x12, waiting for transfers between devices: 32.7 us -> 17.1 us  [traded(): return lax.ppermute(array, axis, [(i, i ^ bits) for i in range(length)])]
    ppermute x4, waiting for transfers between devices: 0.01 us -> 5.94 us  [passed_along(): return lax.ppermute(array, axis, pairs)]
    pallas_call x7 -> x6, Pallas kernels: 25 us -> 19.2 us  [half_pass(): pl.pallas_call(kernel, out_shape=[s for _, s in outs], grid_spec=pltpu.Pr...]
    all_to_all x2, starting transfers between devices: 17.3 us -> 12.1 us  [gathered(): parts = lax.all_to_all(parts, axis, 0, 0, tiled=True)]
    ppermute x4, starting transfers between devices: 14.4 us -> 18.5 us  [passed_along(): return lax.ppermute(array, axis, pairs)]
    all_to_all x2, waiting for transfers between devices: 4.62 us -> 7.4 us  [gathered(): parts = lax.all_to_all(parts, axis, 0, 0, tiled=True)]
    ppermute x2, waiting for transfers between devices: 12.4 us -> 10.1 us  [local(): x_sum = x_sum + lax.ppermute(x_sum, 'y_lo', SWAP)]
  transfers between devices with their start and end apart: 26 -> 26, of which waited for: 15 -> 18; matrix products, arithmetic and copies ran while one was open for 2% -> 2% of each run, Pallas kernels for 9% -> 4%
where the time goes in v6:
time: 143 us
  starting transfers between devices  70.6 us (49%)
  waiting for transfers between devices  43.9 us (31%)
  Pallas kernels  19.2 us (13%)
  other arithmetic  4.92 us (3%)
  local copies, waits for them, and re-layouts  3.15 us (2%)
    pallas_call x6, Pallas kernels, half_pass(): pl.pallas_call(kernel, out_shape=[s for _, s in outs], grid_spec=pltpu.Pr...  19.2 us
    ppermute x4, starting transfers between devices, passed_along(): return lax.ppermute(array, axis, pairs)  18.5 us
    ppermute x12, waiting for transfers between devices, traded(): return lax.ppermute(array, axis, [(i, i ^ bits) for i in range(length)])  17.1 us
    ppermute x12, starting transfers between devices, traded(): return lax.ppermute(array, axis, [(i, i ^ bits) for i in range(length)])  14.6 us
    all_to_all x2, starting transfers between devices, scattered_sum(): return lax.all_to_all(parts, axis, 0, 0, tiled=True).sum(axis=0)  14.4 us
    all_to_all x2, starting transfers between devices, gathered(): parts = lax.all_to_all(parts, axis, 0, 0, tiled=True)  12.1 us
    ppermute x2, waiting for transfers between devices, local(): x_sum = x_sum + lax.ppermute(x_sum, 'y_lo', SWAP)  10.1 us
    all_to_all x2, waiting for transfers between devices, gathered(): parts = lax.all_to_all(parts, axis, 0, 0, tiled=True)  7.4 us
  transfers between devices with their start and end apart: 26, of which 18 were waited for; matrix products, arithmetic and copies ran while one was open for 2% of the time, Pallas kernels for 4%

profile of v6, /device:TPU:1, one launch (start us, length us, event | category | flops | bytes accessed | tf_op | source)
XLA Modules:
  0.0 142.7 jit_solution(7611303972077167668)
XLA Ops:
  1.3 9.6 %first_pass.1 = (f32[640,256]{1,0:T(8,128)}, f32[640,256]{1,0:T(8,128)}, bf16[640,768]{1,0:T(8,128)(2,1)}, bf16[640,768]{1,0:T(8,128)(2,1)}, f32[64,768]{1,0:T(8...) custom-call(s32[2]{0:T(128)} %pad_add_fusion.place_ref._, ...), custom_call_target="tpu_custom_call" | custom-call | flops 1509949440 | bytes 12255232 | tf_op jit(solution)/shard_map/first_pass/pallas_call | solution.py:205
  10.9 3.3 %collective-permute-start = (f32[640,256]{1,0:T(8,128)}, f32[640,256]{1,0:T(8,128)S(1)}, u32[]{:S(2)}, u32[]{:S(2)}) collective-permute-start(f32[640,256]{1,0:T(8,128)} %get-tuple-element.60), channel_id=1, source_target_pairs={{0,1},{1,0},{2,3},{3,2},{4,5},{5,4},{6,7},{7,6},{8,9},{9,8},{10,11... | collective-permute-start | bytes 1966088 | tf_op jit(solution)/shard_map/ppermute | solution.py:270
  18.2 9.2 %all-to-all-start = ((f32[16,40,256]{2,1,0:T(8,128)}), f32[16,40,256]{2,1,0:T(8,128)S(1)}, u32[]{:S(2)}, u32[]{:S(2)}) async-start(f32[16,40,256]{2,1,0:T(8,128)} %bitcast.5), calls=%async_computation | async-start | bytes 1310720 | tf_op jit(solution)/shard_map/all_to_all | solution.py:26
  28.7 2.5 %collective-permute-start.2 = (f32[64,768]{1,0:T(8,128)S(1)}, f32[64,768]{1,0:T(8,128)S(1)}, u32[]{:S(2)}, u32[]{:S(2)}) collective-permute-start(f32[64,768]{1,0:T(8,128)S(1)} %copy-done.7), channel_id=1, source_target_pairs={{0,128},{64,192},{128,0},{192,64},{1,129},{65,193},{129,1},{193,65... | collective-permute-start | bytes 589832 | tf_op jit(solution)/shard_map/ppermute | solution.py:37
  33.3 4.6 %collective-permute-start.4 = (f32[64,168]{1,0:T(8,128)S(1)}, f32[64,168]{1,0:T(8,128)S(1)}, u32[]{:S(2)}, u32[]{:S(2)}) collective-permute-start(f32[64,168]{1,0:T(8,128)S(1)} %get-tuple-element.117), channel_id=1, source_target_pairs={{1,0},{2,1},{3,2},{4,3},{5,4},{6,5},{7,6},{8,7},{9,8},{10,9},{11,1... | collective-permute-start | bytes 129032 | tf_op jit(solution)/shard_map/ppermute | solution.py:43
  37.9 5.0 %collective-permute-start.5 = (f32[64,168]{1,0:T(8,128)S(1)}, f32[64,168]{1,0:T(8,128)S(1)}, u32[]{:S(2)}, u32[]{:S(2)}) collective-permute-start(f32[64,168]{1,0:T(8,128)S(1)} %get-tuple-element.118), channel_id=1, source_target_pairs={{0,1},{1,2},{2,3},{3,4},{4,5},{5,6},{6,7},{7,8},{8,9},{9,10},{10,1... | collective-permute-start | bytes 129032 | tf_op jit(solution)/shard_map/ppermute | solution.py:43
  43.4 2.3 %collective-permute-done.5 = f32[64,168]{1,0:T(8,128)S(1)} collective-permute-done((f32[64,168]{1,0:T(8,128)S(1)}, f32[64,168]{1,0:T(8,128)S(1)}, u32[]{:S(2)}, u32[]{:S(2)}) %collective-permute-start.5) | collective-permute-done | bytes 43040 | tf_op jit(solution)/shard_map/ppermute | solution.py:43
  48.3 6.1 %all-to-all-start.1 = ((f32[16,40,256]{2,1,0:T(8,128)}), f32[16,40,256]{2,1,0:T(8,128)S(1)}, u32[]{:S(2)}, u32[]{:S(2)}) async-start(f32[16,40,256]{2,1,0:T(8,128)} %broadcast_in_dim.32), calls=%async_computation.1 | async-start | bytes 1310720 | tf_op jit(solution)/shard_map/all_to_all | solution.py:31
  54.9 5.1 %collective-permute-done.6 = f32[64,768]{1,0:T(8,128)S(1)} collective-permute-done((f32[64,768]{1,0:T(8,128)S(1)}, f32[64,768]{1,0:T(8,128)S(1)}, u32[]{:S(2)}, u32[]{:S(2)}) %collective-permute-start.6) | collective-permute-done | bytes 196640 | tf_op jit(solution)/shard_map/ppermute | solution.py:313
  60.1 2.6 %collective-permute-start.9 = (f32[64,768]{1,0:T(8,128)S(1)}, f32[64,768]{1,0:T(8,128)S(1)}, u32[]{:S(2)}, u32[]{:S(2)}) collective-permute-start(f32[64,768]{1,0:T(8,128)S(1)} %multiply_subtract_fusion.1.refs_0_), channel_id=1, source_target_pairs={{0,192},{64,128},{128,64},{192,0},{1,193},{65,129},{129,65},{193,1... | collective-permute-start | bytes 589832 | tf_op jit(solution)/shard_map/ppermute | solution.py:37
  63.4 4.4 %collective-permute-done.9.refs_3_ = f32[64,768]{1,0:T(8,128)S(1)} collective-permute-done((f32[64,768]{1,0:T(8,128)S(1)}, f32[64,768]{1,0:T(8,128)S(1)}, u32[]{:S(2)}, u32[]{:S(2)}) %collective-permute-start.9) | collective-permute-done | bytes 196640 | tf_op jit(solution)/shard_map/ppermute | solution.py:37
  69.2 4.3 %all-to-all-done.1 = f32[16,40,256]{2,1,0:T(8,128)S(1)} async-done(((f32[16,40,256]{2,1,0:T(8,128)}), f32[16,40,256]{2,1,0:T(8,128)S(1)}, u32[]{:S(2)}, u32[]{:S(2)}) %all-to-all-start.1) | async-done | bytes 655392 | tf_op jit(solution)/shard_map/all_to_all | solution.py:31
  73.5 3.5 %collective-permute-start.10 = (f32[640,256]{1,0:T(8,128)S(1)}, f32[640,256]{1,0:T(8,128)S(1)}, u32[]{:S(2)}, u32[]{:S(2)}) collective-permute-start(f32[640,256]{1,0:T(8,128)S(1)} %bitcast.14), channel_id=1, source_target_pairs={{0,1},{1,0},{2,3},{3,2},{4,5},{5,4},{6,7},{7,6},{8,9},{9,8},{10,11... | collective-permute-start | bytes 1966088 | tf_op jit(solution)/shard_map/ppermute | solution.py:318
  83.9 5.2 %all-to-all-start.2 = ((f32[16,40,256]{2,1,0:T(8,128)}), f32[16,40,256]{2,1,0:T(8,128)S(1)}, u32[]{:S(2)}, u32[]{:S(2)}) async-start(f32[16,40,256]{2,1,0:T(8,128)} %bitcast.7), calls=%async_computation.2 | async-start | bytes 1310720 | tf_op jit(solution)/shard_map/all_to_all | solution.py:26
  90.3 2.4 %collective-permute-start.13 = (f32[64,768]{1,0:T(8,128)S(1)}, f32[64,768]{1,0:T(8,128)S(1)}, u32[]{:S(2)}, u32[]{:S(2)}) collective-permute-start(f32[64,768]{1,0:T(8,128)S(1)} %get-tuple-element.97), channel_id=1, source_target_pairs={{0,128},{64,192},{128,0},{192,64},{1,129},{65,193},{129,1},{193,65... | collective-permute-start | bytes 589832 | tf_op jit(solution)/shard_map/ppermute | solution.py:37
  95.3 4.0 %collective-permute-start.15 = (f32[64,168]{1,0:T(8,128)S(1)}, f32[64,168]{1,0:T(8,128)S(1)}, u32[]{:S(2)}, u32[]{:S(2)}) collective-permute-start(f32[64,168]{1,0:T(8,128)S(1)} %get-tuple-element.115), channel_id=1, source_target_pairs={{1,0},{2,1},{3,2},{4,3},{5,4},{6,5},{7,6},{8,7},{9,8},{10,9},{11,1... | collective-permute-start | bytes 129032 | tf_op jit(solution)/shard_map/ppermute | solution.py:43
  99.4 4.9 %collective-permute-start.16 = (f32[64,168]{1,0:T(8,128)S(1)}, f32[64,168]{1,0:T(8,128)S(1)}, u32[]{:S(2)}, u32[]{:S(2)}) collective-permute-start(f32[64,168]{1,0:T(8,128)S(1)} %get-tuple-element.116), channel_id=1, source_target_pairs={{0,1},{1,2},{2,3},{3,4},{4,5},{5,6},{6,7},{7,8},{8,9},{9,10},{10,1... | collective-permute-start | bytes 129032 | tf_op jit(solution)/shard_map/ppermute | solution.py:43
  104.5 3.0 %collective-permute-done.16 = f32[64,168]{1,0:T(8,128)S(1)} collective-permute-done((f32[64,168]{1,0:T(8,128)S(1)}, f32[64,168]{1,0:T(8,128)S(1)}, u32[]{:S(2)}, u32[]{:S(2)}) %collective-permute-start.16) | collective-permute-done | bytes 43040 | tf_op jit(solution)/shard_map/ppermute | solution.py:43
  110.1 6.0 %all-to-all-start.3 = ((f32[16,40,256]{2,1,0:T(8,128)}), f32[16,40,256]{2,1,0:T(8,128)S(1)}, u32[]{:S(2)}, u32[]{:S(2)}) async-start(f32[16,40,256]{2,1,0:T(8,128)} %broadcast_in_dim.33), calls=%async_computation.3 | async-start | bytes 1310720 | tf_op jit(solution)/shard_map/all_to_all | solution.py:31
  117.0 5.0 %collective-permute-done.17 = f32[64,768]{1,0:T(8,128)S(1)} collective-permute-done((f32[64,768]{1,0:T(8,128)S(1)}, f32[64,768]{1,0:T(8,128)S(1)}, u32[]{:S(2)}, u32[]{:S(2)}) %collective-permute-start.17) | collective-permute-done | bytes 196640 | tf_op jit(solution)/shard_map/ppermute | solution.py:313
  122.1 2.5 %collective-permute-start.20 = (f32[64,768]{1,0:T(8,128)S(1)}, f32[64,768]{1,0:T(8,128)S(1)}, u32[]{:S(2)}, u32[]{:S(2)}) collective-permute-start(f32[64,768]{1,0:T(8,128)S(1)} %multiply_subtract_fusion.refs_0_), channel_id=1, source_target_pairs={{0,192},{64,128},{128,64},{192,0},{1,193},{65,129},{129,65},{193,1... | collective-permute-start | bytes 589832 | tf_op jit(solution)/shard_map/ppermute | solution.py:37
  125.4 7.2 %collective-permute-done.20.refs_3_ = f32[64,768]{1,0:T(8,128)S(1)} collective-permute-done((f32[64,768]{1,0:T(8,128)S(1)}, f32[64,768]{1,0:T(8,128)S(1)}, u32[]{:S(2)}, u32[]{:S(2)}) %collective-permute-start.20) | collective-permute-done | bytes 196640 | tf_op jit(solution)/shard_map/ppermute | solution.py:37
  132.6 3.1 %all-to-all-done.3 = f32[16,40,256]{2,1,0:T(8,128)S(1)} async-done(((f32[16,40,256]{2,1,0:T(8,128)}), f32[16,40,256]{2,1,0:T(8,128)S(1)}, u32[]{:S(2)}, u32[]{:S(2)}) %all-to-all-start.3) | async-done | bytes 655392 | tf_op jit(solution)/shard_map/all_to_all | solution.py:31
  135.7 2.7 %collective-permute-start.21 = (f32[640,256]{1,0:T(8,128)S(1)}, f32[640,256]{1,0:T(8,128)S(1)}, u32[]{:S(2)}, u32[]{:S(2)}) collective-permute-start(f32[640,256]{1,0:T(8,128)S(1)} %bitcast.12), channel_id=1, source_target_pairs={{0,1},{1,0},{2,3},{3,2},{4,5},{5,4},{6,7},{7,6},{8,9},{9,8},{10,11... | collective-permute-start | bytes 1966088 | tf_op jit(solution)/shard_map/ppermute | solution.py:318
  (77 shorter events, 33.3 us)
Async XLA Ops:
  10.9 5.3 %collective-permute-start = (f32[640,256]{1,0:T(8,128)}, f32[640,256]{1,0:T(8,128)S(1)}, u32[]{:S(2)}, u32[]{:S(2)}) collective-permute-start(f32[640,256]{1,0:T(8,128)} %get-tuple-element.60), channel_id=1, source_target_pairs={{0,1},{1,0},{2,3},{3,2},{4,5},{5,4},{6,7},{7,6},{8,9},{9,8},{10,11... | collective-permute-start | bytes 1966088 | tf_op jit(solution)/shard_map/ppermute | solution.py:270
  18.2 29.2 %all-to-all-start = ((f32[16,40,256]{2,1,0:T(8,128)}), f32[16,40,256]{2,1,0:T(8,128)S(1)}, u32[]{:S(2)}, u32[]{:S(2)}) async-start(f32[16,40,256]{2,1,0:T(8,128)} %bitcast.5), calls=%async_computation | async-start | bytes 1310720 | tf_op jit(solution)/shard_map/all_to_all | solution.py:26
  27.4 5.9 %collective-permute-start.1 = (f32[64,768]{1,0:T(8,128)S(1)}, f32[64,768]{1,0:T(8,128)S(1)}, u32[]{:S(2)}, u32[]{:S(2)}) collective-permute-start(f32[64,768]{1,0:T(8,128)S(1)} %copy-done.8), channel_id=1, source_target_pairs={{0,64},{64,0},{128,192},{192,128},{1,65},{65,1},{129,193},{193,129... | collective-permute-start | bytes 589832 | tf_op jit(solution)/shard_map/ppermute | solution.py:37
  28.7 14.2 %collective-permute-start.2 = (f32[64,768]{1,0:T(8,128)S(1)}, f32[64,768]{1,0:T(8,128)S(1)}, u32[]{:S(2)}, u32[]{:S(2)}) collective-permute-start(f32[64,768]{1,0:T(8,128)S(1)} %copy-done.7), channel_id=1, source_target_pairs={{0,128},{64,192},{128,0},{192,64},{1,129},{65,193},{129,1},{193,65... | collective-permute-start | bytes 589832 | tf_op jit(solution)/shard_map/ppermute | solution.py:37
  31.1 11.8 %collective-permute-start.3 = (f32[64,768]{1,0:T(8,128)S(1)}, f32[64,768]{1,0:T(8,128)S(1)}, u32[]{:S(2)}, u32[]{:S(2)}) collective-permute-start(f32[64,768]{1,0:T(8,128)S(1)} %copy-done.6), channel_id=1, source_target_pairs={{0,192},{64,128},{128,64},{192,0},{1,193},{65,129},{129,65},{193,1... | collective-permute-start | bytes 589832 | tf_op jit(solution)/shard_map/ppermute | solution.py:37
  33.3 10.1 %collective-permute-start.4 = (f32[64,168]{1,0:T(8,128)S(1)}, f32[64,168]{1,0:T(8,128)S(1)}, u32[]{:S(2)}, u32[]{:S(2)}) collective-permute-start(f32[64,168]{1,0:T(8,128)S(1)} %get-tuple-element.117), channel_id=1, source_target_pairs={{1,0},{2,1},{3,2},{4,3},{5,4},{6,5},{7,6},{8,7},{9,8},{10,9},{11,1... | collective-permute-start | bytes 129032 | tf_op jit(solution)/shard_map/ppermute | solution.py:43
  37.9 7.9 %collective-permute-start.5 = (f32[64,168]{1,0:T(8,128)S(1)}, f32[64,168]{1,0:T(8,128)S(1)}, u32[]{:S(2)}, u32[]{:S(2)}) collective-permute-start(f32[64,168]{1,0:T(8,128)S(1)} %get-tuple-element.118), channel_id=1, source_target_pairs={{0,1},{1,2},{2,3},{3,4},{4,5},{5,6},{6,7},{7,8},{8,9},{9,10},{10,1... | collective-permute-start | bytes 129032 | tf_op jit(solution)/shard_map/ppermute | solution.py:43
  48.3 25.2 %all-to-all-start.1 = ((f32[16,40,256]{2,1,0:T(8,128)}), f32[16,40,256]{2,1,0:T(8,128)S(1)}, u32[]{:S(2)}, u32[]{:S(2)}) async-start(f32[16,40,256]{2,1,0:T(8,128)} %broadcast_in_dim.32), calls=%async_computation.1 | async-start | bytes 1310720 | tf_op jit(solution)/shard_map/all_to_all | solution.py:31
  54.4 5.6 %collective-permute-start.6 = (f32[64,768]{1,0:T(8,128)S(1)}, f32[64,768]{1,0:T(8,128)S(1)}, u32[]{:S(2)}, u32[]{:S(2)}) collective-permute-start(f32[64,768]{1,0:T(8,128)S(1)} %add_add_fusion.1), channel_id=1, source_target_pairs={{0,32},{32,0},{1,33},{33,1},{2,34},{34,2},{3,35},{35,3},{4,36},{36... | collective-permute-start | bytes 589832 | tf_op jit(solution)/shard_map/ppermute | solution.py:313
  60.1 7.7 %collective-permute-start.9 = (f32[64,768]{1,0:T(8,128)S(1)}, f32[64,768]{1,0:T(8,128)S(1)}, u32[]{:S(2)}, u32[]{:S(2)}) collective-permute-start(f32[64,768]{1,0:T(8,128)S(1)} %multiply_subtract_fusion.1.refs_0_), channel_id=1, source_target_pairs={{0,192},{64,128},{128,64},{192,0},{1,193},{65,129},{129,65},{193,1... | collective-permute-start | bytes 589832 | tf_op jit(solution)/shard_map/ppermute | solution.py:37
  62.7 6.3 %collective-permute-start.8 = (f32[64,768]{1,0:T(8,128)S(1)}, f32[64,768]{1,0:T(8,128)S(1)}, u32[]{:S(2)}, u32[]{:S(2)}) collective-permute-start(f32[64,768]{1,0:T(8,128)S(1)} %multiply_subtract_fusion.1.refs_0_), channel_id=1, source_target_pairs={{0,128},{64,192},{128,0},{192,64},{1,129},{65,193},{129,1},{193,65... | collective-permute-start | bytes 589832 | tf_op jit(solution)/shard_map/ppermute | solution.py:37
  63.2 6.0 %collective-permute-start.7 = (f32[64,768]{1,0:T(8,128)S(1)}, f32[64,768]{1,0:T(8,128)S(1)}, u32[]{:S(2)}, u32[]{:S(2)}) collective-permute-start(f32[64,768]{1,0:T(8,128)S(1)} %multiply_subtract_fusion.1.refs_0_), channel_id=1, source_target_pairs={{0,64},{64,0},{128,192},{192,128},{1,65},{65,1},{129,193},{193,129... | collective-permute-start | bytes 589832 | tf_op jit(solution)/shard_map/ppermute | solution.py:37
  73.5 5.6 %collective-permute-start.10 = (f32[640,256]{1,0:T(8,128)S(1)}, f32[640,256]{1,0:T(8,128)S(1)}, u32[]{:S(2)}, u32[]{:S(2)}) collective-permute-start(f32[640,256]{1,0:T(8,128)S(1)} %bitcast.14), channel_id=1, source_target_pairs={{0,1},{1,0},{2,3},{3,2},{4,5},{5,4},{6,7},{7,6},{8,9},{9,8},{10,11... | collective-permute-start | bytes 1966088 | tf_op jit(solution)/shard_map/ppermute | solution.py:318
  83.9 25.3 %all-to-all-start.2 = ((f32[16,40,256]{2,1,0:T(8,128)}), f32[16,40,256]{2,1,0:T(8,128)S(1)}, u32[]{:S(2)}, u32[]{:S(2)}) async-start(f32[16,40,256]{2,1,0:T(8,128)} %bitcast.7), calls=%async_computation.2 | async-start | bytes 1310720 | tf_op jit(solution)/shard_map/all_to_all | solution.py:26
  89.1 6.1 %collective-permute-start.12 = (f32[64,768]{1,0:T(8,128)S(1)}, f32[64,768]{1,0:T(8,128)S(1)}, u32[]{:S(2)}, u32[]{:S(2)}) collective-permute-start(f32[64,768]{1,0:T(8,128)S(1)} %get-tuple-element.95), channel_id=1, source_target_pairs={{0,64},{64,0},{128,192},{192,128},{1,65},{65,1},{129,193},{193,129... | collective-permute-start | bytes 589832 | tf_op jit(solution)/shard_map/ppermute | solution.py:37
  90.3 13.9 %collective-permute-start.13 = (f32[64,768]{1,0:T(8,128)S(1)}, f32[64,768]{1,0:T(8,128)S(1)}, u32[]{:S(2)}, u32[]{:S(2)}) collective-permute-start(f32[64,768]{1,0:T(8,128)S(1)} %get-tuple-element.97), channel_id=1, source_target_pairs={{0,128},{64,192},{128,0},{192,64},{1,129},{65,193},{129,1},{193,65... | collective-permute-start | bytes 589832 | tf_op jit(solution)/shard_map/ppermute | solution.py:37
  92.7 11.5 %collective-permute-start.14 = (f32[64,768]{1,0:T(8,128)S(1)}, f32[64,768]{1,0:T(8,128)S(1)}, u32[]{:S(2)}, u32[]{:S(2)}) collective-permute-start(f32[64,768]{1,0:T(8,128)S(1)} %get-tuple-element.98), channel_id=1, source_target_pairs={{0,192},{64,128},{128,64},{192,0},{1,193},{65,129},{129,65},{193,1... | collective-permute-start | bytes 589832 | tf_op jit(solution)/shard_map/ppermute | solution.py:37
  95.3 9.2 %collective-permute-start.15 = (f32[64,168]{1,0:T(8,128)S(1)}, f32[64,168]{1,0:T(8,128)S(1)}, u32[]{:S(2)}, u32[]{:S(2)}) collective-permute-start(f32[64,168]{1,0:T(8,128)S(1)} %get-tuple-element.115), channel_id=1, source_target_pairs={{1,0},{2,1},{3,2},{4,3},{5,4},{6,5},{7,6},{8,7},{9,8},{10,9},{11,1... | collective-permute-start | bytes 129032 | tf_op jit(solution)/shard_map/ppermute | solution.py:43
  99.4 8.2 %collective-permute-start.16 = (f32[64,168]{1,0:T(8,128)S(1)}, f32[64,168]{1,0:T(8,128)S(1)}, u32[]{:S(2)}, u32[]{:S(2)}) collective-permute-start(f32[64,168]{1,0:T(8,128)S(1)} %get-tuple-element.116), channel_id=1, source_target_pairs={{0,1},{1,2},{2,3},{3,4},{4,5},{5,6},{6,7},{7,8},{8,9},{9,10},{10,1... | collective-permute-start | bytes 129032 | tf_op jit(solution)/shard_map/ppermute | solution.py:43
  110.1 25.6 %all-to-all-start.3 = ((f32[16,40,256]{2,1,0:T(8,128)}), f32[16,40,256]{2,1,0:T(8,128)S(1)}, u32[]{:S(2)}, u32[]{:S(2)}) async-start(f32[16,40,256]{2,1,0:T(8,128)} %broadcast_in_dim.33), calls=%async_computation.3 | async-start | bytes 1310720 | tf_op jit(solution)/shard_map/all_to_all | solution.py:31
  116.1 5.9 %collective-permute-start.17 = (f32[64,768]{1,0:T(8,128)S(1)}, f32[64,768]{1,0:T(8,128)S(1)}, u32[]{:S(2)}, u32[]{:S(2)}) collective-permute-start(f32[64,768]{1,0:T(8,128)S(1)} %add_add_fusion), channel_id=1, source_target_pairs={{0,32},{32,0},{1,33},{33,1},{2,34},{34,2},{3,35},{35,3},{4,36},{36... | collective-permute-start | bytes 589832 | tf_op jit(solution)/shard_map/ppermute | solution.py:313
  122.1 10.5 %collective-permute-start.20 = (f32[64,768]{1,0:T(8,128)S(1)}, f32[64,768]{1,0:T(8,128)S(1)}, u32[]{:S(2)}, u32[]{:S(2)}) collective-permute-start(f32[64,768]{1,0:T(8,128)S(1)} %multiply_subtract_fusion.refs_0_), channel_id=1, source_target_pairs={{0,192},{64,128},{128,64},{192,0},{1,193},{65,129},{129,65},{193,1... | collective-permute-start | bytes 589832 | tf_op jit(solution)/shard_map/ppermute | solution.py:37
  124.5 8.0 %collective-permute-start.19 = (f32[64,768]{1,0:T(8,128)S(1)}, f32[64,768]{1,0:T(8,128)S(1)}, u32[]{:S(2)}, u32[]{:S(2)}) collective-permute-start(f32[64,768]{1,0:T(8,128)S(1)} %multiply_subtract_fusion.refs_0_), channel_id=1, source_target_pairs={{0,128},{64,192},{128,0},{192,64},{1,129},{65,193},{129,1},{193,65... | collective-permute-start | bytes 589832 | tf_op jit(solution)/shard_map/ppermute | solution.py:37
  125.0 7.5 %collective-permute-start.18 = (f32[64,768]{1,0:T(8,128)S(1)}, f32[64,768]{1,0:T(8,128)S(1)}, u32[]{:S(2)}, u32[]{:S(2)}) collective-permute-start(f32[64,768]{1,0:T(8,128)S(1)} %multiply_subtract_fusion.refs_0_), channel_id=1, source_target_pairs={{0,64},{64,0},{128,192},{192,128},{1,65},{65,1},{129,193},{193,129... | collective-permute-start | bytes 589832 | tf_op jit(solution)/shard_map/ppermute | solution.py:37
  (11 other events, 215.7 us)

commit v7 on v6

--- a/solution.py
+++ b/solution.py
@@ -16,7 +16,7 @@
 CORE = "core"
 TM = (*FAR, CORE)
 SWAP = ((0, 1), (1, 0))
-FIRST, LATER = 2, 2
+FIRST, LATER, LAST = 2, 1, 2
 HIDDEN = 1e30
 BF16, F32 = jnp.bfloat16, jnp.float32
 
@@ -78,13 +78,8 @@
 
 
 def add_up(total_ref, term, start_ref=None):
-    @pl.when(pl.program_id(0) == 0)
-    def _():
-        total_ref[...] = term if start_ref is None else start_ref[...] + term
-
-    @pl.when(pl.program_id(0) > 0)
-    def _():
-        total_ref[...] += term
+    start = 0.0 if start_ref is None else start_ref[...]
+    total_ref[...] = jnp.where(pl.program_id(0) == 0, start, total_ref[...]) + term
 
 
 def share_out(along, total_ref, pieces):
@@ -107,34 +102,30 @@
 
 
 def first_pass(place_ref, x_ref, f_ref, seen_ref, mask_ref, *refs):
-    halves, (*pieces, x_part_ref, x_low_ref, total_ref) = refs[:4], refs[4:]
+    theirs_ref, mine_ref, kept_ref, *pieces, x_low_ref, total_ref = refs
     i = pl.program_id(0)
 
     @pl.when(i == 0)
     def _():
-        size = x_part_ref.shape[0]
         x_low_ref[...] = x_ref[...].astype(BF16)
-        x_part_ref[...] = x_ref[pl.ds(pl.multiple_of(place_ref[1] * size, size), size), :]
 
     x_low = x_low_ref[...]
     f_low = f_ref[...].astype(BF16)
     keep = mask_ref[...] != 0
     seen = seen_ref[...].astype(F32)
     misfit = jnp.where(keep, dot(f_low, x_low) - seen, 0.0).astype(BF16)
-    kept = jnp.where(keep, seen, HIDDEN).astype(BF16)
+    kept_ref[...] = jnp.where(keep, seen, HIDDEN).astype(BF16)
     grad = by_hours(misfit, x_low)
+    add_up(total_ref, by_rows(f_low, misfit))
 
     @pl.when(i < FIRST)
     def _():
-        halves[0][...] = grad
-        halves[2][...] = kept
+        theirs_ref[...] = grad
 
     @pl.when(i >= FIRST)
     def _():
-        halves[1][...] = grad
-        halves[3][...] = kept
-
-    add_up(total_ref, by_rows(f_low, misfit))
+        mine_ref[...] = grad
+
     share_out(place_ref[1], total_ref, pieces)
 
 
@@ -143,9 +134,17 @@
     return jnp.where(kept < HIDDEN / 2, dot(f_low, x_low) - kept, 0.0).astype(BF16)
 
 
-def later_mine(place_ref, *refs):
-    *came, f_ref, kept_ref, grad_ref, total_ref, x_low_ref = refs
+def placed(place_ref, *refs):
+    *came, x_ref, x_low_ref = refs
+    assembled(place_ref[1], came, x_ref, x_low_ref)
+
+
+def placed_low(place_ref, *refs):
+    *came, x_low_ref = refs
     assembled(place_ref[1], came, x_low_ref)
+
+
+def later_mine(_, x_low_ref, f_ref, kept_ref, grad_ref, total_ref):
     x_low = x_low_ref[...]
     f_low = f_ref[...].astype(BF16)
     misfit = misfit_of(f_low, x_low, kept_ref)
@@ -166,9 +165,7 @@
     share_out(place_ref[1], total_ref, pieces)
 
 
-def last_mine(place_ref, *refs):
-    *came, f_ref, f_out_ref, imputed_ref, x_out_ref, x_low_ref = refs
-    assembled(place_ref[1], came, x_out_ref, x_low_ref)
+def last_mine(_, x_low_ref, f_ref, f_out_ref, imputed_ref):
     f_out_ref[...] = f_ref[...]
     imputed_ref[...] = dot(f_ref[...].astype(BF16), x_low_ref[...]).astype(BF16)
 
@@ -185,11 +182,15 @@
         "mine": lambda i, p: (p[0] * steps + i, 0),
         "theirs": lambda i, p: ((1 - p[0]) * steps + i, 0),
         "both": lambda i, p: ((i // FIRST + 1 + p[0]) % 2 * FIRST + i % FIRST, 0),
+        "all": lambda i, p: (i, 0),
+        "lower": lambda i, p: (i, 0),
+        "upper": lambda i, p: (steps + i, 0),
         "former": lambda i, p: (jnp.minimum(i, FIRST - 1), 0),
         "latter": lambda i, p: (jnp.maximum(i - FIRST, 0), 0),
     }
     tiles = {"whole": 1, "half": steps, "mine": 2 * steps, "theirs": 2 * steps}
-    tiles.update(both=2 * FIRST, former=FIRST, latter=FIRST)
+    tiles.update(both=2 * FIRST, former=FIRST, latter=FIRST, all=steps)
+    tiles.update(lower=2 * steps, upper=2 * steps)
 
     def spec(kind, shape):
         if kind == "held":
@@ -197,7 +198,7 @@
         return pl.BlockSpec((shape[0] // tiles[kind], shape[1]), maps[kind])
 
     moved = sum(
-        a.size * a.dtype.itemsize // (2 if k in ("mine", "theirs") else 1)
+        a.size * a.dtype.itemsize // (2 if k in ("mine", "theirs", "lower", "upper") else 1)
         for k, a in [*ins, *outs]
         if k != "held"
     )
@@ -254,14 +255,15 @@
     total_scratch = pltpu.VMEM((rank, hours), F32)
     low_scratch = pltpu.VMEM((rank, hours), BF16)
     f_part = lax.dynamic_slice_in_dim(series_factors, own_row, line, 0)
+    x_part = lax.dynamic_slice_in_dim(time_factors, along * band, band, 0)
     w_part = lax.dynamic_slice_in_dim(ar_weights, along * band, band, 1)
     for sweep in range(ITERS):
         if sweep == 0:
-            theirs, mine, kept_theirs, kept_mine, *parts, x_part = half_pass(
+            theirs, mine, kept, *parts = half_pass(
                 first_pass,
                 place,
                 [("whole", time_factors), ("both", series_factors), ("both", observed), ("both", mask)],
-                [("former", grad[1]), ("latter", grad[1]), ("former", flags[1]), ("latter", flags[1]), *shares, shares[0]],
+                [("former", grad[1]), ("latter", grad[1]), ("all", shape(rows, hours, BF16)), *shares],
                 2 * FIRST,
                 58,
                 6,
@@ -269,19 +271,20 @@
             )
             came = lax.ppermute(theirs, CORE, SWAP)
         else:
-            mine, start, x_low = half_pass(
+            mine, start = half_pass(
                 later_mine,
                 place,
-                [*[("whole", p) for p in pieces], ("half", f_mine), ("half", kept_mine)],
-                [grad, total, low],
+                [("whole", x_low), ("half", f_mine), ("upper", kept)],
+                [grad, total],
                 LATER,
                 16,
                 3,
             )
+            f_theirs, mine, start = lax.optimization_barrier((f_theirs, mine, start))
             theirs, misfit = half_pass(
                 later_theirs,
                 place,
-                [("whole", x_low), ("half", f_theirs), ("half", kept_theirs)],
+                [("whole", x_low), ("half", f_theirs), ("lower", kept)],
                 [grad, flags],
                 LATER,
                 16,
@@ -314,14 +317,23 @@
         x_part = x_part - step_x * (x_sum + ridge_x * x_part + lam * lag)
         f_mine = gathered(f_part, FAR)
         pieces = [x_part] + [traded(x_part, "x", k) for k in range(1, peers)]
-        f_mine, pieces = lax.optimization_barrier((f_mine, pieces))
+        *x_full, x_low = half_pass(
+            placed if sweep + 1 == ITERS else placed_low,
+            place,
+            [("whole", p) for p in pieces],
+            [total, low] if sweep + 1 == ITERS else [low],
+            1,
+            8,
+            0,
+        )
+        f_mine, x_low = lax.optimization_barrier((f_mine, x_low))
         f_theirs = lax.ppermute(f_mine, CORE, SWAP)
-    f_out, imputed, x_out, x_low = half_pass(
+    f_out, imputed = half_pass(
         last_mine,
         place,
-        [*[("whole", p) for p in pieces], ("half", f_mine)],
-        [("mine", shape(rows, rank)), ("mine", shape(rows, hours, BF16)), total, low],
-        LATER,
+        [("whole", x_low), ("half", f_mine)],
+        [("mine", shape(rows, rank)), ("mine", shape(rows, hours, BF16))],
+        LAST,
         16,
         1,
     )
@@ -330,12 +342,12 @@
         place,
         [("whole", x_low), ("half", f_theirs), ("held", f_out), ("held", imputed)],
         [("theirs", shape(rows, rank)), ("theirs", shape(rows, hours, BF16))],
-        LATER,
+        LAST,
         16,
         1,
         aliases={3: 0, 4: 1},
     )
-    return f_out, x_out, imputed
+    return f_out, x_full[0], imputed
 
 
 def solution(mesh):

time: 143 us -> 142 us (level)
  waiting for transfers between devices: 43.9 us -> 40.4 us
  starting transfers between devices: 70.6 us -> 72.4 us
    ppermute x12, waiting for transfers between devices: 17.1 us -> 15.5 us  [traded(): return lax.ppermute(array, axis, [(i, i ^ bits) for i in range(length)])]
    pallas_call x6 -> x8, Pallas kernels: 19.2 us -> 18.2 us  [half_pass(): pl.pallas_call(kernel, out_shape=[s for _, s in outs], grid_spec=pltpu.Pr...]
  transfers between devices with their start and end apart: 26 -> 26, of which waited for: 18 -> 21; matrix products, arithmetic and copies ran while one was open for 2% -> 3% of each run, Pallas kernels for 4% -> 5%
where the time goes in v7:
time: 142 us; the launch traced here: 141 us
  starting transfers between devices  72.4 us (51%)
  waiting for transfers between devices  40.4 us (28%)
  Pallas kernels  18.2 us (13%)
  other arithmetic  4.89 us (3%)
  local copies, waits for them, and re-layouts  4.12 us (3%)
    ppermute x4, starting transfers between devices, passed_along(): return lax.ppermute(array, axis, pairs)  19 us
    pallas_call x8, Pallas kernels, half_pass(): pl.pallas_call(kernel, out_shape=[s for _, s in outs], grid_spec=pltpu.Pr...  18.2 us
    ppermute x12, waiting for transfers between devices, traded(): return lax.ppermute(array, axis, [(i, i ^ bits) for i in range(length)])  15.5 us
    all_to_all x2, starting transfers between devices, scattered_sum(): return lax.all_to_all(parts, axis, 0, 0, tiled=True).sum(axis=0)  15.1 us
    ppermute x12, starting transfers between devices, traded(): return lax.ppermute(array, axis, [(i, i ^ bits) for i in range(length)])  14.6 us
    all_to_all x2, starting transfers between devices, gathered(): parts = lax.all_to_all(parts, axis, 0, 0, tiled=True)  12.2 us
    ppermute x2, waiting for transfers between devices, local(): x_sum = x_sum + lax.ppermute(x_sum, 'y_lo', SWAP)  9.98 us
    all_to_all x2, waiting for transfers between devices, gathered(): parts = lax.all_to_all(parts, axis, 0, 0, tiled=True)  6.7 us
  transfers between devices with their start and end apart: 26, of which 21 were waited for; matrix products, arithmetic and copies ran while one was open for 3% of the time, Pallas kernels for 5%

profile of v7, /device:TPU:1, one launch (start us, length us, event | category | flops | bytes accessed | tf_op | source)
XLA Modules:
  0.0 140.9 jit_solution(8946676203619999986)
XLA Ops:
  1.3 7.9 %first_pass.1 = (f32[640,256]{1,0:T(8,128)}, f32[640,256]{1,0:T(8,128)}, bf16[1280,768]{1,0:T(8,128)(2,1)}, f32[64,768]{1,0:T(8,128)}, f32[64,768]{1,0:T(8,128)}, /*index=5*/f32[64,768]{1,0:T(8,128)}, f32[64,768]{1,0:T(8,128)}) custom-call(s32[2]{0:T(128)} %pad_add_fusion.place_ref._, f32[256,768]{1,0:T(8,128)} %x_ref.1, f32[1280,256]{1,0:T(8,128)} %f_ref.1, ...), custom_call_target="tpu_custom_call" | custom-call | flops 1509949440 | bytes 12058624 | tf_op jit(solution)/shard_map/first_pass/pallas_call | solution.py:206
  9.2 3.3 %collective-permute-start = (f32[640,256]{1,0:T(8,128)}, f32[640,256]{1,0:T(8,128)S(1)}, u32[]{:S(2)}, u32[]{:S(2)}) collective-permute-start(f32[640,256]{1,0:T(8,128)} %get-tuple-element.54), channel_id=1, source_target_pairs={{0,1},{1,0},{2,3},{3,2},{4,5},{5,4},{6,7},{7,6},{8,9},{9,8},{10,11... | collective-permute-start | bytes 1966088 | tf_op jit(solution)/shard_map/ppermute | solution.py:272
  16.5 9.2 %all-to-all-start = ((f32[16,40,256]{2,1,0:T(8,128)}), f32[16,40,256]{2,1,0:T(8,128)S(1)}, u32[]{:S(2)}, u32[]{:S(2)}) async-start(f32[16,40,256]{2,1,0:T(8,128)} %bitcast.5), calls=%async_computation | async-start | bytes 1310720 | tf_op jit(solution)/shard_map/all_to_all | solution.py:26
  27.0 2.5 %collective-permute-start.2 = (f32[64,768]{1,0:T(8,128)S(1)}, f32[64,768]{1,0:T(8,128)S(1)}, u32[]{:S(2)}, u32[]{:S(2)}) collective-permute-start(f32[64,768]{1,0:T(8,128)S(1)} %copy-done.5), channel_id=1, source_target_pairs={{0,128},{64,192},{128,0},{192,64},{1,129},{65,193},{129,1},{193,65... | collective-permute-start | bytes 589832 | tf_op jit(solution)/shard_map/ppermute | solution.py:37
  31.7 4.6 %collective-permute-start.4 = (f32[64,168]{1,0:T(8,128)S(1)}, f32[64,168]{1,0:T(8,128)S(1)}, u32[]{:S(2)}, u32[]{:S(2)}) collective-permute-start(f32[64,168]{1,0:T(8,128)S(1)} %get-tuple-element.105), channel_id=1, source_target_pairs={{1,0},{2,1},{3,2},{4,3},{5,4},{6,5},{7,6},{8,7},{9,8},{10,9},{11,1... | collective-permute-start | bytes 129032 | tf_op jit(solution)/shard_map/ppermute | solution.py:43
  36.2 5.0 %collective-permute-start.5 = (f32[64,168]{1,0:T(8,128)S(1)}, f32[64,168]{1,0:T(8,128)S(1)}, u32[]{:S(2)}, u32[]{:S(2)}) collective-permute-start(f32[64,168]{1,0:T(8,128)S(1)} %get-tuple-element.106), channel_id=1, source_target_pairs={{0,1},{1,2},{2,3},{3,4},{4,5},{5,6},{6,7},{7,8},{8,9},{9,10},{10,1... | collective-permute-start | bytes 129032 | tf_op jit(solution)/shard_map/ppermute | solution.py:43
  41.8 2.3 %collective-permute-done.5 = f32[64,168]{1,0:T(8,128)S(1)} collective-permute-done((f32[64,168]{1,0:T(8,128)S(1)}, f32[64,168]{1,0:T(8,128)S(1)}, u32[]{:S(2)}, u32[]{:S(2)}) %collective-permute-start.5) | collective-permute-done | bytes 43040 | tf_op jit(solution)/shard_map/ppermute | solution.py:43
  46.6 6.1 %all-to-all-start.1 = ((f32[16,40,256]{2,1,0:T(8,128)}), f32[16,40,256]{2,1,0:T(8,128)S(1)}, u32[]{:S(2)}, u32[]{:S(2)}) async-start(f32[16,40,256]{2,1,0:T(8,128)} %broadcast_in_dim.32), calls=%async_computation.1 | async-start | bytes 1310720 | tf_op jit(solution)/shard_map/all_to_all | solution.py:31
  53.2 5.1 %collective-permute-done.6 = f32[64,768]{1,0:T(8,128)S(1)} collective-permute-done((f32[64,768]{1,0:T(8,128)S(1)}, f32[64,768]{1,0:T(8,128)S(1)}, u32[]{:S(2)}, u32[]{:S(2)}) %collective-permute-start.6) | collective-permute-done | bytes 196640 | tf_op jit(solution)/shard_map/ppermute | solution.py:316
  58.4 2.6 %collective-permute-start.9 = (f32[64,768]{1,0:T(8,128)S(1)}, f32[64,768]{1,0:T(8,128)S(1)}, u32[]{:S(2)}, u32[]{:S(2)}) collective-permute-start(f32[64,768]{1,0:T(8,128)S(1)} %multiply_subtract_fusion.1.refs_0_), channel_id=1, source_target_pairs={{0,192},{64,128},{128,64},{192,0},{1,193},{65,129},{129,65},{193,1... | collective-permute-start | bytes 589832 | tf_op jit(solution)/shard_map/ppermute | solution.py:37
  61.8 4.4 %collective-permute-done.9.refs_3_ = f32[64,768]{1,0:T(8,128)S(1)} collective-permute-done((f32[64,768]{1,0:T(8,128)S(1)}, f32[64,768]{1,0:T(8,128)S(1)}, u32[]{:S(2)}, u32[]{:S(2)}) %collective-permute-start.9) | collective-permute-done | bytes 196640 | tf_op jit(solution)/shard_map/ppermute | solution.py:37
  68.1 3.7 %all-to-all-done.1 = f32[16,40,256]{2,1,0:T(8,128)S(1)} async-done(((f32[16,40,256]{2,1,0:T(8,128)}), f32[16,40,256]{2,1,0:T(8,128)S(1)}, u32[]{:S(2)}, u32[]{:S(2)}) %all-to-all-start.1) | async-done | bytes 655392 | tf_op jit(solution)/shard_map/all_to_all | solution.py:31
  71.8 3.5 %collective-permute-start.10 = (f32[640,256]{1,0:T(8,128)S(1)}, f32[640,256]{1,0:T(8,128)S(1)}, u32[]{:S(2)}, u32[]{:S(2)}) collective-permute-start(f32[640,256]{1,0:T(8,128)S(1)} %bitcast.14), channel_id=1, source_target_pairs={{0,1},{1,0},{2,3},{3,2},{4,5},{5,4},{6,7},{7,6},{8,9},{9,8},{10,11... | collective-permute-start | bytes 1966088 | tf_op jit(solution)/shard_map/ppermute | solution.py:330
  81.7 5.9 %all-to-all-start.2 = ((f32[16,40,256]{2,1,0:T(8,128)}), f32[16,40,256]{2,1,0:T(8,128)S(1)}, u32[]{:S(2)}, u32[]{:S(2)}) async-start(f32[16,40,256]{2,1,0:T(8,128)} %bitcast.7), calls=%async_computation.2 | async-start | bytes 1310720 | tf_op jit(solution)/shard_map/all_to_all | solution.py:26
  88.9 2.4 %collective-permute-start.13 = (f32[64,768]{1,0:T(8,128)S(1)}, f32[64,768]{1,0:T(8,128)S(1)}, u32[]{:S(2)}, u32[]{:S(2)}) collective-permute-start(f32[64,768]{1,0:T(8,128)S(1)} %get-tuple-element.88), channel_id=1, source_target_pairs={{0,128},{64,192},{128,0},{192,64},{1,129},{65,193},{129,1},{193,65... | collective-permute-start | bytes 589832 | tf_op jit(solution)/shard_map/ppermute | solution.py:37
  93.6 4.6 %collective-permute-start.15 = (f32[64,168]{1,0:T(8,128)S(1)}, f32[64,168]{1,0:T(8,128)S(1)}, u32[]{:S(2)}, u32[]{:S(2)}) collective-permute-start(f32[64,168]{1,0:T(8,128)S(1)} %get-tuple-element.103), channel_id=1, source_target_pairs={{1,0},{2,1},{3,2},{4,3},{5,4},{6,5},{7,6},{8,7},{9,8},{10,9},{11,1... | collective-permute-start | bytes 129032 | tf_op jit(solution)/shard_map/ppermute | solution.py:43
  98.1 4.9 %collective-permute-start.16 = (f32[64,168]{1,0:T(8,128)S(1)}, f32[64,168]{1,0:T(8,128)S(1)}, u32[]{:S(2)}, u32[]{:S(2)}) collective-permute-start(f32[64,168]{1,0:T(8,128)S(1)} %get-tuple-element.104), channel_id=1, source_target_pairs={{0,1},{1,2},{2,3},{3,4},{4,5},{5,6},{6,7},{7,8},{8,9},{9,10},{10,1... | collective-permute-start | bytes 129032 | tf_op jit(solution)/shard_map/ppermute | solution.py:43
  103.2 2.8 %collective-permute-done.16 = f32[64,168]{1,0:T(8,128)S(1)} collective-permute-done((f32[64,168]{1,0:T(8,128)S(1)}, f32[64,168]{1,0:T(8,128)S(1)}, u32[]{:S(2)}, u32[]{:S(2)}) %collective-permute-start.16) | collective-permute-done | bytes 43040 | tf_op jit(solution)/shard_map/ppermute | solution.py:43
  108.5 6.1 %all-to-all-start.3 = ((f32[16,40,256]{2,1,0:T(8,128)}), f32[16,40,256]{2,1,0:T(8,128)S(1)}, u32[]{:S(2)}, u32[]{:S(2)}) async-start(f32[16,40,256]{2,1,0:T(8,128)} %broadcast_in_dim.33), calls=%async_computation.3 | async-start | bytes 1310720 | tf_op jit(solution)/shard_map/all_to_all | solution.py:31
  115.4 4.9 %collective-permute-done.17 = f32[64,768]{1,0:T(8,128)S(1)} collective-permute-done((f32[64,768]{1,0:T(8,128)S(1)}, f32[64,768]{1,0:T(8,128)S(1)}, u32[]{:S(2)}, u32[]{:S(2)}) %collective-permute-start.17) | collective-permute-done | bytes 196640 | tf_op jit(solution)/shard_map/ppermute | solution.py:316
  120.3 2.5 %collective-permute-start.20 = (f32[64,768]{1,0:T(8,128)S(1)}, f32[64,768]{1,0:T(8,128)S(1)}, u32[]{:S(2)}, u32[]{:S(2)}) collective-permute-start(f32[64,768]{1,0:T(8,128)S(1)} %multiply_subtract_fusion.refs_0_), channel_id=1, source_target_pairs={{0,192},{64,128},{128,64},{192,0},{1,193},{65,129},{129,65},{193,1... | collective-permute-start | bytes 589832 | tf_op jit(solution)/shard_map/ppermute | solution.py:37
  123.6 4.4 %collective-permute-done.20.refs_3_ = f32[64,768]{1,0:T(8,128)S(1)} collective-permute-done((f32[64,768]{1,0:T(8,128)S(1)}, f32[64,768]{1,0:T(8,128)S(1)}, u32[]{:S(2)}, u32[]{:S(2)}) %collective-permute-start.20) | collective-permute-done | bytes 196640 | tf_op jit(solution)/shard_map/ppermute | solution.py:37
  131.0 3.0 %all-to-all-done.3 = f32[16,40,256]{2,1,0:T(8,128)S(1)} async-done(((f32[16,40,256]{2,1,0:T(8,128)}), f32[16,40,256]{2,1,0:T(8,128)S(1)}, u32[]{:S(2)}, u32[]{:S(2)}) %all-to-all-start.3) | async-done | bytes 655392 | tf_op jit(solution)/shard_map/all_to_all | solution.py:31
  134.0 2.9 %collective-permute-start.21 = (f32[640,256]{1,0:T(8,128)S(1)}, f32[640,256]{1,0:T(8,128)S(1)}, u32[]{:S(2)}, u32[]{:S(2)}) collective-permute-start(f32[640,256]{1,0:T(8,128)S(1)} %bitcast.12), channel_id=1, source_target_pairs={{0,1},{1,0},{2,3},{3,2},{4,5},{5,4},{6,7},{7,6},{8,9},{9,8},{10,11... | collective-permute-start | bytes 1966088 | tf_op jit(solution)/shard_map/ppermute | solution.py:330
  (76 shorter events, 35.5 us)
Async XLA Ops:
  9.2 5.3 %collective-permute-start = (f32[640,256]{1,0:T(8,128)}, f32[640,256]{1,0:T(8,128)S(1)}, u32[]{:S(2)}, u32[]{:S(2)}) collective-permute-start(f32[640,256]{1,0:T(8,128)} %get-tuple-element.54), channel_id=1, source_target_pairs={{0,1},{1,0},{2,3},{3,2},{4,5},{5,4},{6,7},{7,6},{8,9},{9,8},{10,11... | collective-permute-start | bytes 1966088 | tf_op jit(solution)/shard_map/ppermute | solution.py:272
  16.5 29.2 %all-to-all-start = ((f32[16,40,256]{2,1,0:T(8,128)}), f32[16,40,256]{2,1,0:T(8,128)S(1)}, u32[]{:S(2)}, u32[]{:S(2)}) async-start(f32[16,40,256]{2,1,0:T(8,128)} %bitcast.5), calls=%async_computation | async-start | bytes 1310720 | tf_op jit(solution)/shard_map/all_to_all | solution.py:26
  25.7 5.9 %collective-permute-start.1 = (f32[64,768]{1,0:T(8,128)S(1)}, f32[64,768]{1,0:T(8,128)S(1)}, u32[]{:S(2)}, u32[]{:S(2)}) collective-permute-start(f32[64,768]{1,0:T(8,128)S(1)} %copy-done.6), channel_id=1, source_target_pairs={{0,64},{64,0},{128,192},{192,128},{1,65},{65,1},{129,193},{193,129... | collective-permute-start | bytes 589832 | tf_op jit(solution)/shard_map/ppermute | solution.py:37
  27.0 14.2 %collective-permute-start.2 = (f32[64,768]{1,0:T(8,128)S(1)}, f32[64,768]{1,0:T(8,128)S(1)}, u32[]{:S(2)}, u32[]{:S(2)}) collective-permute-start(f32[64,768]{1,0:T(8,128)S(1)} %copy-done.5), channel_id=1, source_target_pairs={{0,128},{64,192},{128,0},{192,64},{1,129},{65,193},{129,1},{193,65... | collective-permute-start | bytes 589832 | tf_op jit(solution)/shard_map/ppermute | solution.py:37
  29.5 11.8 %collective-permute-start.3 = (f32[64,768]{1,0:T(8,128)S(1)}, f32[64,768]{1,0:T(8,128)S(1)}, u32[]{:S(2)}, u32[]{:S(2)}) collective-permute-start(f32[64,768]{1,0:T(8,128)S(1)} %copy-done.4), channel_id=1, source_target_pairs={{0,192},{64,128},{128,64},{192,0},{1,193},{65,129},{129,65},{193,1... | collective-permute-start | bytes 589832 | tf_op jit(solution)/shard_map/ppermute | solution.py:37
  31.7 10.1 %collective-permute-start.4 = (f32[64,168]{1,0:T(8,128)S(1)}, f32[64,168]{1,0:T(8,128)S(1)}, u32[]{:S(2)}, u32[]{:S(2)}) collective-permute-start(f32[64,168]{1,0:T(8,128)S(1)} %get-tuple-element.105), channel_id=1, source_target_pairs={{1,0},{2,1},{3,2},{4,3},{5,4},{6,5},{7,6},{8,7},{9,8},{10,9},{11,1... | collective-permute-start | bytes 129032 | tf_op jit(solution)/shard_map/ppermute | solution.py:43
  36.2 7.9 %collective-permute-start.5 = (f32[64,168]{1,0:T(8,128)S(1)}, f32[64,168]{1,0:T(8,128)S(1)}, u32[]{:S(2)}, u32[]{:S(2)}) collective-permute-start(f32[64,168]{1,0:T(8,128)S(1)} %get-tuple-element.106), channel_id=1, source_target_pairs={{0,1},{1,2},{2,3},{3,4},{4,5},{5,6},{6,7},{7,8},{8,9},{9,10},{10,1... | collective-permute-start | bytes 129032 | tf_op jit(solution)/shard_map/ppermute | solution.py:43
  46.6 25.2 %all-to-all-start.1 = ((f32[16,40,256]{2,1,0:T(8,128)}), f32[16,40,256]{2,1,0:T(8,128)S(1)}, u32[]{:S(2)}, u32[]{:S(2)}) async-start(f32[16,40,256]{2,1,0:T(8,128)} %broadcast_in_dim.32), calls=%async_computation.1 | async-start | bytes 1310720 | tf_op jit(solution)/shard_map/all_to_all | solution.py:31
  52.7 5.6 %collective-permute-start.6 = (f32[64,768]{1,0:T(8,128)S(1)}, f32[64,768]{1,0:T(8,128)S(1)}, u32[]{:S(2)}, u32[]{:S(2)}) collective-permute-start(f32[64,768]{1,0:T(8,128)S(1)} %add_add_fusion.1), channel_id=1, source_target_pairs={{0,32},{32,0},{1,33},{33,1},{2,34},{34,2},{3,35},{35,3},{4,36},{36... | collective-permute-start | bytes 589832 | tf_op jit(solution)/shard_map/ppermute | solution.py:316
  58.4 7.8 %collective-permute-start.9 = (f32[64,768]{1,0:T(8,128)S(1)}, f32[64,768]{1,0:T(8,128)S(1)}, u32[]{:S(2)}, u32[]{:S(2)}) collective-permute-start(f32[64,768]{1,0:T(8,128)S(1)} %multiply_subtract_fusion.1.refs_0_), channel_id=1, source_target_pairs={{0,192},{64,128},{128,64},{192,0},{1,193},{65,129},{129,65},{193,1... | collective-permute-start | bytes 589832 | tf_op jit(solution)/shard_map/ppermute | solution.py:37
  61.0 6.3 %collective-permute-start.8 = (f32[64,768]{1,0:T(8,128)S(1)}, f32[64,768]{1,0:T(8,128)S(1)}, u32[]{:S(2)}, u32[]{:S(2)}) collective-permute-start(f32[64,768]{1,0:T(8,128)S(1)} %multiply_subtract_fusion.1.refs_0_), channel_id=1, source_target_pairs={{0,128},{64,192},{128,0},{192,64},{1,129},{65,193},{129,1},{193,65... | collective-permute-start | bytes 589832 | tf_op jit(solution)/shard_map/ppermute | solution.py:37
  61.5 6.0 %collective-permute-start.7 = (f32[64,768]{1,0:T(8,128)S(1)}, f32[64,768]{1,0:T(8,128)S(1)}, u32[]{:S(2)}, u32[]{:S(2)}) collective-permute-start(f32[64,768]{1,0:T(8,128)S(1)} %multiply_subtract_fusion.1.refs_0_), channel_id=1, source_target_pairs={{0,64},{64,0},{128,192},{192,128},{1,65},{65,1},{129,193},{193,129... | collective-permute-start | bytes 589832 | tf_op jit(solution)/shard_map/ppermute | solution.py:37
  71.8 5.3 %collective-permute-start.10 = (f32[640,256]{1,0:T(8,128)S(1)}, f32[640,256]{1,0:T(8,128)S(1)}, u32[]{:S(2)}, u32[]{:S(2)}) collective-permute-start(f32[640,256]{1,0:T(8,128)S(1)} %bitcast.14), channel_id=1, source_target_pairs={{0,1},{1,0},{2,3},{3,2},{4,5},{5,4},{6,7},{7,6},{8,9},{9,8},{10,11... | collective-permute-start | bytes 1966088 | tf_op jit(solution)/shard_map/ppermute | solution.py:330
  81.7 25.9 %all-to-all-start.2 = ((f32[16,40,256]{2,1,0:T(8,128)}), f32[16,40,256]{2,1,0:T(8,128)S(1)}, u32[]{:S(2)}, u32[]{:S(2)}) async-start(f32[16,40,256]{2,1,0:T(8,128)} %bitcast.7), calls=%async_computation.2 | async-start | bytes 1310720 | tf_op jit(solution)/shard_map/all_to_all | solution.py:26
  87.6 5.9 %collective-permute-start.12 = (f32[64,768]{1,0:T(8,128)S(1)}, f32[64,768]{1,0:T(8,128)S(1)}, u32[]{:S(2)}, u32[]{:S(2)}) collective-permute-start(f32[64,768]{1,0:T(8,128)S(1)} %get-tuple-element.86), channel_id=1, source_target_pairs={{0,64},{64,0},{128,192},{192,128},{1,65},{65,1},{129,193},{193,129... | collective-permute-start | bytes 589832 | tf_op jit(solution)/shard_map/ppermute | solution.py:37
  88.9 14.2 %collective-permute-start.13 = (f32[64,768]{1,0:T(8,128)S(1)}, f32[64,768]{1,0:T(8,128)S(1)}, u32[]{:S(2)}, u32[]{:S(2)}) collective-permute-start(f32[64,768]{1,0:T(8,128)S(1)} %get-tuple-element.88), channel_id=1, source_target_pairs={{0,128},{64,192},{128,0},{192,64},{1,129},{65,193},{129,1},{193,65... | collective-permute-start | bytes 589832 | tf_op jit(solution)/shard_map/ppermute | solution.py:37
  91.3 11.8 %collective-permute-start.14 = (f32[64,768]{1,0:T(8,128)S(1)}, f32[64,768]{1,0:T(8,128)S(1)}, u32[]{:S(2)}, u32[]{:S(2)}) collective-permute-start(f32[64,768]{1,0:T(8,128)S(1)} %get-tuple-element.89), channel_id=1, source_target_pairs={{0,192},{64,128},{128,64},{192,0},{1,193},{65,129},{129,65},{193,1... | collective-permute-start | bytes 589832 | tf_op jit(solution)/shard_map/ppermute | solution.py:37
  93.6 9.7 %collective-permute-start.15 = (f32[64,168]{1,0:T(8,128)S(1)}, f32[64,168]{1,0:T(8,128)S(1)}, u32[]{:S(2)}, u32[]{:S(2)}) collective-permute-start(f32[64,168]{1,0:T(8,128)S(1)} %get-tuple-element.103), channel_id=1, source_target_pairs={{1,0},{2,1},{3,2},{4,3},{5,4},{6,5},{7,6},{8,7},{9,8},{10,9},{11,1... | collective-permute-start | bytes 129032 | tf_op jit(solution)/shard_map/ppermute | solution.py:43
  98.1 7.9 %collective-permute-start.16 = (f32[64,168]{1,0:T(8,128)S(1)}, f32[64,168]{1,0:T(8,128)S(1)}, u32[]{:S(2)}, u32[]{:S(2)}) collective-permute-start(f32[64,168]{1,0:T(8,128)S(1)} %get-tuple-element.104), channel_id=1, source_target_pairs={{0,1},{1,2},{2,3},{3,4},{4,5},{5,6},{6,7},{7,8},{8,9},{9,10},{10,1... | collective-permute-start | bytes 129032 | tf_op jit(solution)/shard_map/ppermute | solution.py:43
  108.5 25.5 %all-to-all-start.3 = ((f32[16,40,256]{2,1,0:T(8,128)}), f32[16,40,256]{2,1,0:T(8,128)S(1)}, u32[]{:S(2)}, u32[]{:S(2)}) async-start(f32[16,40,256]{2,1,0:T(8,128)} %broadcast_in_dim.33), calls=%async_computation.3 | async-start | bytes 1310720 | tf_op jit(solution)/shard_map/all_to_all | solution.py:31
  114.6 5.6 %collective-permute-start.17 = (f32[64,768]{1,0:T(8,128)S(1)}, f32[64,768]{1,0:T(8,128)S(1)}, u32[]{:S(2)}, u32[]{:S(2)}) collective-permute-start(f32[64,768]{1,0:T(8,128)S(1)} %add_add_fusion), channel_id=1, source_target_pairs={{0,32},{32,0},{1,33},{33,1},{2,34},{34,2},{3,35},{35,3},{4,36},{36... | collective-permute-start | bytes 589832 | tf_op jit(solution)/shard_map/ppermute | solution.py:316
  120.3 7.7 %collective-permute-start.20 = (f32[64,768]{1,0:T(8,128)S(1)}, f32[64,768]{1,0:T(8,128)S(1)}, u32[]{:S(2)}, u32[]{:S(2)}) collective-permute-start(f32[64,768]{1,0:T(8,128)S(1)} %multiply_subtract_fusion.refs_0_), channel_id=1, source_target_pairs={{0,192},{64,128},{128,64},{192,0},{1,193},{65,129},{129,65},{193,1... | collective-permute-start | bytes 589832 | tf_op jit(solution)/shard_map/ppermute | solution.py:37
  122.7 6.3 %collective-permute-start.19 = (f32[64,768]{1,0:T(8,128)S(1)}, f32[64,768]{1,0:T(8,128)S(1)}, u32[]{:S(2)}, u32[]{:S(2)}) collective-permute-start(f32[64,768]{1,0:T(8,128)S(1)} %multiply_subtract_fusion.refs_0_), channel_id=1, source_target_pairs={{0,128},{64,192},{128,0},{192,64},{1,129},{65,193},{129,1},{193,65... | collective-permute-start | bytes 589832 | tf_op jit(solution)/shard_map/ppermute | solution.py:37
  123.3 6.2 %collective-permute-start.18 = (f32[64,768]{1,0:T(8,128)S(1)}, f32[64,768]{1,0:T(8,128)S(1)}, u32[]{:S(2)}, u32[]{:S(2)}) collective-permute-start(f32[64,768]{1,0:T(8,128)S(1)} %multiply_subtract_fusion.refs_0_), channel_id=1, source_target_pairs={{0,64},{64,0},{128,192},{192,128},{1,65},{65,1},{129,193},{193,129... | collective-permute-start | bytes 589832 | tf_op jit(solution)/shard_map/ppermute | solution.py:37
  (9 other events, 153.8 us)

commit v8 on v7

--- a/solution.py
+++ b/solution.py
@@ -101,7 +101,7 @@
                 out[pl.ds(start, size), :] = piece[...].astype(out.dtype)
 
 
-def first_pass(place_ref, x_ref, f_ref, seen_ref, mask_ref, *refs):
+def first_pass(_, along_ref, x_ref, f_ref, seen_ref, mask_ref, *refs):
     theirs_ref, mine_ref, kept_ref, *pieces, x_low_ref, total_ref = refs
     i = pl.program_id(0)
 
@@ -126,7 +126,7 @@
     def _():
         mine_ref[...] = grad
 
-    share_out(place_ref[1], total_ref, pieces)
+    share_out(along_ref[0], total_ref, pieces)
 
 
 def misfit_of(f_low, x_low, kept_ref):
@@ -134,17 +134,17 @@
     return jnp.where(kept < HIDDEN / 2, dot(f_low, x_low) - kept, 0.0).astype(BF16)
 
 
-def placed(place_ref, *refs):
+def placed(_, along_ref, *refs):
     *came, x_ref, x_low_ref = refs
-    assembled(place_ref[1], came, x_ref, x_low_ref)
-
-
-def placed_low(place_ref, *refs):
+    assembled(along_ref[0], came, x_ref, x_low_ref)
+
+
+def placed_low(_, along_ref, *refs):
     *came, x_low_ref = refs
-    assembled(place_ref[1], came, x_low_ref)
-
-
-def later_mine(_, x_low_ref, f_ref, kept_ref, grad_ref, total_ref):
+    assembled(along_ref[0], came, x_low_ref)
+
+
+def later_mine(_, __, x_low_ref, f_ref, kept_ref, grad_ref, total_ref):
     x_low = x_low_ref[...]
     f_low = f_ref[...].astype(BF16)
     misfit = misfit_of(f_low, x_low, kept_ref)
@@ -152,41 +152,41 @@
     add_up(total_ref, by_rows(f_low, misfit))
 
 
-def later_theirs(_, x_low_ref, f_ref, kept_ref, grad_ref, misfit_ref):
+def later_theirs(_, __, x_low_ref, f_ref, kept_ref, grad_ref, misfit_ref):
     x_low = x_low_ref[...]
     misfit = misfit_of(f_ref[...].astype(BF16), x_low, kept_ref)
     misfit_ref[...] = misfit
     grad_ref[...] = by_hours(misfit, x_low)
 
 
-def later_rows(place_ref, f_ref, misfit_ref, start_ref, *refs):
+def later_rows(_, along_ref, f_ref, misfit_ref, start_ref, *refs):
     *pieces, total_ref = refs
     add_up(total_ref, by_rows(f_ref[...].astype(BF16), misfit_ref[...]), start_ref)
-    share_out(place_ref[1], total_ref, pieces)
-
-
-def last_mine(_, x_low_ref, f_ref, f_out_ref, imputed_ref):
+    share_out(along_ref[0], total_ref, pieces)
+
+
+def last_mine(_, __, x_low_ref, f_ref, f_out_ref, imputed_ref):
     f_out_ref[...] = f_ref[...]
     imputed_ref[...] = dot(f_ref[...].astype(BF16), x_low_ref[...]).astype(BF16)
 
 
-def last_theirs(_, x_low_ref, f_ref, f_held_ref, imputed_held_ref, f_out_ref, imputed_ref):
+def last_theirs(_, __, x_low_ref, f_ref, f_held_ref, imputed_held_ref, f_out_ref, imputed_ref):
     f_out_ref[...] = f_ref[...]
     imputed_ref[...] = dot(f_ref[...].astype(BF16), x_low_ref[...]).astype(BF16)
 
 
 def half_pass(kernel, place, ins, outs, steps, limit, matmuls, scratch=(), aliases=()):
     maps = {
-        "whole": lambda i, p: (0, 0),
-        "half": lambda i, p: (i, 0),
-        "mine": lambda i, p: (p[0] * steps + i, 0),
-        "theirs": lambda i, p: ((1 - p[0]) * steps + i, 0),
-        "both": lambda i, p: ((i // FIRST + 1 + p[0]) % 2 * FIRST + i % FIRST, 0),
-        "all": lambda i, p: (i, 0),
-        "lower": lambda i, p: (i, 0),
-        "upper": lambda i, p: (steps + i, 0),
-        "former": lambda i, p: (jnp.minimum(i, FIRST - 1), 0),
-        "latter": lambda i, p: (jnp.maximum(i - FIRST, 0), 0),
+        "whole": lambda i, p, _: (0, 0),
+        "half": lambda i, p, _: (i, 0),
+        "mine": lambda i, p, _: (p[0] * steps + i, 0),
+        "theirs": lambda i, p, _: ((1 - p[0]) * steps + i, 0),
+        "both": lambda i, p, _: ((i // FIRST + 1 + p[0]) % 2 * FIRST + i % FIRST, 0),
+        "all": lambda i, p, _: (i, 0),
+        "lower": lambda i, p, _: (i, 0),
+        "upper": lambda i, p, _: (steps + i, 0),
+        "former": lambda i, p, _: (jnp.minimum(i, FIRST - 1), 0),
+        "latter": lambda i, p, _: (jnp.maximum(i - FIRST, 0), 0),
     }
     tiles = {"whole": 1, "half": steps, "mine": 2 * steps, "theirs": 2 * steps}
     tiles.update(both=2 * FIRST, former=FIRST, latter=FIRST, all=steps)
@@ -207,7 +207,7 @@
         kernel,
         out_shape=[s for _, s in outs],
         grid_spec=pltpu.PrefetchScalarGridSpec(
-            num_scalar_prefetch=1,
+            num_scalar_prefetch=2,
             grid=(steps,),
             in_specs=[spec(k, a.shape) for k, a in ins],
             out_specs=[spec(k, s.shape) for k, s in outs],
@@ -219,7 +219,7 @@
         ),
         input_output_aliases=dict(aliases),
         name=kernel.__name__,
-    )(place, *[a for _, a in ins])
+    )(*place, *[a for _, a in ins])
 
 
 def local(observed, mask, series_factors, time_factors, ar_weights):
@@ -242,7 +242,7 @@
     along = lax.axis_index("x")
     position = lax.axis_index(TM)
     first, last = position == 0, position == lax.axis_size(TM) - 1
-    place = jnp.stack([core, along])
+    place = (core.reshape(1), along.reshape(1))
 
     def shape(n, m, dtype=F32):
         return jax.ShapeDtypeStruct((n, m), dtype)
@@ -345,7 +345,7 @@
         LAST,
         16,
         1,
-        aliases={3: 0, 4: 1},
+        aliases={4: 0, 5: 1},
     )
     return f_out, x_full[0], imputed
 

time: 142 us -> 139 us (0.979)
  Pallas kernels: 18.2 us -> 13.7 us
  waiting for transfers between devices: 40.4 us -> 42.9 us
    pallas_call x8, Pallas kernels: 18.2 us -> 13.7 us  [half_pass(): pl.pallas_call(kernel, out_shape=[s for _, s in outs], grid_spec=pltpu.Pr...]
  transfers between devices with their start and end apart: 26 -> 26, of which waited for: 21 -> 22; matrix products, arithmetic and copies ran while one was open for 3% -> 3% of each run, Pallas kernels for 5% -> 3%
where the time goes in v8:
time: 139 us; the launch traced here: 138 us
  starting transfers between devices  71.8 us (52%)
  waiting for transfers between devices  42.9 us (31%)
  Pallas kernels  13.7 us (10%)
  other arithmetic  4.35 us (3%)
  local copies, waits for them, and re-layouts  4.12 us (3%)
    ppermute x4, starting transfers between devices, passed_along(): return lax.ppermute(array, axis, pairs)  19 us
    ppermute x12, waiting for transfers between devices, traded(): return lax.ppermute(array, axis, [(i, i ^ bits) for i in range(length)])  15.5 us
    ppermute x12, starting transfers between devices, traded(): return lax.ppermute(array, axis, [(i, i ^ bits) for i in range(length)])  14.6 us
    all_to_all x2, starting transfers between devices, scattered_sum(): return lax.all_to_all(parts, axis, 0, 0, tiled=True).sum(axis=0)  14.5 us
    pallas_call x8, Pallas kernels, half_pass(): pl.pallas_call(kernel, out_shape=[s for _, s in outs], grid_spec=pltpu.Pr...  13.7 us
    all_to_all x2, starting transfers between devices, gathered(): parts = lax.all_to_all(parts, axis, 0, 0, tiled=True)  12.2 us
    ppermute x2, waiting for transfers between devices, local(): x_sum = x_sum + lax.ppermute(x_sum, 'y_lo', SWAP)  9.98 us
    all_to_all x2, waiting for transfers between devices, gathered(): parts = lax.all_to_all(parts, axis, 0, 0, tiled=True)  7.79 us
  transfers between devices with their start and end apart: 26, of which 22 were waited for; matrix products, arithmetic and copies ran while one was open for 3% of the time, Pallas kernels for 3%

profile of v8, /device:TPU:1, one launch (start us, length us, event | category | flops | bytes accessed | tf_op | source)
XLA Modules:
  0.0 137.8 jit_solution(12012660911769164836)
XLA Ops:
  0.7 7.3 %first_pass.1 = (f32[640,256]{1,0:T(8,128)}, f32[640,256]{1,0:T(8,128)}, bf16[1280,768]{1,0:T(8,128)(2,1)}, f32[64,768]{1,0:T(8,128)}, f32[64,768]{1,0:T(8,128)}, /*index=5*/f32[64,768]{1,0:T(8,128)}, f32[64,768]{1,0:T(8,128)}) custom-call(s32[1]{0:T(128)} %bitcast._, s32[1]{0:T(128)} %bitcast.1.along_ref.__, f32[256,768]{1,0:T(8,128)} %x_ref.1, ...), custom_call_target="tpu_custom_call" | custom-call | flops 1509949440 | bytes 12058624 | tf_op jit(solution)/shard_map/first_pass/pallas_call | solution.py:206
  8.0 3.3 %collective-permute-start = (f32[640,256]{1,0:T(8,128)}, f32[640,256]{1,0:T(8,128)S(1)}, u32[]{:S(2)}, u32[]{:S(2)}) collective-permute-start(f32[640,256]{1,0:T(8,128)} %get-tuple-element.54), channel_id=1, source_target_pairs={{0,1},{1,0},{2,3},{3,2},{4,5},{5,4},{6,7},{7,6},{8,9},{9,8},{10,11... | collective-permute-start | bytes 1966088 | tf_op jit(solution)/shard_map/ppermute | solution.py:272
  15.3 9.2 %all-to-all-start = ((f32[16,40,256]{2,1,0:T(8,128)}), f32[16,40,256]{2,1,0:T(8,128)S(1)}, u32[]{:S(2)}, u32[]{:S(2)}) async-start(f32[16,40,256]{2,1,0:T(8,128)} %bitcast.5), calls=%async_computation | async-start | bytes 1310720 | tf_op jit(solution)/shard_map/all_to_all | solution.py:26
  25.8 2.5 %collective-permute-start.2 = (f32[64,768]{1,0:T(8,128)S(1)}, f32[64,768]{1,0:T(8,128)S(1)}, u32[]{:S(2)}, u32[]{:S(2)}) collective-permute-start(f32[64,768]{1,0:T(8,128)S(1)} %copy-done.4), channel_id=1, source_target_pairs={{0,128},{64,192},{128,0},{192,64},{1,129},{65,193},{129,1},{193,65... | collective-permute-start | bytes 589832 | tf_op jit(solution)/shard_map/ppermute | solution.py:37
  30.5 4.6 %collective-permute-start.4 = (f32[64,168]{1,0:T(8,128)S(1)}, f32[64,168]{1,0:T(8,128)S(1)}, u32[]{:S(2)}, u32[]{:S(2)}) collective-permute-start(f32[64,168]{1,0:T(8,128)S(1)} %get-tuple-element.105), channel_id=1, source_target_pairs={{1,0},{2,1},{3,2},{4,3},{5,4},{6,5},{7,6},{8,7},{9,8},{10,9},{11,1... | collective-permute-start | bytes 129032 | tf_op jit(solution)/shard_map/ppermute | solution.py:43
  35.0 5.0 %collective-permute-start.5 = (f32[64,168]{1,0:T(8,128)S(1)}, f32[64,168]{1,0:T(8,128)S(1)}, u32[]{:S(2)}, u32[]{:S(2)}) collective-permute-start(f32[64,168]{1,0:T(8,128)S(1)} %get-tuple-element.106), channel_id=1, source_target_pairs={{0,1},{1,2},{2,3},{3,4},{4,5},{5,6},{6,7},{7,8},{8,9},{9,10},{10,1... | collective-permute-start | bytes 129032 | tf_op jit(solution)/shard_map/ppermute | solution.py:43
  40.6 2.3 %collective-permute-done.5 = f32[64,168]{1,0:T(8,128)S(1)} collective-permute-done((f32[64,168]{1,0:T(8,128)S(1)}, f32[64,168]{1,0:T(8,128)S(1)}, u32[]{:S(2)}, u32[]{:S(2)}) %collective-permute-start.5) | collective-permute-done | bytes 43040 | tf_op jit(solution)/shard_map/ppermute | solution.py:43
  45.4 6.1 %all-to-all-start.1 = ((f32[16,40,256]{2,1,0:T(8,128)}), f32[16,40,256]{2,1,0:T(8,128)S(1)}, u32[]{:S(2)}, u32[]{:S(2)}) async-start(f32[16,40,256]{2,1,0:T(8,128)} %broadcast_in_dim.32), calls=%async_computation.1 | async-start | bytes 1310720 | tf_op jit(solution)/shard_map/all_to_all | solution.py:31
  52.0 5.1 %collective-permute-done.6 = f32[64,768]{1,0:T(8,128)S(1)} collective-permute-done((f32[64,768]{1,0:T(8,128)S(1)}, f32[64,768]{1,0:T(8,128)S(1)}, u32[]{:S(2)}, u32[]{:S(2)}) %collective-permute-start.6) | collective-permute-done | bytes 196640 | tf_op jit(solution)/shard_map/ppermute | solution.py:316
  57.2 2.6 %collective-permute-start.9 = (f32[64,768]{1,0:T(8,128)S(1)}, f32[64,768]{1,0:T(8,128)S(1)}, u32[]{:S(2)}, u32[]{:S(2)}) collective-permute-start(f32[64,768]{1,0:T(8,128)S(1)} %multiply_subtract_fusion.1.refs_0_), channel_id=1, source_target_pairs={{0,192},{64,128},{128,64},{192,0},{1,193},{65,129},{129,65},{193,1... | collective-permute-start | bytes 589832 | tf_op jit(solution)/shard_map/ppermute | solution.py:37
  60.6 4.4 %collective-permute-done.9.refs_3_ = f32[64,768]{1,0:T(8,128)S(1)} collective-permute-done((f32[64,768]{1,0:T(8,128)S(1)}, f32[64,768]{1,0:T(8,128)S(1)}, u32[]{:S(2)}, u32[]{:S(2)}) %collective-permute-start.9) | collective-permute-done | bytes 196640 | tf_op jit(solution)/shard_map/ppermute | solution.py:37
  66.4 4.2 %all-to-all-done.1 = f32[16,40,256]{2,1,0:T(8,128)S(1)} async-done(((f32[16,40,256]{2,1,0:T(8,128)}), f32[16,40,256]{2,1,0:T(8,128)S(1)}, u32[]{:S(2)}, u32[]{:S(2)}) %all-to-all-start.1) | async-done | bytes 655392 | tf_op jit(solution)/shard_map/all_to_all | solution.py:31
  70.6 3.5 %collective-permute-start.10 = (f32[640,256]{1,0:T(8,128)S(1)}, f32[640,256]{1,0:T(8,128)S(1)}, u32[]{:S(2)}, u32[]{:S(2)}) collective-permute-start(f32[640,256]{1,0:T(8,128)S(1)} %bitcast.14), channel_id=1, source_target_pairs={{0,1},{1,0},{2,3},{3,2},{4,5},{5,4},{6,7},{7,6},{8,9},{9,8},{10,11... | collective-permute-start | bytes 1966088 | tf_op jit(solution)/shard_map/ppermute | solution.py:330
  80.0 5.4 %all-to-all-start.2 = ((f32[16,40,256]{2,1,0:T(8,128)}), f32[16,40,256]{2,1,0:T(8,128)S(1)}, u32[]{:S(2)}, u32[]{:S(2)}) async-start(f32[16,40,256]{2,1,0:T(8,128)} %bitcast.7), calls=%async_computation.2 | async-start | bytes 1310720 | tf_op jit(solution)/shard_map/all_to_all | solution.py:26
  86.6 2.4 %collective-permute-start.13 = (f32[64,768]{1,0:T(8,128)S(1)}, f32[64,768]{1,0:T(8,128)S(1)}, u32[]{:S(2)}, u32[]{:S(2)}) collective-permute-start(f32[64,768]{1,0:T(8,128)S(1)} %get-tuple-element.88), channel_id=1, source_target_pairs={{0,128},{64,192},{128,0},{192,64},{1,129},{65,193},{129,1},{193,65... | collective-permute-start | bytes 589832 | tf_op jit(solution)/shard_map/ppermute | solution.py:37
  91.3 4.6 %collective-permute-start.15 = (f32[64,168]{1,0:T(8,128)S(1)}, f32[64,168]{1,0:T(8,128)S(1)}, u32[]{:S(2)}, u32[]{:S(2)}) collective-permute-start(f32[64,168]{1,0:T(8,128)S(1)} %get-tuple-element.103), channel_id=1, source_target_pairs={{1,0},{2,1},{3,2},{4,3},{5,4},{6,5},{7,6},{8,7},{9,8},{10,9},{11,1... | collective-permute-start | bytes 129032 | tf_op jit(solution)/shard_map/ppermute | solution.py:43
  95.8 4.9 %collective-permute-start.16 = (f32[64,168]{1,0:T(8,128)S(1)}, f32[64,168]{1,0:T(8,128)S(1)}, u32[]{:S(2)}, u32[]{:S(2)}) collective-permute-start(f32[64,168]{1,0:T(8,128)S(1)} %get-tuple-element.104), channel_id=1, source_target_pairs={{0,1},{1,2},{2,3},{3,4},{4,5},{5,6},{6,7},{7,8},{8,9},{9,10},{10,1... | collective-permute-start | bytes 129032 | tf_op jit(solution)/shard_map/ppermute | solution.py:43
  101.0 2.8 %collective-permute-done.16 = f32[64,168]{1,0:T(8,128)S(1)} collective-permute-done((f32[64,168]{1,0:T(8,128)S(1)}, f32[64,168]{1,0:T(8,128)S(1)}, u32[]{:S(2)}, u32[]{:S(2)}) %collective-permute-start.16) | collective-permute-done | bytes 43040 | tf_op jit(solution)/shard_map/ppermute | solution.py:43
  106.2 6.1 %all-to-all-start.3 = ((f32[16,40,256]{2,1,0:T(8,128)}), f32[16,40,256]{2,1,0:T(8,128)S(1)}, u32[]{:S(2)}, u32[]{:S(2)}) async-start(f32[16,40,256]{2,1,0:T(8,128)} %broadcast_in_dim.33), calls=%async_computation.3 | async-start | bytes 1310720 | tf_op jit(solution)/shard_map/all_to_all | solution.py:31
  113.1 4.9 %collective-permute-done.17 = f32[64,768]{1,0:T(8,128)S(1)} collective-permute-done((f32[64,768]{1,0:T(8,128)S(1)}, f32[64,768]{1,0:T(8,128)S(1)}, u32[]{:S(2)}, u32[]{:S(2)}) %collective-permute-start.17) | collective-permute-done | bytes 196640 | tf_op jit(solution)/shard_map/ppermute | solution.py:316
  118.0 2.5 %collective-permute-start.20 = (f32[64,768]{1,0:T(8,128)S(1)}, f32[64,768]{1,0:T(8,128)S(1)}, u32[]{:S(2)}, u32[]{:S(2)}) collective-permute-start(f32[64,768]{1,0:T(8,128)S(1)} %multiply_subtract_fusion.refs_0_), channel_id=1, source_target_pairs={{0,192},{64,128},{128,64},{192,0},{1,193},{65,129},{129,65},{193,1... | collective-permute-start | bytes 589832 | tf_op jit(solution)/shard_map/ppermute | solution.py:37
  121.3 4.4 %collective-permute-done.20.refs_3_ = f32[64,768]{1,0:T(8,128)S(1)} collective-permute-done((f32[64,768]{1,0:T(8,128)S(1)}, f32[64,768]{1,0:T(8,128)S(1)}, u32[]{:S(2)}, u32[]{:S(2)}) %collective-permute-start.20) | collective-permute-done | bytes 196640 | tf_op jit(solution)/shard_map/ppermute | solution.py:37
  128.2 3.5 %all-to-all-done.3 = f32[16,40,256]{2,1,0:T(8,128)S(1)} async-done(((f32[16,40,256]{2,1,0:T(8,128)}), f32[16,40,256]{2,1,0:T(8,128)S(1)}, u32[]{:S(2)}, u32[]{:S(2)}) %all-to-all-start.3) | async-done | bytes 655392 | tf_op jit(solution)/shard_map/all_to_all | solution.py:31
  131.7 2.9 %collective-permute-start.21 = (f32[640,256]{1,0:T(8,128)S(1)}, f32[640,256]{1,0:T(8,128)S(1)}, u32[]{:S(2)}, u32[]{:S(2)}) collective-permute-start(f32[640,256]{1,0:T(8,128)S(1)} %bitcast.12), channel_id=1, source_target_pairs={{0,1},{1,0},{2,3},{3,2},{4,5},{5,4},{6,7},{7,6},{8,9},{9,8},{10,11... | collective-permute-start | bytes 1966088 | tf_op jit(solution)/shard_map/ppermute | solution.py:330
  (73 shorter events, 32.4 us)
Async XLA Ops:
  8.0 5.3 %collective-permute-start = (f32[640,256]{1,0:T(8,128)}, f32[640,256]{1,0:T(8,128)S(1)}, u32[]{:S(2)}, u32[]{:S(2)}) collective-permute-start(f32[640,256]{1,0:T(8,128)} %get-tuple-element.54), channel_id=1, source_target_pairs={{0,1},{1,0},{2,3},{3,2},{4,5},{5,4},{6,7},{7,6},{8,9},{9,8},{10,11... | collective-permute-start | bytes 1966088 | tf_op jit(solution)/shard_map/ppermute | solution.py:272
  15.3 29.2 %all-to-all-start = ((f32[16,40,256]{2,1,0:T(8,128)}), f32[16,40,256]{2,1,0:T(8,128)S(1)}, u32[]{:S(2)}, u32[]{:S(2)}) async-start(f32[16,40,256]{2,1,0:T(8,128)} %bitcast.5), calls=%async_computation | async-start | bytes 1310720 | tf_op jit(solution)/shard_map/all_to_all | solution.py:26
  24.5 5.9 %collective-permute-start.1 = (f32[64,768]{1,0:T(8,128)S(1)}, f32[64,768]{1,0:T(8,128)S(1)}, u32[]{:S(2)}, u32[]{:S(2)}) collective-permute-start(f32[64,768]{1,0:T(8,128)S(1)} %copy-done.5), channel_id=1, source_target_pairs={{0,64},{64,0},{128,192},{192,128},{1,65},{65,1},{129,193},{193,129... | collective-permute-start | bytes 589832 | tf_op jit(solution)/shard_map/ppermute | solution.py:37
  25.8 14.2 %collective-permute-start.2 = (f32[64,768]{1,0:T(8,128)S(1)}, f32[64,768]{1,0:T(8,128)S(1)}, u32[]{:S(2)}, u32[]{:S(2)}) collective-permute-start(f32[64,768]{1,0:T(8,128)S(1)} %copy-done.4), channel_id=1, source_target_pairs={{0,128},{64,192},{128,0},{192,64},{1,129},{65,193},{129,1},{193,65... | collective-permute-start | bytes 589832 | tf_op jit(solution)/shard_map/ppermute | solution.py:37
  28.3 11.8 %collective-permute-start.3 = (f32[64,768]{1,0:T(8,128)S(1)}, f32[64,768]{1,0:T(8,128)S(1)}, u32[]{:S(2)}, u32[]{:S(2)}) collective-permute-start(f32[64,768]{1,0:T(8,128)S(1)} %copy-done.3), channel_id=1, source_target_pairs={{0,192},{64,128},{128,64},{192,0},{1,193},{65,129},{129,65},{193,1... | collective-permute-start | bytes 589832 | tf_op jit(solution)/shard_map/ppermute | solution.py:37
  30.5 10.1 %collective-permute-start.4 = (f32[64,168]{1,0:T(8,128)S(1)}, f32[64,168]{1,0:T(8,128)S(1)}, u32[]{:S(2)}, u32[]{:S(2)}) collective-permute-start(f32[64,168]{1,0:T(8,128)S(1)} %get-tuple-element.105), channel_id=1, source_target_pairs={{1,0},{2,1},{3,2},{4,3},{5,4},{6,5},{7,6},{8,7},{9,8},{10,9},{11,1... | collective-permute-start | bytes 129032 | tf_op jit(solution)/shard_map/ppermute | solution.py:43
  35.0 7.9 %collective-permute-start.5 = (f32[64,168]{1,0:T(8,128)S(1)}, f32[64,168]{1,0:T(8,128)S(1)}, u32[]{:S(2)}, u32[]{:S(2)}) collective-permute-start(f32[64,168]{1,0:T(8,128)S(1)} %get-tuple-element.106), channel_id=1, source_target_pairs={{0,1},{1,2},{2,3},{3,4},{4,5},{5,6},{6,7},{7,8},{8,9},{9,10},{10,1... | collective-permute-start | bytes 129032 | tf_op jit(solution)/shard_map/ppermute | solution.py:43
  45.4 25.2 %all-to-all-start.1 = ((f32[16,40,256]{2,1,0:T(8,128)}), f32[16,40,256]{2,1,0:T(8,128)S(1)}, u32[]{:S(2)}, u32[]{:S(2)}) async-start(f32[16,40,256]{2,1,0:T(8,128)} %broadcast_in_dim.32), calls=%async_computation.1 | async-start | bytes 1310720 | tf_op jit(solution)/shard_map/all_to_all | solution.py:31
  51.5 5.6 %collective-permute-start.6 = (f32[64,768]{1,0:T(8,128)S(1)}, f32[64,768]{1,0:T(8,128)S(1)}, u32[]{:S(2)}, u32[]{:S(2)}) collective-permute-start(f32[64,768]{1,0:T(8,128)S(1)} %add_add_fusion.1), channel_id=1, source_target_pairs={{0,32},{32,0},{1,33},{33,1},{2,34},{34,2},{3,35},{35,3},{4,36},{36... | collective-permute-start | bytes 589832 | tf_op jit(solution)/shard_map/ppermute | solution.py:316
  57.2 7.8 %collective-permute-start.9 = (f32[64,768]{1,0:T(8,128)S(1)}, f32[64,768]{1,0:T(8,128)S(1)}, u32[]{:S(2)}, u32[]{:S(2)}) collective-permute-start(f32[64,768]{1,0:T(8,128)S(1)} %multiply_subtract_fusion.1.refs_0_), channel_id=1, source_target_pairs={{0,192},{64,128},{128,64},{192,0},{1,193},{65,129},{129,65},{193,1... | collective-permute-start | bytes 589832 | tf_op jit(solution)/shard_map/ppermute | solution.py:37
  59.8 6.3 %collective-permute-start.8 = (f32[64,768]{1,0:T(8,128)S(1)}, f32[64,768]{1,0:T(8,128)S(1)}, u32[]{:S(2)}, u32[]{:S(2)}) collective-permute-start(f32[64,768]{1,0:T(8,128)S(1)} %multiply_subtract_fusion.1.refs_0_), channel_id=1, source_target_pairs={{0,128},{64,192},{128,0},{192,64},{1,129},{65,193},{129,1},{193,65... | collective-permute-start | bytes 589832 | tf_op jit(solution)/shard_map/ppermute | solution.py:37
  60.3 6.0 %collective-permute-start.7 = (f32[64,768]{1,0:T(8,128)S(1)}, f32[64,768]{1,0:T(8,128)S(1)}, u32[]{:S(2)}, u32[]{:S(2)}) collective-permute-start(f32[64,768]{1,0:T(8,128)S(1)} %multiply_subtract_fusion.1.refs_0_), channel_id=1, source_target_pairs={{0,64},{64,0},{128,192},{192,128},{1,65},{65,1},{129,193},{193,129... | collective-permute-start | bytes 589832 | tf_op jit(solution)/shard_map/ppermute | solution.py:37
  70.6 5.3 %collective-permute-start.10 = (f32[640,256]{1,0:T(8,128)S(1)}, f32[640,256]{1,0:T(8,128)S(1)}, u32[]{:S(2)}, u32[]{:S(2)}) collective-permute-start(f32[640,256]{1,0:T(8,128)S(1)} %bitcast.14), channel_id=1, source_target_pairs={{0,1},{1,0},{2,3},{3,2},{4,5},{5,4},{6,7},{7,6},{8,9},{9,8},{10,11... | collective-permute-start | bytes 1966088 | tf_op jit(solution)/shard_map/ppermute | solution.py:330
  80.0 25.3 %all-to-all-start.2 = ((f32[16,40,256]{2,1,0:T(8,128)}), f32[16,40,256]{2,1,0:T(8,128)S(1)}, u32[]{:S(2)}, u32[]{:S(2)}) async-start(f32[16,40,256]{2,1,0:T(8,128)} %bitcast.7), calls=%async_computation.2 | async-start | bytes 1310720 | tf_op jit(solution)/shard_map/all_to_all | solution.py:26
  85.3 5.9 %collective-permute-start.12 = (f32[64,768]{1,0:T(8,128)S(1)}, f32[64,768]{1,0:T(8,128)S(1)}, u32[]{:S(2)}, u32[]{:S(2)}) collective-permute-start(f32[64,768]{1,0:T(8,128)S(1)} %get-tuple-element.86), channel_id=1, source_target_pairs={{0,64},{64,0},{128,192},{192,128},{1,65},{65,1},{129,193},{193,129... | collective-permute-start | bytes 589832 | tf_op jit(solution)/shard_map/ppermute | solution.py:37
  86.6 14.2 %collective-permute-start.13 = (f32[64,768]{1,0:T(8,128)S(1)}, f32[64,768]{1,0:T(8,128)S(1)}, u32[]{:S(2)}, u32[]{:S(2)}) collective-permute-start(f32[64,768]{1,0:T(8,128)S(1)} %get-tuple-element.88), channel_id=1, source_target_pairs={{0,128},{64,192},{128,0},{192,64},{1,129},{65,193},{129,1},{193,65... | collective-permute-start | bytes 589832 | tf_op jit(solution)/shard_map/ppermute | solution.py:37
  89.0 11.8 %collective-permute-start.14 = (f32[64,768]{1,0:T(8,128)S(1)}, f32[64,768]{1,0:T(8,128)S(1)}, u32[]{:S(2)}, u32[]{:S(2)}) collective-permute-start(f32[64,768]{1,0:T(8,128)S(1)} %get-tuple-element.89), channel_id=1, source_target_pairs={{0,192},{64,128},{128,64},{192,0},{1,193},{65,129},{129,65},{193,1... | collective-permute-start | bytes 589832 | tf_op jit(solution)/shard_map/ppermute | solution.py:37
  91.3 9.7 %collective-permute-start.15 = (f32[64,168]{1,0:T(8,128)S(1)}, f32[64,168]{1,0:T(8,128)S(1)}, u32[]{:S(2)}, u32[]{:S(2)}) collective-permute-start(f32[64,168]{1,0:T(8,128)S(1)} %get-tuple-element.103), channel_id=1, source_target_pairs={{1,0},{2,1},{3,2},{4,3},{5,4},{6,5},{7,6},{8,7},{9,8},{10,9},{11,1... | collective-permute-start | bytes 129032 | tf_op jit(solution)/shard_map/ppermute | solution.py:43
  95.8 7.9 %collective-permute-start.16 = (f32[64,168]{1,0:T(8,128)S(1)}, f32[64,168]{1,0:T(8,128)S(1)}, u32[]{:S(2)}, u32[]{:S(2)}) collective-permute-start(f32[64,168]{1,0:T(8,128)S(1)} %get-tuple-element.104), channel_id=1, source_target_pairs={{0,1},{1,2},{2,3},{3,4},{4,5},{5,6},{6,7},{7,8},{8,9},{9,10},{10,1... | collective-permute-start | bytes 129032 | tf_op jit(solution)/shard_map/ppermute | solution.py:43
  106.2 25.5 %all-to-all-start.3 = ((f32[16,40,256]{2,1,0:T(8,128)}), f32[16,40,256]{2,1,0:T(8,128)S(1)}, u32[]{:S(2)}, u32[]{:S(2)}) async-start(f32[16,40,256]{2,1,0:T(8,128)} %broadcast_in_dim.33), calls=%async_computation.3 | async-start | bytes 1310720 | tf_op jit(solution)/shard_map/all_to_all | solution.py:31
  112.3 5.6 %collective-permute-start.17 = (f32[64,768]{1,0:T(8,128)S(1)}, f32[64,768]{1,0:T(8,128)S(1)}, u32[]{:S(2)}, u32[]{:S(2)}) collective-permute-start(f32[64,768]{1,0:T(8,128)S(1)} %add_add_fusion), channel_id=1, source_target_pairs={{0,32},{32,0},{1,33},{33,1},{2,34},{34,2},{3,35},{35,3},{4,36},{36... | collective-permute-start | bytes 589832 | tf_op jit(solution)/shard_map/ppermute | solution.py:316
  118.0 7.7 %collective-permute-start.20 = (f32[64,768]{1,0:T(8,128)S(1)}, f32[64,768]{1,0:T(8,128)S(1)}, u32[]{:S(2)}, u32[]{:S(2)}) collective-permute-start(f32[64,768]{1,0:T(8,128)S(1)} %multiply_subtract_fusion.refs_0_), channel_id=1, source_target_pairs={{0,192},{64,128},{128,64},{192,0},{1,193},{65,129},{129,65},{193,1... | collective-permute-start | bytes 589832 | tf_op jit(solution)/shard_map/ppermute | solution.py:37
  120.5 6.3 %collective-permute-start.19 = (f32[64,768]{1,0:T(8,128)S(1)}, f32[64,768]{1,0:T(8,128)S(1)}, u32[]{:S(2)}, u32[]{:S(2)}) collective-permute-start(f32[64,768]{1,0:T(8,128)S(1)} %multiply_subtract_fusion.refs_0_), channel_id=1, source_target_pairs={{0,128},{64,192},{128,0},{192,64},{1,129},{65,193},{129,1},{193,65... | collective-permute-start | bytes 589832 | tf_op jit(solution)/shard_map/ppermute | solution.py:37
  121.0 6.2 %collective-permute-start.18 = (f32[64,768]{1,0:T(8,128)S(1)}, f32[64,768]{1,0:T(8,128)S(1)}, u32[]{:S(2)}, u32[]{:S(2)}) collective-permute-start(f32[64,768]{1,0:T(8,128)S(1)} %multiply_subtract_fusion.refs_0_), channel_id=1, source_target_pairs={{0,64},{64,0},{128,192},{192,128},{1,65},{65,1},{129,193},{193,129... | collective-permute-start | bytes 589832 | tf_op jit(solution)/shard_map/ppermute | solution.py:37
  (8 other events, 129.8 us)

commit v9 on v8

--- a/solution.py
+++ b/solution.py
@@ -134,17 +134,17 @@
     return jnp.where(kept < HIDDEN / 2, dot(f_low, x_low) - kept, 0.0).astype(BF16)
 
 
-def placed(_, along_ref, *refs):
+def placed(along_ref, *refs):
     *came, x_ref, x_low_ref = refs
     assembled(along_ref[0], came, x_ref, x_low_ref)
 
 
-def placed_low(_, along_ref, *refs):
+def placed_low(along_ref, *refs):
     *came, x_low_ref = refs
     assembled(along_ref[0], came, x_low_ref)
 
 
-def later_mine(_, __, x_low_ref, f_ref, kept_ref, grad_ref, total_ref):
+def later_mine(x_low_ref, f_ref, kept_ref, grad_ref, total_ref):
     x_low = x_low_ref[...]
     f_low = f_ref[...].astype(BF16)
     misfit = misfit_of(f_low, x_low, kept_ref)
@@ -152,41 +152,41 @@
     add_up(total_ref, by_rows(f_low, misfit))
 
 
-def later_theirs(_, __, x_low_ref, f_ref, kept_ref, grad_ref, misfit_ref):
+def later_theirs(x_low_ref, f_ref, kept_ref, grad_ref, misfit_ref):
     x_low = x_low_ref[...]
     misfit = misfit_of(f_ref[...].astype(BF16), x_low, kept_ref)
     misfit_ref[...] = misfit
     grad_ref[...] = by_hours(misfit, x_low)
 
 
-def later_rows(_, along_ref, f_ref, misfit_ref, start_ref, *refs):
+def later_rows(along_ref, f_ref, misfit_ref, start_ref, *refs):
     *pieces, total_ref = refs
     add_up(total_ref, by_rows(f_ref[...].astype(BF16), misfit_ref[...]), start_ref)
     share_out(along_ref[0], total_ref, pieces)
 
 
-def last_mine(_, __, x_low_ref, f_ref, f_out_ref, imputed_ref):
+def last_mine(_, x_low_ref, f_ref, f_out_ref, imputed_ref):
     f_out_ref[...] = f_ref[...]
     imputed_ref[...] = dot(f_ref[...].astype(BF16), x_low_ref[...]).astype(BF16)
 
 
-def last_theirs(_, __, x_low_ref, f_ref, f_held_ref, imputed_held_ref, f_out_ref, imputed_ref):
+def last_theirs(_, x_low_ref, f_ref, f_held_ref, imputed_held_ref, f_out_ref, imputed_ref):
     f_out_ref[...] = f_ref[...]
     imputed_ref[...] = dot(f_ref[...].astype(BF16), x_low_ref[...]).astype(BF16)
 
 
 def half_pass(kernel, place, ins, outs, steps, limit, matmuls, scratch=(), aliases=()):
     maps = {
-        "whole": lambda i, p, _: (0, 0),
-        "half": lambda i, p, _: (i, 0),
-        "mine": lambda i, p, _: (p[0] * steps + i, 0),
-        "theirs": lambda i, p, _: ((1 - p[0]) * steps + i, 0),
-        "both": lambda i, p, _: ((i // FIRST + 1 + p[0]) % 2 * FIRST + i % FIRST, 0),
-        "all": lambda i, p, _: (i, 0),
-        "lower": lambda i, p, _: (i, 0),
-        "upper": lambda i, p, _: (steps + i, 0),
-        "former": lambda i, p, _: (jnp.minimum(i, FIRST - 1), 0),
-        "latter": lambda i, p, _: (jnp.maximum(i - FIRST, 0), 0),
+        "whole": lambda i, *p: (0, 0),
+        "half": lambda i, *p: (i, 0),
+        "mine": lambda i, *p: (p[0][0] * steps + i, 0),
+        "theirs": lambda i, *p: ((1 - p[0][0]) * steps + i, 0),
+        "both": lambda i, *p: ((i // FIRST + 1 + p[0][0]) % 2 * FIRST + i % FIRST, 0),
+        "all": lambda i, *p: (i, 0),
+        "lower": lambda i, *p: (i, 0),
+        "upper": lambda i, *p: (steps + i, 0),
+        "former": lambda i, *p: (jnp.minimum(i, FIRST - 1), 0),
+        "latter": lambda i, *p: (jnp.maximum(i - FIRST, 0), 0),
     }
     tiles = {"whole": 1, "half": steps, "mine": 2 * steps, "theirs": 2 * steps}
     tiles.update(both=2 * FIRST, former=FIRST, latter=FIRST, all=steps)
@@ -207,7 +207,7 @@
         kernel,
         out_shape=[s for _, s in outs],
         grid_spec=pltpu.PrefetchScalarGridSpec(
-            num_scalar_prefetch=2,
+            num_scalar_prefetch=len(place),
             grid=(steps,),
             in_specs=[spec(k, a.shape) for k, a in ins],
             out_specs=[spec(k, s.shape) for k, s in outs],
@@ -242,7 +242,7 @@
     along = lax.axis_index("x")
     position = lax.axis_index(TM)
     first, last = position == 0, position == lax.axis_size(TM) - 1
-    place = (core.reshape(1), along.reshape(1))
+    which_core, which_place = core.reshape(1), along.reshape(1)
 
     def shape(n, m, dtype=F32):
         return jax.ShapeDtypeStruct((n, m), dtype)
@@ -261,7 +261,7 @@
         if sweep == 0:
             theirs, mine, kept, *parts = half_pass(
                 first_pass,
-                place,
+                (which_core, which_place),
                 [("whole", time_factors), ("both", series_factors), ("both", observed), ("both", mask)],
                 [("former", grad[1]), ("latter", grad[1]), ("all", shape(rows, hours, BF16)), *shares],
                 2 * FIRST,
@@ -273,7 +273,7 @@
         else:
             mine, start = half_pass(
                 later_mine,
-                place,
+                (),
                 [("whole", x_low), ("half", f_mine), ("upper", kept)],
                 [grad, total],
                 LATER,
@@ -283,7 +283,7 @@
             f_theirs, mine, start = lax.optimization_barrier((f_theirs, mine, start))
             theirs, misfit = half_pass(
                 later_theirs,
-                place,
+                (),
                 [("whole", x_low), ("half", f_theirs), ("lower", kept)],
                 [grad, flags],
                 LATER,
@@ -293,7 +293,7 @@
             came = lax.ppermute(theirs, CORE, SWAP)
             parts = half_pass(
                 later_rows,
-                place,
+                (which_place,),
                 [("half", f_theirs), ("half", misfit), ("whole", start)],
                 shares,
                 LATER,
@@ -319,7 +319,7 @@
         pieces = [x_part] + [traded(x_part, "x", k) for k in range(1, peers)]
         *x_full, x_low = half_pass(
             placed if sweep + 1 == ITERS else placed_low,
-            place,
+            (which_place,),
             [("whole", p) for p in pieces],
             [total, low] if sweep + 1 == ITERS else [low],
             1,
@@ -330,7 +330,7 @@
         f_theirs = lax.ppermute(f_mine, CORE, SWAP)
     f_out, imputed = half_pass(
         last_mine,
-        place,
+        (which_core,),
         [("whole", x_low), ("half", f_mine)],
         [("mine", shape(rows, rank)), ("mine", shape(rows, hours, BF16))],
         LAST,
@@ -339,13 +339,13 @@
     )
     f_out, imputed = half_pass(
         last_theirs,
-        place,
+        (which_core,),
         [("whole", x_low), ("half", f_theirs), ("held", f_out), ("held", imputed)],
         [("theirs", shape(rows, rank)), ("theirs", shape(rows, hours, BF16))],
         LAST,
         16,
         1,
-        aliases={4: 0, 5: 1},
+        aliases={3: 0, 4: 1},
     )
     return f_out, x_full[0], imputed
 

time: 139 us -> 139 us (level)
  no operation moved by 1% of the time
where the time goes in v9:
time: 139 us; the launch traced here: 138 us
  starting transfers between devices  71.8 us (52%)
  waiting for transfers between devices  42.9 us (31%)
  Pallas kernels  13.7 us (10%)
  other arithmetic  4.35 us (3%)
  local copies, waits for them, and re-layouts  4.12 us (3%)
    ppermute x4, starting transfers between devices, passed_along(): return lax.ppermute(array, axis, pairs)  19 us
    ppermute x12, waiting for transfers between devices, traded(): return lax.ppermute(array, axis, [(i, i ^ bits) for i in range(length)])  15.5 us
    ppermute x12, starting transfers between devices, traded(): return lax.ppermute(array, axis, [(i, i ^ bits) for i in range(length)])  14.6 us
    all_to_all x2, starting transfers between devices, scattered_sum(): return lax.all_to_all(parts, axis, 0, 0, tiled=True).sum(axis=0)  14.5 us
    pallas_call x8, Pallas kernels, half_pass(): pl.pallas_call(kernel, out_shape=[s for _, s in outs], grid_spec=pltpu.Pr...  13.7 us
    all_to_all x2, starting transfers between devices, gathered(): parts = lax.all_to_all(parts, axis, 0, 0, tiled=True)  12.2 us
    ppermute x2, waiting for transfers between devices, local(): x_sum = x_sum + lax.ppermute(x_sum, 'y_lo', SWAP)  9.98 us
    all_to_all x2, waiting for transfers between devices, gathered(): parts = lax.all_to_all(parts, axis, 0, 0, tiled=True)  7.79 us
  transfers between devices with their start and end apart: 26, of which 22 were waited for; matrix products, arithmetic and copies ran while one was open for 3% of the time, Pallas kernels for 3%

profile of v9, /device:TPU:1, one launch (start us, length us, event | category | flops | bytes accessed | tf_op | source)
XLA Modules:
  0.0 137.8 jit_solution(10442531351515901327)
XLA Ops:
  0.7 7.3 %first_pass.1 = (f32[640,256]{1,0:T(8,128)}, f32[640,256]{1,0:T(8,128)}, bf16[1280,768]{1,0:T(8,128)(2,1)}, f32[64,768]{1,0:T(8,128)}, f32[64,768]{1,0:T(8,128)}, /*index=5*/f32[64,768]{1,0:T(8,128)}, f32[64,768]{1,0:T(8,128)}) custom-call(s32[1]{0:T(128)} %bitcast._, s32[1]{0:T(128)} %bitcast.1.along_ref, f32[256,768]{1,0:T(8,128)} %x_ref.1, ...), custom_call_target="tpu_custom_call" | custom-call | flops 1509949440 | bytes 12058624 | tf_op jit(solution)/shard_map/first_pass/pallas_call | solution.py:206
  8.0 3.3 %collective-permute-start = (f32[640,256]{1,0:T(8,128)}, f32[640,256]{1,0:T(8,128)S(1)}, u32[]{:S(2)}, u32[]{:S(2)}) collective-permute-start(f32[640,256]{1,0:T(8,128)} %get-tuple-element.54), channel_id=1, source_target_pairs={{0,1},{1,0},{2,3},{3,2},{4,5},{5,4},{6,7},{7,6},{8,9},{9,8},{10,11... | collective-permute-start | bytes 1966088 | tf_op jit(solution)/shard_map/ppermute | solution.py:272
  15.3 9.2 %all-to-all-start = ((f32[16,40,256]{2,1,0:T(8,128)}), f32[16,40,256]{2,1,0:T(8,128)S(1)}, u32[]{:S(2)}, u32[]{:S(2)}) async-start(f32[16,40,256]{2,1,0:T(8,128)} %bitcast.5), calls=%async_computation | async-start | bytes 1310720 | tf_op jit(solution)/shard_map/all_to_all | solution.py:26
  25.8 2.5 %collective-permute-start.2 = (f32[64,768]{1,0:T(8,128)S(1)}, f32[64,768]{1,0:T(8,128)S(1)}, u32[]{:S(2)}, u32[]{:S(2)}) collective-permute-start(f32[64,768]{1,0:T(8,128)S(1)} %copy-done.4), channel_id=1, source_target_pairs={{0,128},{64,192},{128,0},{192,64},{1,129},{65,193},{129,1},{193,65... | collective-permute-start | bytes 589832 | tf_op jit(solution)/shard_map/ppermute | solution.py:37
  30.5 4.6 %collective-permute-start.4 = (f32[64,168]{1,0:T(8,128)S(1)}, f32[64,168]{1,0:T(8,128)S(1)}, u32[]{:S(2)}, u32[]{:S(2)}) collective-permute-start(f32[64,168]{1,0:T(8,128)S(1)} %get-tuple-element.105), channel_id=1, source_target_pairs={{1,0},{2,1},{3,2},{4,3},{5,4},{6,5},{7,6},{8,7},{9,8},{10,9},{11,1... | collective-permute-start | bytes 129032 | tf_op jit(solution)/shard_map/ppermute | solution.py:43
  35.0 5.0 %collective-permute-start.5 = (f32[64,168]{1,0:T(8,128)S(1)}, f32[64,168]{1,0:T(8,128)S(1)}, u32[]{:S(2)}, u32[]{:S(2)}) collective-permute-start(f32[64,168]{1,0:T(8,128)S(1)} %get-tuple-element.106), channel_id=1, source_target_pairs={{0,1},{1,2},{2,3},{3,4},{4,5},{5,6},{6,7},{7,8},{8,9},{9,10},{10,1... | collective-permute-start | bytes 129032 | tf_op jit(solution)/shard_map/ppermute | solution.py:43
  40.6 2.3 %collective-permute-done.5 = f32[64,168]{1,0:T(8,128)S(1)} collective-permute-done((f32[64,168]{1,0:T(8,128)S(1)}, f32[64,168]{1,0:T(8,128)S(1)}, u32[]{:S(2)}, u32[]{:S(2)}) %collective-permute-start.5) | collective-permute-done | bytes 43040 | tf_op jit(solution)/shard_map/ppermute | solution.py:43
  45.4 6.1 %all-to-all-start.1 = ((f32[16,40,256]{2,1,0:T(8,128)}), f32[16,40,256]{2,1,0:T(8,128)S(1)}, u32[]{:S(2)}, u32[]{:S(2)}) async-start(f32[16,40,256]{2,1,0:T(8,128)} %broadcast_in_dim.32), calls=%async_computation.1 | async-start | bytes 1310720 | tf_op jit(solution)/shard_map/all_to_all | solution.py:31
  52.0 5.1 %collective-permute-done.6 = f32[64,768]{1,0:T(8,128)S(1)} collective-permute-done((f32[64,768]{1,0:T(8,128)S(1)}, f32[64,768]{1,0:T(8,128)S(1)}, u32[]{:S(2)}, u32[]{:S(2)}) %collective-permute-start.6) | collective-permute-done | bytes 196640 | tf_op jit(solution)/shard_map/ppermute | solution.py:316
  57.2 2.6 %collective-permute-start.9 = (f32[64,768]{1,0:T(8,128)S(1)}, f32[64,768]{1,0:T(8,128)S(1)}, u32[]{:S(2)}, u32[]{:S(2)}) collective-permute-start(f32[64,768]{1,0:T(8,128)S(1)} %multiply_subtract_fusion.1.refs_0_), channel_id=1, source_target_pairs={{0,192},{64,128},{128,64},{192,0},{1,193},{65,129},{129,65},{193,1... | collective-permute-start | bytes 589832 | tf_op jit(solution)/shard_map/ppermute | solution.py:37
  60.6 4.4 %collective-permute-done.9.refs_3_ = f32[64,768]{1,0:T(8,128)S(1)} collective-permute-done((f32[64,768]{1,0:T(8,128)S(1)}, f32[64,768]{1,0:T(8,128)S(1)}, u32[]{:S(2)}, u32[]{:S(2)}) %collective-permute-start.9) | collective-permute-done | bytes 196640 | tf_op jit(solution)/shard_map/ppermute | solution.py:37
  66.4 4.2 %all-to-all-done.1 = f32[16,40,256]{2,1,0:T(8,128)S(1)} async-done(((f32[16,40,256]{2,1,0:T(8,128)}), f32[16,40,256]{2,1,0:T(8,128)S(1)}, u32[]{:S(2)}, u32[]{:S(2)}) %all-to-all-start.1) | async-done | bytes 655392 | tf_op jit(solution)/shard_map/all_to_all | solution.py:31
  70.6 3.5 %collective-permute-start.10 = (f32[640,256]{1,0:T(8,128)S(1)}, f32[640,256]{1,0:T(8,128)S(1)}, u32[]{:S(2)}, u32[]{:S(2)}) collective-permute-start(f32[640,256]{1,0:T(8,128)S(1)} %bitcast.14), channel_id=1, source_target_pairs={{0,1},{1,0},{2,3},{3,2},{4,5},{5,4},{6,7},{7,6},{8,9},{9,8},{10,11... | collective-permute-start | bytes 1966088 | tf_op jit(solution)/shard_map/ppermute | solution.py:330
  80.0 5.4 %all-to-all-start.2 = ((f32[16,40,256]{2,1,0:T(8,128)}), f32[16,40,256]{2,1,0:T(8,128)S(1)}, u32[]{:S(2)}, u32[]{:S(2)}) async-start(f32[16,40,256]{2,1,0:T(8,128)} %bitcast.7), calls=%async_computation.2 | async-start | bytes 1310720 | tf_op jit(solution)/shard_map/all_to_all | solution.py:26
  86.6 2.4 %collective-permute-start.13 = (f32[64,768]{1,0:T(8,128)S(1)}, f32[64,768]{1,0:T(8,128)S(1)}, u32[]{:S(2)}, u32[]{:S(2)}) collective-permute-start(f32[64,768]{1,0:T(8,128)S(1)} %get-tuple-element.88), channel_id=1, source_target_pairs={{0,128},{64,192},{128,0},{192,64},{1,129},{65,193},{129,1},{193,65... | collective-permute-start | bytes 589832 | tf_op jit(solution)/shard_map/ppermute | solution.py:37
  91.3 4.6 %collective-permute-start.15 = (f32[64,168]{1,0:T(8,128)S(1)}, f32[64,168]{1,0:T(8,128)S(1)}, u32[]{:S(2)}, u32[]{:S(2)}) collective-permute-start(f32[64,168]{1,0:T(8,128)S(1)} %get-tuple-element.103), channel_id=1, source_target_pairs={{1,0},{2,1},{3,2},{4,3},{5,4},{6,5},{7,6},{8,7},{9,8},{10,9},{11,1... | collective-permute-start | bytes 129032 | tf_op jit(solution)/shard_map/ppermute | solution.py:43
  95.8 4.9 %collective-permute-start.16 = (f32[64,168]{1,0:T(8,128)S(1)}, f32[64,168]{1,0:T(8,128)S(1)}, u32[]{:S(2)}, u32[]{:S(2)}) collective-permute-start(f32[64,168]{1,0:T(8,128)S(1)} %get-tuple-element.104), channel_id=1, source_target_pairs={{0,1},{1,2},{2,3},{3,4},{4,5},{5,6},{6,7},{7,8},{8,9},{9,10},{10,1... | collective-permute-start | bytes 129032 | tf_op jit(solution)/shard_map/ppermute | solution.py:43
  101.0 2.8 %collective-permute-done.16 = f32[64,168]{1,0:T(8,128)S(1)} collective-permute-done((f32[64,168]{1,0:T(8,128)S(1)}, f32[64,168]{1,0:T(8,128)S(1)}, u32[]{:S(2)}, u32[]{:S(2)}) %collective-permute-start.16) | collective-permute-done | bytes 43040 | tf_op jit(solution)/shard_map/ppermute | solution.py:43
  106.2 6.1 %all-to-all-start.3 = ((f32[16,40,256]{2,1,0:T(8,128)}), f32[16,40,256]{2,1,0:T(8,128)S(1)}, u32[]{:S(2)}, u32[]{:S(2)}) async-start(f32[16,40,256]{2,1,0:T(8,128)} %broadcast_in_dim.33), calls=%async_computation.3 | async-start | bytes 1310720 | tf_op jit(solution)/shard_map/all_to_all | solution.py:31
  113.1 4.9 %collective-permute-done.17 = f32[64,768]{1,0:T(8,128)S(1)} collective-permute-done((f32[64,768]{1,0:T(8,128)S(1)}, f32[64,768]{1,0:T(8,128)S(1)}, u32[]{:S(2)}, u32[]{:S(2)}) %collective-permute-start.17) | collective-permute-done | bytes 196640 | tf_op jit(solution)/shard_map/ppermute | solution.py:316
  118.0 2.5 %collective-permute-start.20 = (f32[64,768]{1,0:T(8,128)S(1)}, f32[64,768]{1,0:T(8,128)S(1)}, u32[]{:S(2)}, u32[]{:S(2)}) collective-permute-start(f32[64,768]{1,0:T(8,128)S(1)} %multiply_subtract_fusion.refs_0_), channel_id=1, source_target_pairs={{0,192},{64,128},{128,64},{192,0},{1,193},{65,129},{129,65},{193,1... | collective-permute-start | bytes 589832 | tf_op jit(solution)/shard_map/ppermute | solution.py:37
  121.3 4.4 %collective-permute-done.20.refs_3_ = f32[64,768]{1,0:T(8,128)S(1)} collective-permute-done((f32[64,768]{1,0:T(8,128)S(1)}, f32[64,768]{1,0:T(8,128)S(1)}, u32[]{:S(2)}, u32[]{:S(2)}) %collective-permute-start.20) | collective-permute-done | bytes 196640 | tf_op jit(solution)/shard_map/ppermute | solution.py:37
  128.2 3.5 %all-to-all-done.3 = f32[16,40,256]{2,1,0:T(8,128)S(1)} async-done(((f32[16,40,256]{2,1,0:T(8,128)}), f32[16,40,256]{2,1,0:T(8,128)S(1)}, u32[]{:S(2)}, u32[]{:S(2)}) %all-to-all-start.3) | async-done | bytes 655392 | tf_op jit(solution)/shard_map/all_to_all | solution.py:31
  131.7 2.9 %collective-permute-start.21 = (f32[640,256]{1,0:T(8,128)S(1)}, f32[640,256]{1,0:T(8,128)S(1)}, u32[]{:S(2)}, u32[]{:S(2)}) collective-permute-start(f32[640,256]{1,0:T(8,128)S(1)} %bitcast.12), channel_id=1, source_target_pairs={{0,1},{1,0},{2,3},{3,2},{4,5},{5,4},{6,7},{7,6},{8,9},{9,8},{10,11... | collective-permute-start | bytes 1966088 | tf_op jit(solution)/shard_map/ppermute | solution.py:330
  (73 shorter events, 32.4 us)
Async XLA Ops:
  8.0 5.3 %collective-permute-start = (f32[640,256]{1,0:T(8,128)}, f32[640,256]{1,0:T(8,128)S(1)}, u32[]{:S(2)}, u32[]{:S(2)}) collective-permute-start(f32[640,256]{1,0:T(8,128)} %get-tuple-element.54), channel_id=1, source_target_pairs={{0,1},{1,0},{2,3},{3,2},{4,5},{5,4},{6,7},{7,6},{8,9},{9,8},{10,11... | collective-permute-start | bytes 1966088 | tf_op jit(solution)/shard_map/ppermute | solution.py:272
  15.3 29.2 %all-to-all-start = ((f32[16,40,256]{2,1,0:T(8,128)}), f32[16,40,256]{2,1,0:T(8,128)S(1)}, u32[]{:S(2)}, u32[]{:S(2)}) async-start(f32[16,40,256]{2,1,0:T(8,128)} %bitcast.5), calls=%async_computation | async-start | bytes 1310720 | tf_op jit(solution)/shard_map/all_to_all | solution.py:26
  24.5 5.9 %collective-permute-start.1 = (f32[64,768]{1,0:T(8,128)S(1)}, f32[64,768]{1,0:T(8,128)S(1)}, u32[]{:S(2)}, u32[]{:S(2)}) collective-permute-start(f32[64,768]{1,0:T(8,128)S(1)} %copy-done.5), channel_id=1, source_target_pairs={{0,64},{64,0},{128,192},{192,128},{1,65},{65,1},{129,193},{193,129... | collective-permute-start | bytes 589832 | tf_op jit(solution)/shard_map/ppermute | solution.py:37
  25.8 14.2 %collective-permute-start.2 = (f32[64,768]{1,0:T(8,128)S(1)}, f32[64,768]{1,0:T(8,128)S(1)}, u32[]{:S(2)}, u32[]{:S(2)}) collective-permute-start(f32[64,768]{1,0:T(8,128)S(1)} %copy-done.4), channel_id=1, source_target_pairs={{0,128},{64,192},{128,0},{192,64},{1,129},{65,193},{129,1},{193,65... | collective-permute-start | bytes 589832 | tf_op jit(solution)/shard_map/ppermute | solution.py:37
  28.3 11.8 %collective-permute-start.3 = (f32[64,768]{1,0:T(8,128)S(1)}, f32[64,768]{1,0:T(8,128)S(1)}, u32[]{:S(2)}, u32[]{:S(2)}) collective-permute-start(f32[64,768]{1,0:T(8,128)S(1)} %copy-done.3), channel_id=1, source_target_pairs={{0,192},{64,128},{128,64},{192,0},{1,193},{65,129},{129,65},{193,1... | collective-permute-start | bytes 589832 | tf_op jit(solution)/shard_map/ppermute | solution.py:37
  30.5 10.1 %collective-permute-start.4 = (f32[64,168]{1,0:T(8,128)S(1)}, f32[64,168]{1,0:T(8,128)S(1)}, u32[]{:S(2)}, u32[]{:S(2)}) collective-permute-start(f32[64,168]{1,0:T(8,128)S(1)} %get-tuple-element.105), channel_id=1, source_target_pairs={{1,0},{2,1},{3,2},{4,3},{5,4},{6,5},{7,6},{8,7},{9,8},{10,9},{11,1... | collective-permute-start | bytes 129032 | tf_op jit(solution)/shard_map/ppermute | solution.py:43
  35.0 7.9 %collective-permute-start.5 = (f32[64,168]{1,0:T(8,128)S(1)}, f32[64,168]{1,0:T(8,128)S(1)}, u32[]{:S(2)}, u32[]{:S(2)}) collective-permute-start(f32[64,168]{1,0:T(8,128)S(1)} %get-tuple-element.106), channel_id=1, source_target_pairs={{0,1},{1,2},{2,3},{3,4},{4,5},{5,6},{6,7},{7,8},{8,9},{9,10},{10,1... | collective-permute-start | bytes 129032 | tf_op jit(solution)/shard_map/ppermute | solution.py:43
  45.4 25.2 %all-to-all-start.1 = ((f32[16,40,256]{2,1,0:T(8,128)}), f32[16,40,256]{2,1,0:T(8,128)S(1)}, u32[]{:S(2)}, u32[]{:S(2)}) async-start(f32[16,40,256]{2,1,0:T(8,128)} %broadcast_in_dim.32), calls=%async_computation.1 | async-start | bytes 1310720 | tf_op jit(solution)/shard_map/all_to_all | solution.py:31
  51.5 5.6 %collective-permute-start.6 = (f32[64,768]{1,0:T(8,128)S(1)}, f32[64,768]{1,0:T(8,128)S(1)}, u32[]{:S(2)}, u32[]{:S(2)}) collective-permute-start(f32[64,768]{1,0:T(8,128)S(1)} %add_add_fusion.1), channel_id=1, source_target_pairs={{0,32},{32,0},{1,33},{33,1},{2,34},{34,2},{3,35},{35,3},{4,36},{36... | collective-permute-start | bytes 589832 | tf_op jit(solution)/shard_map/ppermute | solution.py:316
  57.2 7.8 %collective-permute-start.9 = (f32[64,768]{1,0:T(8,128)S(1)}, f32[64,768]{1,0:T(8,128)S(1)}, u32[]{:S(2)}, u32[]{:S(2)}) collective-permute-start(f32[64,768]{1,0:T(8,128)S(1)} %multiply_subtract_fusion.1.refs_0_), channel_id=1, source_target_pairs={{0,192},{64,128},{128,64},{192,0},{1,193},{65,129},{129,65},{193,1... | collective-permute-start | bytes 589832 | tf_op jit(solution)/shard_map/ppermute | solution.py:37
  59.8 6.3 %collective-permute-start.8 = (f32[64,768]{1,0:T(8,128)S(1)}, f32[64,768]{1,0:T(8,128)S(1)}, u32[]{:S(2)}, u32[]{:S(2)}) collective-permute-start(f32[64,768]{1,0:T(8,128)S(1)} %multiply_subtract_fusion.1.refs_0_), channel_id=1, source_target_pairs={{0,128},{64,192},{128,0},{192,64},{1,129},{65,193},{129,1},{193,65... | collective-permute-start | bytes 589832 | tf_op jit(solution)/shard_map/ppermute | solution.py:37
  60.3 6.0 %collective-permute-start.7 = (f32[64,768]{1,0:T(8,128)S(1)}, f32[64,768]{1,0:T(8,128)S(1)}, u32[]{:S(2)}, u32[]{:S(2)}) collective-permute-start(f32[64,768]{1,0:T(8,128)S(1)} %multiply_subtract_fusion.1.refs_0_), channel_id=1, source_target_pairs={{0,64},{64,0},{128,192},{192,128},{1,65},{65,1},{129,193},{193,129... | collective-permute-start | bytes 589832 | tf_op jit(solution)/shard_map/ppermute | solution.py:37
  70.6 5.3 %collective-permute-start.10 = (f32[640,256]{1,0:T(8,128)S(1)}, f32[640,256]{1,0:T(8,128)S(1)}, u32[]{:S(2)}, u32[]{:S(2)}) collective-permute-start(f32[640,256]{1,0:T(8,128)S(1)} %bitcast.14), channel_id=1, source_target_pairs={{0,1},{1,0},{2,3},{3,2},{4,5},{5,4},{6,7},{7,6},{8,9},{9,8},{10,11... | collective-permute-start | bytes 1966088 | tf_op jit(solution)/shard_map/ppermute | solution.py:330
  80.0 25.3 %all-to-all-start.2 = ((f32[16,40,256]{2,1,0:T(8,128)}), f32[16,40,256]{2,1,0:T(8,128)S(1)}, u32[]{:S(2)}, u32[]{:S(2)}) async-start(f32[16,40,256]{2,1,0:T(8,128)} %bitcast.7), calls=%async_computation.2 | async-start | bytes 1310720 | tf_op jit(solution)/shard_map/all_to_all | solution.py:26
  85.3 5.9 %collective-permute-start.12 = (f32[64,768]{1,0:T(8,128)S(1)}, f32[64,768]{1,0:T(8,128)S(1)}, u32[]{:S(2)}, u32[]{:S(2)}) collective-permute-start(f32[64,768]{1,0:T(8,128)S(1)} %get-tuple-element.86), channel_id=1, source_target_pairs={{0,64},{64,0},{128,192},{192,128},{1,65},{65,1},{129,193},{193,129... | collective-permute-start | bytes 589832 | tf_op jit(solution)/shard_map/ppermute | solution.py:37
  86.6 14.2 %collective-permute-start.13 = (f32[64,768]{1,0:T(8,128)S(1)}, f32[64,768]{1,0:T(8,128)S(1)}, u32[]{:S(2)}, u32[]{:S(2)}) collective-permute-start(f32[64,768]{1,0:T(8,128)S(1)} %get-tuple-element.88), channel_id=1, source_target_pairs={{0,128},{64,192},{128,0},{192,64},{1,129},{65,193},{129,1},{193,65... | collective-permute-start | bytes 589832 | tf_op jit(solution)/shard_map/ppermute | solution.py:37
  89.0 11.8 %collective-permute-start.14 = (f32[64,768]{1,0:T(8,128)S(1)}, f32[64,768]{1,0:T(8,128)S(1)}, u32[]{:S(2)}, u32[]{:S(2)}) collective-permute-start(f32[64,768]{1,0:T(8,128)S(1)} %get-tuple-element.89), channel_id=1, source_target_pairs={{0,192},{64,128},{128,64},{192,0},{1,193},{65,129},{129,65},{193,1... | collective-permute-start | bytes 589832 | tf_op jit(solution)/shard_map/ppermute | solution.py:37
  91.3 9.7 %collective-permute-start.15 = (f32[64,168]{1,0:T(8,128)S(1)}, f32[64,168]{1,0:T(8,128)S(1)}, u32[]{:S(2)}, u32[]{:S(2)}) collective-permute-start(f32[64,168]{1,0:T(8,128)S(1)} %get-tuple-element.103), channel_id=1, source_target_pairs={{1,0},{2,1},{3,2},{4,3},{5,4},{6,5},{7,6},{8,7},{9,8},{10,9},{11,1... | collective-permute-start | bytes 129032 | tf_op jit(solution)/shard_map/ppermute | solution.py:43
  95.8 7.9 %collective-permute-start.16 = (f32[64,168]{1,0:T(8,128)S(1)}, f32[64,168]{1,0:T(8,128)S(1)}, u32[]{:S(2)}, u32[]{:S(2)}) collective-permute-start(f32[64,168]{1,0:T(8,128)S(1)} %get-tuple-element.104), channel_id=1, source_target_pairs={{0,1},{1,2},{2,3},{3,4},{4,5},{5,6},{6,7},{7,8},{8,9},{9,10},{10,1... | collective-permute-start | bytes 129032 | tf_op jit(solution)/shard_map/ppermute | solution.py:43
  106.2 25.5 %all-to-all-start.3 = ((f32[16,40,256]{2,1,0:T(8,128)}), f32[16,40,256]{2,1,0:T(8,128)S(1)}, u32[]{:S(2)}, u32[]{:S(2)}) async-start(f32[16,40,256]{2,1,0:T(8,128)} %broadcast_in_dim.33), calls=%async_computation.3 | async-start | bytes 1310720 | tf_op jit(solution)/shard_map/all_to_all | solution.py:31
  112.3 5.6 %collective-permute-start.17 = (f32[64,768]{1,0:T(8,128)S(1)}, f32[64,768]{1,0:T(8,128)S(1)}, u32[]{:S(2)}, u32[]{:S(2)}) collective-permute-start(f32[64,768]{1,0:T(8,128)S(1)} %add_add_fusion), channel_id=1, source_target_pairs={{0,32},{32,0},{1,33},{33,1},{2,34},{34,2},{3,35},{35,3},{4,36},{36... | collective-permute-start | bytes 589832 | tf_op jit(solution)/shard_map/ppermute | solution.py:316
  118.0 7.7 %collective-permute-start.20 = (f32[64,768]{1,0:T(8,128)S(1)}, f32[64,768]{1,0:T(8,128)S(1)}, u32[]{:S(2)}, u32[]{:S(2)}) collective-permute-start(f32[64,768]{1,0:T(8,128)S(1)} %multiply_subtract_fusion.refs_0_), channel_id=1, source_target_pairs={{0,192},{64,128},{128,64},{192,0},{1,193},{65,129},{129,65},{193,1... | collective-permute-start | bytes 589832 | tf_op jit(solution)/shard_map/ppermute | solution.py:37
  120.5 6.3 %collective-permute-start.19 = (f32[64,768]{1,0:T(8,128)S(1)}, f32[64,768]{1,0:T(8,128)S(1)}, u32[]{:S(2)}, u32[]{:S(2)}) collective-permute-start(f32[64,768]{1,0:T(8,128)S(1)} %multiply_subtract_fusion.refs_0_), channel_id=1, source_target_pairs={{0,128},{64,192},{128,0},{192,64},{1,129},{65,193},{129,1},{193,65... | collective-permute-start | bytes 589832 | tf_op jit(solution)/shard_map/ppermute | solution.py:37
  121.0 6.2 %collective-permute-start.18 = (f32[64,768]{1,0:T(8,128)S(1)}, f32[64,768]{1,0:T(8,128)S(1)}, u32[]{:S(2)}, u32[]{:S(2)}) collective-permute-start(f32[64,768]{1,0:T(8,128)S(1)} %multiply_subtract_fusion.refs_0_), channel_id=1, source_target_pairs={{0,64},{64,0},{128,192},{192,128},{1,65},{65,1},{129,193},{193,129... | collective-permute-start | bytes 589832 | tf_op jit(solution)/shard_map/ppermute | solution.py:37
  (8 other events, 129.8 us)

commit v10 on v8

--- a/solution.py
+++ b/solution.py
@@ -305,13 +305,12 @@
         mine, parts, x_part = lax.optimization_barrier((mine, parts, x_part))
         f_sum = scattered_sum(mine, FAR)
         received = [traded(parts[k], "x", k) for k in range(1, peers)]
-        edge_x, received[0] = lax.optimization_barrier((x_part, received[0]))
-        edges = edges_of(edge_x)
+        edges = edges_of(x_part)
         x_sum = parts[0]
         for part in received:
             x_sum = x_sum + part
+        f_part, x_sum, edges = lax.optimization_barrier((f_part, x_sum, edges))
         lag = lag_terms(x_part, edges, w_part, first, last)
-        f_part, x_sum, lag = lax.optimization_barrier((f_part, x_sum, lag))
         f_part = f_part - step_f * (f_sum + ridge_f * f_part)
         x_sum = x_sum + lax.ppermute(x_sum, "y_lo", SWAP)
         x_part = x_part - step_x * (x_sum + ridge_x * x_part + lam * lag)

time: 139 us -> 139 us (level)
  starting transfers between devices: 71.8 us -> 69 us
  waiting for transfers between devices: 42.9 us -> 44.7 us
    all_to_all x2, waiting for transfers between devices: 1.67 us -> 9.16 us  [scattered_sum(): return lax.all_to_all(parts, axis, 0, 0, tiled=True).sum(axis=0)]
    ppermute x4, waiting for transfers between devices: 5.67 us -> 0.01 us  [passed_along(): return lax.ppermute(array, axis, pairs)]
    all_to_all x2, waiting for transfers between devices: 7.79 us -> 3.73 us  [gathered(): parts = lax.all_to_all(parts, axis, 0, 0, tiled=True)]
    ppermute x12, waiting for transfers between devices: 15.5 us -> 19.3 us  [traded(): return lax.ppermute(array, axis, [(i, i ^ bits) for i in range(length)])]
    ppermute x4, starting transfers between devices: 19 us -> 16.6 us  [passed_along(): return lax.ppermute(array, axis, pairs)]
    all_to_all x2, starting transfers between devices: 14.5 us -> 16.5 us  [scattered_sum(): return lax.all_to_all(parts, axis, 0, 0, tiled=True).sum(axis=0)]
    all_to_all x2, starting transfers between devices: 12.2 us -> 10.6 us  [gathered(): parts = lax.all_to_all(parts, axis, 0, 0, tiled=True)]
  transfers between devices with their start and end apart: 26 -> 26, of which waited for: 22 -> 14; matrix products, arithmetic and copies ran while one was open for 3% -> 3% of each run, Pallas kernels for 3% -> 3%
where the time goes in v10:
time: 139 us; the launch traced here: 138 us
  starting transfers between devices  69 us (50%)
  waiting for transfers between devices  44.7 us (32%)
  Pallas kernels  13.7 us (10%)
  other arithmetic  5.14 us (4%)
  local copies, waits for them, and re-layouts  4.15 us (3%)
    ppermute x12, waiting for transfers between devices, traded(): return lax.ppermute(array, axis, [(i, i ^ bits) for i in range(length)])  19.3 us
    ppermute x4, starting transfers between devices, passed_along(): return lax.ppermute(array, axis, pairs)  16.6 us
    all_to_all x2, starting transfers between devices, scattered_sum(): return lax.all_to_all(parts, axis, 0, 0, tiled=True).sum(axis=0)  16.5 us
    ppermute x12, starting transfers between devices, traded(): return lax.ppermute(array, axis, [(i, i ^ bits) for i in range(length)])  14.5 us
    pallas_call x8, Pallas kernels, half_pass(): pl.pallas_call(kernel, out_shape=[s for _, s in outs], grid_spec=pltpu.Pr...  13.7 us
    all_to_all x2, starting transfers between devices, gathered(): parts = lax.all_to_all(parts, axis, 0, 0, tiled=True)  10.6 us
    ppermute x2, waiting for transfers between devices, local(): x_sum = x_sum + lax.ppermute(x_sum, 'y_lo', SWAP)  9.44 us
    all_to_all x2, waiting for transfers between devices, scattered_sum(): return lax.all_to_all(parts, axis, 0, 0, tiled=True).sum(axis=0)  9.16 us
  transfers between devices with their start and end apart: 26, of which 14 were waited for; matrix products, arithmetic and copies ran while one was open for 3% of the time, Pallas kernels for 3%

profile of v10, /device:TPU:1, one launch (start us, length us, event | category | flops | bytes accessed | tf_op | source)
XLA Modules:
  0.0 137.8 jit_solution(11456280675925313427)
XLA Ops:
  0.7 7.3 %first_pass.1 = (f32[640,256]{1,0:T(8,128)}, f32[640,256]{1,0:T(8,128)}, bf16[1280,768]{1,0:T(8,128)(2,1)}, f32[64,768]{1,0:T(8,128)}, f32[64,768]{1,0:T(8,128)}, /*index=5*/f32[64,768]{1,0:T(8,128)}, f32[64,768]{1,0:T(8,128)}) custom-call(s32[1]{0:T(128)} %bitcast._, s32[1]{0:T(128)} %bitcast.1.along_ref.__, f32[256,768]{1,0:T(8,128)} %x_ref.1, ...), custom_call_target="tpu_custom_call" | custom-call | flops 1509949440 | bytes 12058624 | tf_op jit(solution)/shard_map/first_pass/pallas_call | solution.py:206
  8.0 3.3 %collective-permute-start = (f32[640,256]{1,0:T(8,128)}, f32[640,256]{1,0:T(8,128)S(1)}, u32[]{:S(2)}, u32[]{:S(2)}) collective-permute-start(f32[640,256]{1,0:T(8,128)} %get-tuple-element.52), channel_id=1, source_target_pairs={{0,1},{1,0},{2,3},{3,2},{4,5},{5,4},{6,7},{7,6},{8,9},{9,8},{10,11... | collective-permute-start | bytes 1966088 | tf_op jit(solution)/shard_map/ppermute | solution.py:272
  15.3 9.2 %all-to-all-start = ((f32[16,40,256]{2,1,0:T(8,128)}), f32[16,40,256]{2,1,0:T(8,128)S(1)}, u32[]{:S(2)}, u32[]{:S(2)}) async-start(f32[16,40,256]{2,1,0:T(8,128)} %bitcast.2), calls=%async_computation | async-start | bytes 1310720 | tf_op jit(solution)/shard_map/all_to_all | solution.py:26
  26.5 2.5 %collective-permute-start.2 = (f32[64,768]{1,0:T(8,128)S(1)}, f32[64,768]{1,0:T(8,128)S(1)}, u32[]{:S(2)}, u32[]{:S(2)}) collective-permute-start(f32[64,768]{1,0:T(8,128)S(1)} %copy-done.10), channel_id=1, source_target_pairs={{0,128},{64,192},{128,0},{192,64},{1,129},{65,193},{129,1},{193,65... | collective-permute-start | bytes 589832 | tf_op jit(solution)/shard_map/ppermute | solution.py:37
  29.2 3.4 %collective-permute-start.5 = (f32[64,168]{1,0:T(8,128)S(1)}, f32[64,168]{1,0:T(8,128)S(1)}, u32[]{:S(2)}, u32[]{:S(2)}) collective-permute-start(f32[64,168]{1,0:T(8,128)S(1)} %get-tuple-element.101), channel_id=1, source_target_pairs={{1,0},{2,1},{3,2},{4,3},{5,4},{6,5},{7,6},{8,7},{9,8},{10,9},{11,1... | collective-permute-start | bytes 129032 | tf_op jit(solution)/shard_map/ppermute | solution.py:43
  32.6 4.9 %collective-permute-start.4 = (f32[64,168]{1,0:T(8,128)S(1)}, f32[64,168]{1,0:T(8,128)S(1)}, u32[]{:S(2)}, u32[]{:S(2)}) collective-permute-start(f32[64,168]{1,0:T(8,128)S(1)} %get-tuple-element.102), channel_id=1, source_target_pairs={{0,1},{1,2},{2,3},{3,4},{4,5},{5,6},{6,7},{7,8},{8,9},{9,10},{10,1... | collective-permute-start | bytes 129032 | tf_op jit(solution)/shard_map/ppermute | solution.py:43
  37.6 2.6 %collective-permute-done.3 = f32[64,768]{1,0:T(8,128)S(1)} collective-permute-done((f32[64,768]{1,0:T(8,128)S(1)}, f32[64,768]{1,0:T(8,128)S(1)}, u32[]{:S(2)}, u32[]{:S(2)}) %collective-permute-start.3) | collective-permute-done | bytes 196640 | tf_op jit(solution)/shard_map/ppermute | solution.py:37
  40.2 4.2 %all-to-all-done = f32[16,40,256]{2,1,0:T(8,128)S(1)} async-done(((f32[16,40,256]{2,1,0:T(8,128)}), f32[16,40,256]{2,1,0:T(8,128)S(1)}, u32[]{:S(2)}, u32[]{:S(2)}) %all-to-all-start) | async-done | bytes 655392 | tf_op jit(solution)/shard_map/all_to_all | solution.py:26
  45.4 5.3 %all-to-all-start.1 = ((f32[16,40,256]{2,1,0:T(8,128)}), f32[16,40,256]{2,1,0:T(8,128)S(1)}, u32[]{:S(2)}, u32[]{:S(2)}) async-start(f32[16,40,256]{2,1,0:T(8,128)} %broadcast_in_dim.30), calls=%async_computation.1 | async-start | bytes 1310720 | tf_op jit(solution)/shard_map/all_to_all | solution.py:31
  51.8 5.0 %collective-permute-done.6 = f32[64,768]{1,0:T(8,128)} collective-permute-done((f32[64,768]{1,0:T(8,128)S(1)}, f32[64,768]{1,0:T(8,128)}, u32[]{:S(2)}, u32[]{:S(2)}) %collective-permute-start.6) | collective-permute-done | bytes 196640 | tf_op jit(solution)/shard_map/ppermute | solution.py:315
  58.0 2.6 %collective-permute-start.9 = (f32[64,768]{1,0:T(8,128)S(1)}, f32[64,768]{1,0:T(8,128)S(1)}, u32[]{:S(2)}, u32[]{:S(2)}) collective-permute-start(f32[64,768]{1,0:T(8,128)S(1)} %fusion.20.refs_0_), channel_id=1, source_target_pairs={{0,192},{64,128},{128,64},{192,0},{1,193},{65,129},{129,65},{193,1... | collective-permute-start | bytes 589832 | tf_op jit(solution)/shard_map/ppermute | solution.py:37
  61.3 7.0 %collective-permute-done.9.refs_3_ = f32[64,768]{1,0:T(8,128)S(1)} collective-permute-done((f32[64,768]{1,0:T(8,128)S(1)}, f32[64,768]{1,0:T(8,128)S(1)}, u32[]{:S(2)}, u32[]{:S(2)}) %collective-permute-start.9) | collective-permute-done | bytes 196640 | tf_op jit(solution)/shard_map/ppermute | solution.py:37
  70.2 2.8 %collective-permute-start.10 = (f32[640,256]{1,0:T(8,128)S(1)}, f32[640,256]{1,0:T(8,128)S(1)}, u32[]{:S(2)}, u32[]{:S(2)}) collective-permute-start(f32[640,256]{1,0:T(8,128)S(1)} %bitcast.14), channel_id=1, source_target_pairs={{0,1},{1,0},{2,3},{3,2},{4,5},{5,4},{6,7},{7,6},{8,9},{9,8},{10,11... | collective-permute-start | bytes 1966088 | tf_op jit(solution)/shard_map/ppermute | solution.py:329
  78.8 7.3 %all-to-all-start.2 = ((f32[16,40,256]{2,1,0:T(8,128)}), f32[16,40,256]{2,1,0:T(8,128)S(1)}, u32[]{:S(2)}, u32[]{:S(2)}) async-start(f32[16,40,256]{2,1,0:T(8,128)} %bitcast.7), calls=%async_computation.2 | async-start | bytes 1310720 | tf_op jit(solution)/shard_map/all_to_all | solution.py:26
  87.4 2.4 %collective-permute-start.13 = (f32[64,768]{1,0:T(8,128)S(1)}, f32[64,768]{1,0:T(8,128)S(1)}, u32[]{:S(2)}, u32[]{:S(2)}) collective-permute-start(f32[64,768]{1,0:T(8,128)S(1)} %get-tuple-element.83), channel_id=1, source_target_pairs={{0,128},{64,192},{128,0},{192,64},{1,129},{65,193},{129,1},{193,65... | collective-permute-start | bytes 589832 | tf_op jit(solution)/shard_map/ppermute | solution.py:37
  90.1 3.4 %collective-permute-start.16 = (f32[64,168]{1,0:T(8,128)S(1)}, f32[64,168]{1,0:T(8,128)S(1)}, u32[]{:S(2)}, u32[]{:S(2)}) collective-permute-start(f32[64,168]{1,0:T(8,128)S(1)} %get-tuple-element.99), channel_id=1, source_target_pairs={{1,0},{2,1},{3,2},{4,3},{5,4},{6,5},{7,6},{8,7},{9,8},{10,9},{11,1... | collective-permute-start | bytes 129032 | tf_op jit(solution)/shard_map/ppermute | solution.py:43
  93.5 4.9 %collective-permute-start.15 = (f32[64,168]{1,0:T(8,128)S(1)}, f32[64,168]{1,0:T(8,128)S(1)}, u32[]{:S(2)}, u32[]{:S(2)}) collective-permute-start(f32[64,168]{1,0:T(8,128)S(1)} %get-tuple-element.100), channel_id=1, source_target_pairs={{0,1},{1,2},{2,3},{3,4},{4,5},{5,6},{6,7},{7,8},{8,9},{9,10},{10,1... | collective-permute-start | bytes 129032 | tf_op jit(solution)/shard_map/ppermute | solution.py:43
  98.4 2.6 %collective-permute-done.14 = f32[64,768]{1,0:T(8,128)S(1)} collective-permute-done((f32[64,768]{1,0:T(8,128)S(1)}, f32[64,768]{1,0:T(8,128)S(1)}, u32[]{:S(2)}, u32[]{:S(2)}) %collective-permute-start.14) | collective-permute-done | bytes 196640 | tf_op jit(solution)/shard_map/ppermute | solution.py:37
  101.1 5.0 %all-to-all-done.2 = f32[16,40,256]{2,1,0:T(8,128)S(1)} async-done(((f32[16,40,256]{2,1,0:T(8,128)}), f32[16,40,256]{2,1,0:T(8,128)S(1)}, u32[]{:S(2)}, u32[]{:S(2)}) %all-to-all-start.2) | async-done | bytes 655392 | tf_op jit(solution)/shard_map/all_to_all | solution.py:26
  107.0 5.3 %all-to-all-start.3 = ((f32[16,40,256]{2,1,0:T(8,128)}), f32[16,40,256]{2,1,0:T(8,128)S(1)}, u32[]{:S(2)}, u32[]{:S(2)}) async-start(f32[16,40,256]{2,1,0:T(8,128)} %broadcast_in_dim.33), calls=%async_computation.3 | async-start | bytes 1310720 | tf_op jit(solution)/shard_map/all_to_all | solution.py:31
  113.8 4.4 %collective-permute-done.17 = f32[64,768]{1,0:T(8,128)S(1)} collective-permute-done((f32[64,768]{1,0:T(8,128)S(1)}, f32[64,768]{1,0:T(8,128)S(1)}, u32[]{:S(2)}, u32[]{:S(2)}) %collective-permute-start.17) | collective-permute-done | bytes 196640 | tf_op jit(solution)/shard_map/ppermute | solution.py:315
  118.4 2.5 %collective-permute-start.20 = (f32[64,768]{1,0:T(8,128)S(1)}, f32[64,768]{1,0:T(8,128)S(1)}, u32[]{:S(2)}, u32[]{:S(2)}) collective-permute-start(f32[64,768]{1,0:T(8,128)S(1)} %fusion.13.refs_0_), channel_id=1, source_target_pairs={{0,192},{64,128},{128,64},{192,0},{1,193},{65,129},{129,65},{193,1... | collective-permute-start | bytes 589832 | tf_op jit(solution)/shard_map/ppermute | solution.py:37
  121.8 7.2 %collective-permute-done.20.refs_3_ = f32[64,768]{1,0:T(8,128)S(1)} collective-permute-done((f32[64,768]{1,0:T(8,128)S(1)}, f32[64,768]{1,0:T(8,128)S(1)}, u32[]{:S(2)}, u32[]{:S(2)}) %collective-permute-start.20) | collective-permute-done | bytes 196640 | tf_op jit(solution)/shard_map/ppermute | solution.py:37
  131.8 2.8 %collective-permute-start.21 = (f32[640,256]{1,0:T(8,128)S(1)}, f32[640,256]{1,0:T(8,128)S(1)}, u32[]{:S(2)}, u32[]{:S(2)}) collective-permute-start(f32[640,256]{1,0:T(8,128)S(1)} %bitcast.12), channel_id=1, source_target_pairs={{0,1},{1,0},{2,3},{3,2},{4,5},{5,4},{6,7},{7,6},{8,9},{9,8},{10,11... | collective-permute-start | bytes 1966088 | tf_op jit(solution)/shard_map/ppermute | solution.py:329
  (83 shorter events, 29.1 us)
Async XLA Ops:
  8.0 5.3 %collective-permute-start = (f32[640,256]{1,0:T(8,128)}, f32[640,256]{1,0:T(8,128)S(1)}, u32[]{:S(2)}, u32[]{:S(2)}) collective-permute-start(f32[640,256]{1,0:T(8,128)} %get-tuple-element.52), channel_id=1, source_target_pairs={{0,1},{1,0},{2,3},{3,2},{4,5},{5,4},{6,7},{7,6},{8,9},{9,8},{10,11... | collective-permute-start | bytes 1966088 | tf_op jit(solution)/shard_map/ppermute | solution.py:272
  15.3 29.2 %all-to-all-start = ((f32[16,40,256]{2,1,0:T(8,128)}), f32[16,40,256]{2,1,0:T(8,128)S(1)}, u32[]{:S(2)}, u32[]{:S(2)}) async-start(f32[16,40,256]{2,1,0:T(8,128)} %bitcast.2), calls=%async_computation | async-start | bytes 1310720 | tf_op jit(solution)/shard_map/all_to_all | solution.py:26
  25.3 12.3 %collective-permute-start.1 = (f32[64,768]{1,0:T(8,128)S(1)}, f32[64,768]{1,0:T(8,128)S(1)}, u32[]{:S(2)}, u32[]{:S(2)}) collective-permute-start(f32[64,768]{1,0:T(8,128)S(1)} %copy-done.11), channel_id=1, source_target_pairs={{0,64},{64,0},{128,192},{192,128},{1,65},{65,1},{129,193},{193,129... | collective-permute-start | bytes 589832 | tf_op jit(solution)/shard_map/ppermute | solution.py:37
  26.5 11.1 %collective-permute-start.2 = (f32[64,768]{1,0:T(8,128)S(1)}, f32[64,768]{1,0:T(8,128)S(1)}, u32[]{:S(2)}, u32[]{:S(2)}) collective-permute-start(f32[64,768]{1,0:T(8,128)S(1)} %copy-done.10), channel_id=1, source_target_pairs={{0,128},{64,192},{128,0},{192,64},{1,129},{65,193},{129,1},{193,65... | collective-permute-start | bytes 589832 | tf_op jit(solution)/shard_map/ppermute | solution.py:37
  28.9 11.2 %collective-permute-start.3 = (f32[64,768]{1,0:T(8,128)S(1)}, f32[64,768]{1,0:T(8,128)S(1)}, u32[]{:S(2)}, u32[]{:S(2)}) collective-permute-start(f32[64,768]{1,0:T(8,128)S(1)} %copy-done.9), channel_id=1, source_target_pairs={{0,192},{64,128},{128,64},{192,0},{1,193},{65,129},{129,65},{193,1... | collective-permute-start | bytes 589832 | tf_op jit(solution)/shard_map/ppermute | solution.py:37
  29.2 11.0 %collective-permute-start.5 = (f32[64,168]{1,0:T(8,128)S(1)}, f32[64,168]{1,0:T(8,128)S(1)}, u32[]{:S(2)}, u32[]{:S(2)}) collective-permute-start(f32[64,168]{1,0:T(8,128)S(1)} %get-tuple-element.101), channel_id=1, source_target_pairs={{1,0},{2,1},{3,2},{4,3},{5,4},{6,5},{7,6},{8,7},{9,8},{10,9},{11,1... | collective-permute-start | bytes 129032 | tf_op jit(solution)/shard_map/ppermute | solution.py:43
  32.6 7.6 %collective-permute-start.4 = (f32[64,168]{1,0:T(8,128)S(1)}, f32[64,168]{1,0:T(8,128)S(1)}, u32[]{:S(2)}, u32[]{:S(2)}) collective-permute-start(f32[64,168]{1,0:T(8,128)S(1)} %get-tuple-element.102), channel_id=1, source_target_pairs={{0,1},{1,2},{2,3},{3,4},{4,5},{5,6},{6,7},{7,8},{8,9},{9,10},{10,1... | collective-permute-start | bytes 129032 | tf_op jit(solution)/shard_map/ppermute | solution.py:43
  45.4 24.8 %all-to-all-start.1 = ((f32[16,40,256]{2,1,0:T(8,128)}), f32[16,40,256]{2,1,0:T(8,128)S(1)}, u32[]{:S(2)}, u32[]{:S(2)}) async-start(f32[16,40,256]{2,1,0:T(8,128)} %broadcast_in_dim.30), calls=%async_computation.1 | async-start | bytes 1310720 | tf_op jit(solution)/shard_map/all_to_all | solution.py:31
  50.8 6.0 %collective-permute-start.6 = (f32[64,768]{1,0:T(8,128)S(1)}, f32[64,768]{1,0:T(8,128)}, u32[]{:S(2)}, u32[]{:S(2)}) collective-permute-start(f32[64,768]{1,0:T(8,128)S(1)} %add_add_fusion.1), channel_id=1, source_target_pairs={{0,32},{32,0},{1,33},{33,1},{2,34},{34,2},{3,35},{35,3},{4,36},{36... | collective-permute-start | bytes 589832 | tf_op jit(solution)/shard_map/ppermute | solution.py:315
  58.0 10.3 %collective-permute-start.9 = (f32[64,768]{1,0:T(8,128)S(1)}, f32[64,768]{1,0:T(8,128)S(1)}, u32[]{:S(2)}, u32[]{:S(2)}) collective-permute-start(f32[64,768]{1,0:T(8,128)S(1)} %fusion.20.refs_0_), channel_id=1, source_target_pairs={{0,192},{64,128},{128,64},{192,0},{1,193},{65,129},{129,65},{193,1... | collective-permute-start | bytes 589832 | tf_op jit(solution)/shard_map/ppermute | solution.py:37
  60.6 7.8 %collective-permute-start.8 = (f32[64,768]{1,0:T(8,128)S(1)}, f32[64,768]{1,0:T(8,128)S(1)}, u32[]{:S(2)}, u32[]{:S(2)}) collective-permute-start(f32[64,768]{1,0:T(8,128)S(1)} %fusion.20.refs_0_), channel_id=1, source_target_pairs={{0,128},{64,192},{128,0},{192,64},{1,129},{65,193},{129,1},{193,65... | collective-permute-start | bytes 589832 | tf_op jit(solution)/shard_map/ppermute | solution.py:37
  61.1 7.2 %collective-permute-start.7 = (f32[64,768]{1,0:T(8,128)S(1)}, f32[64,768]{1,0:T(8,128)S(1)}, u32[]{:S(2)}, u32[]{:S(2)}) collective-permute-start(f32[64,768]{1,0:T(8,128)S(1)} %fusion.20.refs_0_), channel_id=1, source_target_pairs={{0,64},{64,0},{128,192},{192,128},{1,65},{65,1},{129,193},{193,129... | collective-permute-start | bytes 589832 | tf_op jit(solution)/shard_map/ppermute | solution.py:37
  78.8 27.3 %all-to-all-start.2 = ((f32[16,40,256]{2,1,0:T(8,128)}), f32[16,40,256]{2,1,0:T(8,128)S(1)}, u32[]{:S(2)}, u32[]{:S(2)}) async-start(f32[16,40,256]{2,1,0:T(8,128)} %bitcast.7), calls=%async_computation.2 | async-start | bytes 1310720 | tf_op jit(solution)/shard_map/all_to_all | solution.py:26
  86.1 12.3 %collective-permute-start.12 = (f32[64,768]{1,0:T(8,128)S(1)}, f32[64,768]{1,0:T(8,128)S(1)}, u32[]{:S(2)}, u32[]{:S(2)}) collective-permute-start(f32[64,768]{1,0:T(8,128)S(1)} %get-tuple-element.82), channel_id=1, source_target_pairs={{0,64},{64,0},{128,192},{192,128},{1,65},{65,1},{129,193},{193,129... | collective-permute-start | bytes 589832 | tf_op jit(solution)/shard_map/ppermute | solution.py:37
  87.4 11.0 %collective-permute-start.13 = (f32[64,768]{1,0:T(8,128)S(1)}, f32[64,768]{1,0:T(8,128)S(1)}, u32[]{:S(2)}, u32[]{:S(2)}) collective-permute-start(f32[64,768]{1,0:T(8,128)S(1)} %get-tuple-element.83), channel_id=1, source_target_pairs={{0,128},{64,192},{128,0},{192,64},{1,129},{65,193},{129,1},{193,65... | collective-permute-start | bytes 589832 | tf_op jit(solution)/shard_map/ppermute | solution.py:37
  89.7 11.2 %collective-permute-start.14 = (f32[64,768]{1,0:T(8,128)S(1)}, f32[64,768]{1,0:T(8,128)S(1)}, u32[]{:S(2)}, u32[]{:S(2)}) collective-permute-start(f32[64,768]{1,0:T(8,128)S(1)} %get-tuple-element.84), channel_id=1, source_target_pairs={{0,192},{64,128},{128,64},{192,0},{1,193},{65,129},{129,65},{193,1... | collective-permute-start | bytes 589832 | tf_op jit(solution)/shard_map/ppermute | solution.py:37
  90.1 10.9 %collective-permute-start.16 = (f32[64,168]{1,0:T(8,128)S(1)}, f32[64,168]{1,0:T(8,128)S(1)}, u32[]{:S(2)}, u32[]{:S(2)}) collective-permute-start(f32[64,168]{1,0:T(8,128)S(1)} %get-tuple-element.99), channel_id=1, source_target_pairs={{1,0},{2,1},{3,2},{4,3},{5,4},{6,5},{7,6},{8,7},{9,8},{10,9},{11,1... | collective-permute-start | bytes 129032 | tf_op jit(solution)/shard_map/ppermute | solution.py:43
  93.5 7.5 %collective-permute-start.15 = (f32[64,168]{1,0:T(8,128)S(1)}, f32[64,168]{1,0:T(8,128)S(1)}, u32[]{:S(2)}, u32[]{:S(2)}) collective-permute-start(f32[64,168]{1,0:T(8,128)S(1)} %get-tuple-element.100), channel_id=1, source_target_pairs={{0,1},{1,2},{2,3},{3,4},{4,5},{5,6},{6,7},{7,8},{8,9},{9,10},{10,1... | collective-permute-start | bytes 129032 | tf_op jit(solution)/shard_map/ppermute | solution.py:43
  107.0 24.8 %all-to-all-start.3 = ((f32[16,40,256]{2,1,0:T(8,128)}), f32[16,40,256]{2,1,0:T(8,128)S(1)}, u32[]{:S(2)}, u32[]{:S(2)}) async-start(f32[16,40,256]{2,1,0:T(8,128)} %broadcast_in_dim.33), calls=%async_computation.3 | async-start | bytes 1310720 | tf_op jit(solution)/shard_map/all_to_all | solution.py:31
  112.3 5.9 %collective-permute-start.17 = (f32[64,768]{1,0:T(8,128)S(1)}, f32[64,768]{1,0:T(8,128)S(1)}, u32[]{:S(2)}, u32[]{:S(2)}) collective-permute-start(f32[64,768]{1,0:T(8,128)S(1)} %add_add_fusion), channel_id=1, source_target_pairs={{0,32},{32,0},{1,33},{33,1},{2,34},{34,2},{3,35},{35,3},{4,36},{36... | collective-permute-start | bytes 589832 | tf_op jit(solution)/shard_map/ppermute | solution.py:315
  118.4 10.5 %collective-permute-start.20 = (f32[64,768]{1,0:T(8,128)S(1)}, f32[64,768]{1,0:T(8,128)S(1)}, u32[]{:S(2)}, u32[]{:S(2)}) collective-permute-start(f32[64,768]{1,0:T(8,128)S(1)} %fusion.13.refs_0_), channel_id=1, source_target_pairs={{0,192},{64,128},{128,64},{192,0},{1,193},{65,129},{129,65},{193,1... | collective-permute-start | bytes 589832 | tf_op jit(solution)/shard_map/ppermute | solution.py:37
  120.9 8.0 %collective-permute-start.19 = (f32[64,768]{1,0:T(8,128)S(1)}, f32[64,768]{1,0:T(8,128)S(1)}, u32[]{:S(2)}, u32[]{:S(2)}) collective-permute-start(f32[64,768]{1,0:T(8,128)S(1)} %fusion.13.refs_0_), channel_id=1, source_target_pairs={{0,128},{64,192},{128,0},{192,64},{1,129},{65,193},{129,1},{193,65... | collective-permute-start | bytes 589832 | tf_op jit(solution)/shard_map/ppermute | solution.py:37
  121.6 7.4 %collective-permute-start.18 = (f32[64,768]{1,0:T(8,128)S(1)}, f32[64,768]{1,0:T(8,128)S(1)}, u32[]{:S(2)}, u32[]{:S(2)}) collective-permute-start(f32[64,768]{1,0:T(8,128)S(1)} %fusion.13.refs_0_), channel_id=1, source_target_pairs={{0,64},{64,0},{128,192},{192,128},{1,65},{65,1},{129,193},{193,129... | collective-permute-start | bytes 589832 | tf_op jit(solution)/shard_map/ppermute | solution.py:37
  131.8 4.5 %collective-permute-start.21 = (f32[640,256]{1,0:T(8,128)S(1)}, f32[640,256]{1,0:T(8,128)S(1)}, u32[]{:S(2)}, u32[]{:S(2)}) collective-permute-start(f32[640,256]{1,0:T(8,128)S(1)} %bitcast.12), channel_id=1, source_target_pairs={{0,1},{1,0},{2,3},{3,2},{4,5},{5,4},{6,7},{7,6},{8,9},{9,8},{10,11... | collective-permute-start | bytes 1966088 | tf_op jit(solution)/shard_map/ppermute | solution.py:329
  (14 other events, 204.1 us)
